TPU v7x, 32 devices: a whole 2x2x4 slice. The times are simulated.
32 devices in a mesh: dp: 16 (over z, y, x), mp: 2 (over core).
Axes of the slice: x: 2, y: 2, z: 4, core: 2. Of those that a mesh axis runs over, the one named last changes fastest.
Arguments:
- layer_in: bfloat16 [8192, 2048], P(('dp', 'mp')), may hold values from -6 to 6
- out_grad: bfloat16 [8192, 2048], P(('dp', 'mp')), may hold values from -6 to 6
- parents: int32 [2, 7], replicated, may hold values from 0 to 5, as said below
- lengths: int32 [2, 7], replicated, may hold values from 1 to 2048, 4096 in all within a row
- attn_gain: bfloat16 [2048], P(('dp', 'mp')), may hold values from 0.099609375 to 1.8984375
- mlp_gain: bfloat16 [2048], P(('dp', 'mp')), may hold values from 0.099609375 to 1.8984375
- query_norm_gain: bfloat16 [128], P(('dp', 'mp')), may hold values from 0.099609375 to 1.8984375
- key_gain: bfloat16 [128], P(('dp', 'mp')), may hold values from 0.099609375 to 1.8984375
- query_weight: bfloat16 [2048, 2048], P('dp', 'mp'), may hold values from -0.125 to 0.125
- key_matrix: bfloat16 [2048, 1024], P('dp', 'mp'), may hold values from -0.125 to 0.125
- value_matrix: bfloat16 [2048, 1024], P('dp', 'mp'), may hold values from -0.125 to 0.125
- headgate_weight: bfloat16 [2048, 16], P('dp', 'mp'), may hold values from -0.125 to 0.125
- output_weight: bfloat16 [2048, 2048], P('mp', 'dp'), may hold values from -0.75 to 0.75
- gate_weight: bfloat16 [2048, 6144], P('dp', 'mp'), may hold values from -0.125 to 0.125
- up_weight: bfloat16 [2048, 6144], P('dp', 'mp'), may hold values from -0.125 to 0.125
- down_weight: bfloat16 [6144, 2048], P('mp', 'dp'), may hold values from -0.078125 to 0.078125
Outputs:
- layer_out: bfloat16 [8192, 2048], P(('dp', 'mp'))
- input_grad: bfloat16 [8192, 2048], P(('dp', 'mp'))
- attn_gain_grad: float32 [2048], P(('dp', 'mp'))
- mlp_gain_grad: float32 [2048], P(('dp', 'mp'))
- query_gain_grad: float32 [128], P(('dp', 'mp'))
- key_gain_grad: float32 [128], P(('dp', 'mp'))
- query_weight_grad: float32 [2048, 2048], P('dp', 'mp')
- key_weight_grad: float32 [2048, 1024], P('dp', 'mp')
- value_weight_grad: float32 [2048, 1024], P('dp', 'mp')
- headgate_weight_grad: float32 [2048, 16], P('dp', 'mp')
- output_weight_grad: float32 [2048, 2048], P('mp', 'dp')
- gate_weight_grad: float32 [2048, 6144], P('dp', 'mp')
- up_weight_grad: float32 [2048, 6144], P('dp', 'mp')
- down_weight_grad: float32 [6144, 2048], P('mp', 'dp')
Inputs may be any that keep to these rules, and one draw needn't show every extreme that they name: Segments are numbered in token order and segment 0 is a tree's root: parents[t, s] is 0 for s <= 1 and s - 1 or s - 2 for s >= 2. `lengths`: each row sums to 4096.
All inputs are finite; a program needn't handle non-finite values.
Results may differ from a plain program's by a relative error of at most 0.035.
Values may be sent and summed in bfloat16 or wider, within the bound.
A program may use at most 256 MiB of HBM per device.

v0:
```python
from functools import partial

import jax
import jax.numpy as jnp
from jax import lax
from jax.sharding import PartitionSpec as P

HEAD_SIZE = 128
TREE_TOKENS = 4096


EPS = 1e-06
THETA = 1000000.0


def shifted(value, axis, steps):
    count = lax.axis_size(axis)
    initial, last = (max(0, -steps), min(count, count - steps))
    return lax.ppermute(value, axis, [(source, source + steps) for source in range(initial, last)])


def row_norm(values, gain):
    scale = lax.rsqrt(jnp.mean(values * values, axis=-1, keepdims=True) + EPS)
    return values * scale * gain


def rotate(values):
    half = values.shape[-1] // 2
    return jnp.concatenate([-values[..., half:], values[..., :half]], axis=-1)


def rope_tables(positions, width):
    half = width // 2
    freqs = THETA ** (-(jnp.arange(half, dtype=jnp.float32) / half))
    angle = positions.astype(jnp.float32)[:, None] * freqs[None, :]
    angle = jnp.concatenate([angle, angle], axis=-1)
    return (jnp.cos(angle)[:, None, :], jnp.sin(angle)[:, None, :])


def prepare_heads(raw, gain, cosine_table, sine_table):
    normed = row_norm(raw, gain)
    return normed * cosine_table + rotate(normed) * sine_table


def swiglu(gate, up):
    return jax.nn.silu(gate) * up


def gating(attn, logit):
    return attn * jax.nn.sigmoid(logit)[..., None]


def ancestors(parent_row, count):
    table = jnp.eye(count, dtype=jnp.int32)
    for seg_index in range(1, count):
        joined = jnp.maximum(table[seg_index], table[parent_row[seg_index]])
        table = table.at[seg_index].set(joined)
    return table


def segment_onehot(offsets, starts, count):
    segment = jnp.sum((offsets[:, None] >= starts[None, 1:]).astype(jnp.int32), axis=1)
    return (segment[:, None] == jnp.arange(count, dtype=jnp.int32)[None, :]).astype(jnp.int32)


def inner(left, right):
    return lax.dot_general(
        left, right, (((0,), (0,)), ((), ())), preferred_element_type=jnp.float32
    )


def against(left, right):
    return lax.dot_general(
        left, right, (((1,), (1,)), ((), ())), preferred_element_type=jnp.float32
    )


def fetch_attention(query_weight, key_matrix, value_matrix, headgate_weight, output_weight):
    return (
        lax.all_gather(query_weight, "dp", axis=0, tiled=True),
        lax.all_gather(key_matrix, "dp", axis=0, tiled=True),
        lax.all_gather(value_matrix, "dp", axis=0, tiled=True),
        lax.all_gather(headgate_weight, "dp", axis=0, tiled=True),
        lax.all_gather(output_weight, "dp", axis=1, tiled=True),
    )


def fetch_mlp(gate_weight, up_weight, down_weight):
    return (
        lax.all_gather(gate_weight, "dp", axis=0, tiled=True),
        lax.all_gather(up_weight, "dp", axis=0, tiled=True),
        lax.all_gather(down_weight, "dp", axis=1, tiled=True),
    )


def gather_rows(rows):
    return lax.all_gather(rows, "mp", axis=0, tiled=True)


def spread_sums(terms):
    return lax.psum_scatter(
        terms.astype(jnp.bfloat16), "mp", scatter_dimension=0, tiled=True
    ).astype(jnp.float32)


def per_device(
    layer_in,
    out_grad,
    parents,
    lengths,
    attn_gain,
    mlp_gain,
    query_norm_gain,
    key_gain,
    query_weight,
    key_matrix,
    value_matrix,
    headgate_weight,
    output_weight,
    gate_weight,
    up_weight,
    down_weight,
):
    model_count = lax.axis_size("mp")
    share = layer_in.shape[0]
    tok_count = share * model_count
    blocks = TREE_TOKENS // tok_count
    seg_count = parents.shape[1]
    scale = HEAD_SIZE ** (-0.5)
    bf = jnp.bfloat16
    f32 = jnp.float32
    gains = (
        lax.all_gather(attn_gain, ("dp", "mp"), axis=0, tiled=True),
        lax.all_gather(mlp_gain, ("dp", "mp"), axis=0, tiled=True),
        lax.all_gather(query_norm_gain, ("dp", "mp"), axis=0, tiled=True),
        lax.all_gather(key_gain, ("dp", "mp"), axis=0, tiled=True),
    )
    gain_one = gains[0].astype(f32)
    gain_two = gains[1].astype(f32)
    gain_query = gains[2].astype(f32)
    gain_key = gains[3].astype(f32)
    first = lax.axis_index("dp") * tok_count
    tree = first // TREE_TOKENS
    piece = lax.axis_index("dp") % blocks
    parent_row = lax.dynamic_index_in_dim(parents, tree, 0, keepdims=False)
    length_row = lax.dynamic_index_in_dim(lengths, tree, 0, keepdims=False)
    starts = jnp.cumsum(length_row) - length_row
    table = ancestors(parent_row, seg_count)
    depth = jnp.sum(table * length_row[None, :], axis=1) - length_row
    offsets = first - tree * TREE_TOKENS + jnp.arange(tok_count, dtype=jnp.int32)
    onehot = segment_onehot(offsets, starts, seg_count)
    positions = jnp.sum(onehot * (depth - starts)[None, :], axis=1) + offsets
    reach = jnp.dot(onehot, table, preferred_element_type=jnp.int32)
    cosine_table, sine_table = rope_tables(positions, HEAD_SIZE)

    def visible(step):
        keys_at = offsets - step * tok_count
        key_hot = segment_onehot(keys_at, starts, seg_count)
        linked = jnp.dot(reach, key_hot.T, preferred_element_type=jnp.int32) > 0
        return linked & (keys_at[None, :] >= 0) & (keys_at[None, :] <= offsets[:, None])

    full_query, full_key, full_value, full_headgate, full_output = fetch_attention(
        query_weight, key_matrix, value_matrix, headgate_weight, output_weight
    )
    rows = layer_in.astype(f32)
    normed_one, norm_one_back = jax.vjp(row_norm, rows, gain_one)
    hidden_first = gather_rows(normed_one.astype(bf))
    query_unnormed = jnp.dot(hidden_first, full_query, preferred_element_type=f32).reshape(
        tok_count, -1, HEAD_SIZE
    )
    key_unnormed = jnp.dot(hidden_first, full_key, preferred_element_type=f32).reshape(
        tok_count, -1, HEAD_SIZE
    )
    value_rows = (
        jnp.dot(hidden_first, full_value, preferred_element_type=f32)
        .astype(bf)
        .reshape(tok_count, -1, HEAD_SIZE)
    )
    logit = jnp.dot(hidden_first, full_headgate, preferred_element_type=f32)
    kv_heads = key_unnormed.shape[1]
    group = query_unnormed.shape[1] // kv_heads
    prepare = partial(prepare_heads, cosine_table=cosine_table, sine_table=sine_table)
    query_f, query_back = jax.vjp(prepare, query_unnormed, gain_query)
    key_f, key_back = jax.vjp(prepare, key_unnormed, gain_key)
    query_rows = query_f.astype(bf).reshape(tok_count, kv_heads, group, HEAD_SIZE)
    key = key_f.astype(bf)

    def scores(key_block, step):
        raw = (
            jnp.einsum("qkgd,tkd->kgqt", query_rows, key_block, preferred_element_type=f32) * scale
        )
        return jnp.where(visible(step)[None, None], raw, -1e30)

    local_scores = scores(key, 0)
    top_first = jnp.max(local_scores, axis=-1)
    total_first = jnp.sum(jnp.exp(local_scores - top_first[..., None]), axis=-1)

    def collect(carry, step):
        key_block, value_block, top, total = carry
        key_block, value_block = shifted((key_block, value_block), "dp", 1)

        def take(operands):
            block, old_top, old_total = operands
            block_scores = scores(block, step)
            new_top = jnp.maximum(old_top, jnp.max(block_scores, axis=-1))
            new_total = old_total * jnp.exp(old_top - new_top) + jnp.sum(
                jnp.exp(block_scores - new_top[..., None]), axis=-1
            )
            return (new_top, new_total)

        def leave(operands):
            return (operands[1], operands[2])

        top, total = lax.cond(step <= piece, take, leave, (key_block, top, total))
        return ((key_block, value_block, top, total), (key_block, value_block))

    later = jnp.arange(1, blocks, dtype=jnp.int32)
    (_, _, top, total), (keys_in, values_in) = lax.scan(
        collect, (key, value_rows, top_first, total_first), later
    )
    logsum = top + jnp.log(total)
    key_stack = jnp.concatenate([key[None], keys_in], axis=0)
    value_stack = jnp.concatenate([value_rows[None], values_in], axis=0)
    every = jnp.arange(blocks, dtype=jnp.int32)

    def weigh(key_block, step):
        return jnp.exp(scores(key_block, step) - logsum[..., None])

    def attend(carry, item):
        key_block, value_block, step = item

        def attend_add_block(total_sum):
            prob = weigh(key_block, step).astype(bf)
            return total_sum + jnp.einsum(
                "kgqt,tkd->qkgd", prob, value_block, preferred_element_type=f32
            )

        return (lax.cond(step <= piece, attend_add_block, lambda total_sum: total_sum, carry), None)

    attn_init = jnp.zeros((tok_count, kv_heads, group, HEAD_SIZE), f32)
    attn, _ = lax.scan(attend, attn_init, (key_stack, value_stack, every))
    attn = attn.reshape(tok_count, -1, HEAD_SIZE)
    mixed_f, gate_back = jax.vjp(gating, attn, logit)
    mixed = mixed_f.astype(bf).reshape(tok_count, -1)
    middle = rows + spread_sums(jnp.dot(mixed, full_output, preferred_element_type=f32))
    full_gate, full_up, full_down = fetch_mlp(gate_weight, up_weight, down_weight)
    normed_two, norm_two_back = jax.vjp(row_norm, middle, gain_two)
    h_two = gather_rows(normed_two.astype(bf))
    gate = jnp.dot(h_two, full_gate, preferred_element_type=f32)
    up = jnp.dot(h_two, full_up, preferred_element_type=f32)
    hidden_f, glu_back = jax.vjp(swiglu, gate, up)
    hidden = hidden_f.astype(bf)
    layer_out = (
        middle + spread_sums(jnp.dot(hidden, full_down, preferred_element_type=f32))
    ).astype(bf)
    full_gate, full_up, full_down = fetch_mlp(gate_weight, up_weight, down_weight)
    full_query, full_key, full_value, full_headgate, full_output = fetch_attention(
        query_weight, key_matrix, value_matrix, headgate_weight, output_weight
    )
    grad_tokens = gather_rows(out_grad)
    down_grad = inner(hidden, grad_tokens)
    grad_hidden = against(grad_tokens, full_down)
    grad_gate_f, grad_up_f = glu_back(grad_hidden)
    grad_gate = grad_gate_f.astype(bf)
    grad_up = grad_up_f.astype(bf)
    gate_grad = inner(h_two, grad_gate)
    up_grad = inner(h_two, grad_up)
    grad_h_two = spread_sums(against(grad_gate, full_gate) + against(grad_up, full_up))
    grad_mid_norm, gain_two_grad = norm_two_back(grad_h_two)
    grad_middle = out_grad.astype(f32) + grad_mid_norm
    mlp_sums = (
        lax.psum_scatter(gate_grad, "dp", scatter_dimension=0, tiled=True),
        lax.psum_scatter(up_grad, "dp", scatter_dimension=0, tiled=True),
        lax.psum_scatter(down_grad, "dp", scatter_dimension=1, tiled=True),
    )
    grad_branch = gather_rows(grad_middle.astype(bf))
    output_grad = inner(mixed, grad_branch)
    grad_mixed = against(grad_branch, full_output).reshape(tok_count, -1, HEAD_SIZE)
    grad_attn_f, grad_logit_f = gate_back(grad_mixed)
    grad_attn = grad_attn_f.astype(bf).reshape(tok_count, kv_heads, group, HEAD_SIZE)
    grad_logit = grad_logit_f.astype(bf)

    def grad_probs(value_block):
        return jnp.einsum("qkgd,tkd->kgqt", grad_attn, value_block, preferred_element_type=f32)

    def settle(carry, item):
        key_block, value_block, step = item

        def settle_add_block(total_sum):
            prob = weigh(key_block, step)
            return total_sum + jnp.sum(prob * grad_probs(value_block), axis=-1)

        return (lax.cond(step <= piece, settle_add_block, lambda total_sum: total_sum, carry), None)

    delta, _ = lax.scan(settle, jnp.zeros_like(logsum), (key_stack, value_stack, every))

    def block_grads(operands):
        key_block, value_block, step = operands
        prob = weigh(key_block, step)
        grad_score = (prob * (grad_probs(value_block) - delta[..., None])).astype(bf)
        query_part = (
            jnp.einsum("kgqt,tkd->qkgd", grad_score, key_block, preferred_element_type=f32) * scale
        )
        key_part = (
            jnp.einsum("kgqt,qkgd->tkd", grad_score, query_rows, preferred_element_type=f32) * scale
        )
        value_part = jnp.einsum(
            "kgqt,qkgd->tkd", prob.astype(bf), grad_attn, preferred_element_type=f32
        )
        return (query_part, key_part, value_part)

    def no_grads(operands):
        return (
            jnp.zeros((tok_count, kv_heads, group, HEAD_SIZE), f32),
            jnp.zeros((tok_count, kv_heads, HEAD_SIZE), f32),
            jnp.zeros((tok_count, kv_heads, HEAD_SIZE), f32),
        )

    def masked_grads(key_block, value_block, step):
        return lax.cond(step <= piece, block_grads, no_grads, (key_block, value_block, step))

    last = blocks - 1
    start_grads = masked_grads(key_stack[last], value_stack[last], every[last])

    def return_grads(carry, item):
        query_sum, key_sum, value_sum = carry
        key_block, value_block, step = item
        key_sum, value_sum = (
            shifted(key_sum.astype(jnp.bfloat16), "dp", -1).astype(key_sum.dtype),
            shifted(value_sum.astype(jnp.bfloat16), "dp", -1).astype(value_sum.dtype),
        )
        query_part, key_part, value_part = masked_grads(key_block, value_block, step)
        return ((query_sum + query_part, key_sum + key_part, value_sum + value_part), None)

    (grad_query, grad_key, grad_value), _ = lax.scan(
        return_grads,
        start_grads,
        (key_stack[:last], value_stack[:last], every[:last]),
        reverse=True,
    )
    grad_q_raw_f, query_gain_grad = query_back(grad_query.reshape(tok_count, -1, HEAD_SIZE))
    grad_k_raw_f, key_gain_grad = key_back(grad_key)
    grad_q_raw = grad_q_raw_f.astype(bf).reshape(tok_count, -1)
    grad_k_raw = grad_k_raw_f.astype(bf).reshape(tok_count, -1)
    grad_v = grad_value.astype(bf).reshape(tok_count, -1)
    query_grad = inner(hidden_first, grad_q_raw)
    key_grad = inner(hidden_first, grad_k_raw)
    value_grad = inner(hidden_first, grad_v)
    headgate_grad = inner(hidden_first, grad_logit)
    grad_h_one = against(grad_q_raw, full_query) + against(grad_k_raw, full_key)
    grad_h_one = grad_h_one + against(grad_v, full_value) + against(grad_logit, full_headgate)
    grad_h_one = spread_sums(grad_h_one)
    grad_in_norm, gain_one_grad = norm_one_back(grad_h_one)
    input_grad = (grad_middle + grad_in_norm).astype(bf)
    attn_sums = (
        lax.psum_scatter(query_grad, "dp", scatter_dimension=0, tiled=True),
        lax.psum_scatter(key_grad, "dp", scatter_dimension=0, tiled=True),
        lax.psum_scatter(value_grad, "dp", scatter_dimension=0, tiled=True),
        lax.psum_scatter(headgate_grad, "dp", scatter_dimension=0, tiled=True),
        lax.psum_scatter(output_grad, "dp", scatter_dimension=1, tiled=True),
    )
    gain_sums = (
        lax.psum_scatter(gain_one_grad, ("dp", "mp"), scatter_dimension=0, tiled=True),
        lax.psum_scatter(gain_two_grad, ("dp", "mp"), scatter_dimension=0, tiled=True),
        lax.psum_scatter(query_gain_grad, ("dp", "mp"), scatter_dimension=0, tiled=True),
        lax.psum_scatter(key_gain_grad, ("dp", "mp"), scatter_dimension=0, tiled=True),
    )
    return (
        layer_out,
        input_grad,
        gain_sums[0],
        gain_sums[1],
        gain_sums[2],
        gain_sums[3],
        attn_sums[0],
        attn_sums[1],
        attn_sums[2],
        attn_sums[3],
        attn_sums[4],
        mlp_sums[0],
        mlp_sums[1],
        mlp_sums[2],
    )


def solution(mesh):
    in_specs = (
        P(("dp", "mp"), None),
        P(("dp", "mp"), None),
        P(),
        P(),
        P(("dp", "mp")),
        P(("dp", "mp")),
        P(("dp", "mp")),
        P(("dp", "mp")),
        P("dp", "mp"),
        P("dp", "mp"),
        P("dp", "mp"),
        P("dp", "mp"),
        P("mp", "dp"),
        P("dp", "mp"),
        P("dp", "mp"),
        P("mp", "dp"),
    )
    out_specs = (
        P(("dp", "mp"), None),
        P(("dp", "mp"), None),
        P(("dp", "mp")),
        P(("dp", "mp")),
        P(("dp", "mp")),
        P(("dp", "mp")),
        P("dp", "mp"),
        P("dp", "mp"),
        P("dp", "mp"),
        P("dp", "mp"),
        P("mp", "dp"),
        P("dp", "mp"),
        P("dp", "mp"),
        P("mp", "dp"),
    )
    return jax.shard_map(
        per_device, mesh=mesh, in_specs=in_specs, out_specs=out_specs, check_vma=False
    )
```

profile of v0, /device:TPU:0, one launch (start us, length us, event | category | flops | bytes accessed | tf_op | source)
XLA Modules:
  0.0 3442.3 jit_solution(13352091678694354629)
XLA Ops:
  10.7 42.2 %all-reduce.13 = (bf16[128]{0:T(256)(128)(2,1)S(1)}, bf16[2048]{0:T(1024)(128)(2,1)S(1)}, bf16[128]{0:T(256)(128)(2,1)S(1)}, bf16[2048]{0:T(1024)(128)(2,1)S(1)}) all-reduce(bf16[128]{0:T(256)(128)(2,1)S(1)} %dynamic-update-slice.19, bf16[2048]{0:T(1024)(128)(2,1)S(1)} %dynamic-update-slice.18, ...), channel_id=1, replica_groups=mesh['dp'=16,'mp'=2] {'dp','mp'}, use_global_device_ids=true, to_apply=%add.5 | all-reduce | flops 4352 | bytes 17408
  78.1 40.0 %all_gather.63 = bf16[2048,8]{0,1:T(8,128)(2,1)S(1)} all-gather(bf16[128,8]{0,1:T(8,128)(2,1)S(1)} %copy-done.84), channel_id=1, replica_groups=mesh['dp'=16,'mp'=2] {'dp'}, dimensions={0}, use_global_device_ids=true | all-gather | bytes 34816 | tf_op jit(solution)/shard_map/all_gather | solution.py:83
  140.2 53.8 %all-gather.16.cloned.1.call-done = bf16[2048,512]{1,0:T(8,128)(2,1)} async-done(((bf16[128,512]{1,0:T(8,128)(2,1)}), bf16[2048,512]{1,0:T(8,128)(2,1)}) %all-gather.16.cloned.1.call-update) | async-done | bytes 2097168 | tf_op jit(solution)/shard_map/all_gather | solution.py:82
  206.5 64.6 %all-gather.18.cloned.1.call-done = bf16[2048,1024]{1,0:T(8,128)(2,1)} async-done(((bf16[128,1024]{1,0:T(8,128)(2,1)}), bf16[2048,1024]{1,0:T(8,128)(2,1)}) %all-gather.18.cloned.1.call-update) | async-done | bytes 4194320 | tf_op jit(solution)/shard_map/all_gather | solution.py:80
  298.3 215.2 %while.74 = (s32[]{:T(128)}, bf16[512,4,128]{2,0,1:T(8,128)(2,1)S(1)}, bf16[512,4,128]{2,1,0:T(4,128)(2,1)S(1)}, f32[4,2,512]{2,1,0:T(2,128)S(1)}, f32[4,2,512]{...) while((s32[]{:T(128)}, ...), condition=%wide.region_15.16_spmd.clone, body=%wide.region_9.15_spmd.clone.sunk | while | flops 556291584 | bytes 27772364 | solution.py:218
  552.0 87.9 %reduce-scatter.13.cloned.1.call-done = bf16[256,2048]{1,0:T(8,128)(2,1)} async-done(((bf16[512,2048]{1,0:T(8,128)(2,1)}), bf16[256,2048]{1,0:T(8,128)(2,1)}) %reduce-scatter.13.cloned.1.call-update) | async-done | bytes 1048592 | tf_op jit(solution)/shard_map/reduce_scatter | solution.py:101
  656.2 155.4 %all-gather.24.cloned.1.call-done = bf16[2048,3072]{1,0:T(8,128)(2,1)} async-done(((bf16[128,3072]{1,0:T(8,128)(2,1)}), bf16[2048,3072]{1,0:T(8,128)(2,1)}) %all-gather.24.cloned.1.call-update) | async-done | bytes 12582928 | tf_op jit(solution)/shard_map/all_gather | solution.py:90
  823.5 140.5 %all-gather.26.cloned.1.call-done = bf16[2048,3072]{1,0:T(8,128)(2,1)} async-done(((bf16[128,3072]{1,0:T(8,128)(2,1)}), bf16[2048,3072]{1,0:T(8,128)(2,1)}) %all-gather.26.cloned.1.call-update) | async-done | bytes 12582928 | tf_op jit(solution)/shard_map/all_gather | solution.py:91
  975.9 197.6 %all-gather.28.cloned.1.call-done = bf16[3072,2048]{1,0:T(8,128)(2,1)} async-done(((bf16[3072,128]{1,0:T(8,128)(2,1)}), bf16[3072,2048]{1,0:T(8,128)(2,1)}) %all-gather.28.cloned.1.call-update) | async-done | bytes 12582928 | tf_op jit(solution)/shard_map/all_gather | solution.py:92
  1256.3 22.7 while.76
  1283.7 321.4 %while.77 = (s32[]{:T(128)}, f32[512,4,2,128]{3,0,2,1:T(8,128)S(1)}, f32[512,4,128]{2,0,1:T(8,128)}, bf16[512,4,128]{2,0,1:T(8,128)(2,1)}, s32[7]{0:T(128)S(1)},...) while((s32[]{:T(128)}, ...), condition=%wide.region_39.40_spmd.clone, body=%wide.region_35.39_spmd.clone.sunk | while | flops 2712942080 | bytes 115690648 | solution.py:335
  1295.8 19.8 collective-permute-done.2
  1385.0 19.6 collective-permute-done.2
  1428.6 19.6 collective-permute-done.2
  1550.5 20.8 conditional.17
  1574.5 21.0 collective-permute-done.2
  1715.8 89.8 %all-reduce.12 = (f32[2048]{0:T(1024)S(1)}, f32[2048]{0:T(1024)S(1)}, f32[128]{0:T(128)S(1)}, f32[128]{0:T(128)S(1)}) all-reduce(f32[2048]{0:T(1024)S(1)} %get-tuple-element.1189, f32[2048]{0:T(1024)S(1)} %copy-done.67, f32[128]{0:T(128)S(1)} %get-tuple-element.1187, ...), channel_id=6, replica_groups=mesh['dp'=16,'mp'=2] {'dp','mp'}, use_global_device_ids=true, to_apply=%region_46.47.clone | all-reduce | flops 4352 | bytes 34816
  1813.1 65.7 %reduce-scatter.23.cloned.1.call-done = f32[128,512]{1,0:T(8,128)} async-done(((f32[2048,512]{1,0:T(8,128)}), f32[128,512]{1,0:T(8,128)}) %reduce-scatter.23.cloned.1.call-update) | async-done | bytes 262160 | tf_op jit(solution)/shard_map/reduce_scatter | solution.py:357
  1878.9 97.5 %reduce-scatter.25.cloned.1.call-done = f32[128,512]{1,0:T(8,128)} async-done(((f32[2048,512]{1,0:T(8,128)}), f32[128,512]{1,0:T(8,128)}) %reduce-scatter.25.cloned.1.call-update) | async-done | bytes 262160 | tf_op jit(solution)/shard_map/reduce_scatter | solution.py:358
  1976.4 180.3 %reduce-scatter.21.cloned.1.call-done = f32[128,1024]{1,0:T(8,128)} async-done(((f32[2048,1024]{1,0:T(8,128)}), f32[128,1024]{1,0:T(8,128)}) %reduce-scatter.21.cloned.1.call-update) | async-done | bytes 524304 | tf_op jit(solution)/shard_map/reduce_scatter | solution.py:356
  2156.6 183.0 %reduce-scatter.29.cloned.1.call-done = f32[1024,128]{1,0:T(8,128)} async-done(((f32[1024,2048]{1,0:T(8,128)}), f32[1024,128]{1,0:T(8,128)}) %reduce-scatter.29.cloned.1.call-update) | async-done | bytes 524304 | tf_op jit(solution)/shard_map/reduce_scatter | solution.py:360
  2339.7 367.4 %reduce-scatter.31.cloned.1.call-done = f32[128,3072]{1,0:T(8,128)} async-done(((f32[2048,3072]{1,0:T(8,128)}), f32[128,3072]{1,0:T(8,128)}) %reduce-scatter.31.cloned.1.call-update) | async-done | bytes 1572880 | tf_op jit(solution)/shard_map/reduce_scatter | solution.py:272
  2707.1 364.0 %reduce-scatter.33.cloned.1.call-done = f32[128,3072]{1,0:T(8,128)} async-done(((f32[2048,3072]{1,0:T(8,128)}), f32[128,3072]{1,0:T(8,128)}) %reduce-scatter.33.cloned.1.call-update) | async-done | bytes 1572880 | tf_op jit(solution)/shard_map/reduce_scatter | solution.py:273
  3071.1 364.2 %reduce-scatter.35.cloned.1.call-done = f32[3072,128]{1,0:T(8,128)} async-done(((f32[3072,2048]{1,0:T(8,128)}), f32[3072,128]{1,0:T(8,128)}) %reduce-scatter.35.cloned.1.call-update) | async-done | bytes 1572880 | tf_op jit(solution)/shard_map/reduce_scatter | solution.py:274
  (648 shorter events, 871.3 us)
Async XLA Ops:
  7.2 110.9 %all-gather.12.cloned.1.call-start = ((), (), s32[]{:S(2)}) async-start(), calls=%async_computation.12 | async-start | bytes 3145728 | tf_op jit(solution)/shard_map/all_gather | solution.py:97
  56.9 75.1 %all-gather.14.cloned.1.call-start = ((), (), s32[]{:S(2)}) async-start(), calls=%async_computation.13 | async-start | bytes 2228224 | tf_op jit(solution)/shard_map/all_gather | solution.py:81
  57.7 136.4 %all-gather.16.cloned.1.call-start = ((), (), s32[]{:S(2)}) async-start(), calls=%async_computation.14 | async-start | bytes 2228224 | tf_op jit(solution)/shard_map/all_gather | solution.py:82
  58.4 212.7 %all-gather.18.cloned.1.call-start = ((), (), s32[]{:S(2)}) async-start(), calls=%async_computation.15 | async-start | bytes 4456448 | tf_op jit(solution)/shard_map/all_gather | solution.py:80
  59.0 486.6 %all-gather.20.cloned.1.call-start = ((), (), s32[]{:S(2)}) async-start(), calls=%async_computation.16 | async-start | bytes 4456448 | tf_op jit(solution)/shard_map/all_gather | solution.py:84
  59.6 580.3 %reduce-scatter.13.cloned.1.call-start = ((), (), s32[]{:S(2)}) async-start(), calls=%async_computation.17 | async-start | bytes 3145728 | tf_op jit(solution)/shard_map/reduce_scatter | solution.py:101
  552.0 104.2 %all-gather.22.cloned.1.call-start = ((), (), s32[]{:S(2)}) async-start(), calls=%async_computation.18 | async-start | bytes 3145728 | tf_op jit(solution)/shard_map/all_gather | solution.py:97
  644.2 167.4 %all-gather.24.cloned.1.call-start = ((), (), s32[]{:S(2)}) async-start(), calls=%async_computation.19 | async-start | bytes 13369344 | tf_op jit(solution)/shard_map/all_gather | solution.py:90
  644.9 319.1 %all-gather.26.cloned.1.call-start = ((), (), s32[]{:S(2)}) async-start(), calls=%async_computation.20 | async-start | bytes 13369344 | tf_op jit(solution)/shard_map/all_gather | solution.py:91
  645.7 330.3 %all-gather.30.cloned.1.call-start = ((), (), s32[]{:S(2)}) async-start(), calls=%async_computation.23 | async-start | bytes 3145728 | tf_op jit(solution)/shard_map/all_gather | solution.py:97
  646.2 527.3 %all-gather.28.cloned.1.call-start = ((), (), s32[]{:S(2)}) async-start(), calls=%async_computation.21 | async-start | bytes 13369344 | tf_op jit(solution)/shard_map/all_gather | solution.py:92
  647.0 577.7 %reduce-scatter.17.cloned.1.call-start = ((), (), s32[]{:S(2)}) async-start(), calls=%async_computation.24 | async-start | bytes 3145728 | tf_op jit(solution)/shard_map/reduce_scatter | solution.py:101
  1229.7 482.6 %reduce-scatter.19.cloned.1.call-start = ((), (), s32[]{:S(2)}) async-start(), calls=%async_computation.26 | async-start | bytes 3145728 | tf_op jit(solution)/shard_map/reduce_scatter | solution.py:101
  1546.7 48.8 %collective-permute-start.2 = (bf16[512,4,128]{2,0,1:T(8,128)(2,1)}, bf16[512,4,128]{2,0,1:T(8,128)(2,1)}, u32[]{:S(2)}, u32[]{:S(2)}) collective-permute-start(bf16[512,4,128]{2,0,1:T(8,128)(2,1)} %convert_element_type.423), channel_id=1, source_target_pairs={{2,0},{4,2},{6,4},{8,6},{10,8},{12,10},{14,12},{16,14},{18,16},{20... | collective-permute-start | bytes 1572872 | tf_op jit(solution)/shard_map/while/body/eval_jaxpr/ppermute | solution.py:19
  1548.0 54.9 %collective-permute-start.3 = (bf16[512,4,128]{2,0,1:T(8,128)(2,1)}, bf16[512,4,128]{2,0,1:T(8,128)(2,1)}, u32[]{:S(2)}, u32[]{:S(2)}) collective-permute-start(bf16[512,4,128]{2,0,1:T(8,128)(2,1)} %get-tuple-element.1825), channel_id=1, source_target_pairs={{2,0},{4,2},{6,4},{8,6},{10,8},{12,10},{14,12},{16,14},{18,16},{20... | collective-permute-start | bytes 1572872 | tf_op jit(solution)/shard_map/while/body/eval_jaxpr/ppermute | solution.py:19
  1631.8 176.1 %reduce-scatter.15.cloned.1.call-start = ((), (), s32[]{:S(2)}) async-start(), calls=%async_computation.22 | async-start | bytes 3145728 | tf_op jit(solution)/shard_map/reduce_scatter | solution.py:101
  1643.6 169.5 %reduce-scatter.27.cloned.1.call-start = ((), (), s32[]{:S(2)}) async-start(), calls=%async_computation.30 | async-start | bytes 69632 | tf_op jit(solution)/shard_map/reduce_scatter | solution.py:359
  1644.7 234.2 %reduce-scatter.23.cloned.1.call-start = ((), (), s32[]{:S(2)}) async-start(), calls=%async_computation.28 | async-start | bytes 4456448 | tf_op jit(solution)/shard_map/reduce_scatter | solution.py:357
  1648.5 327.9 %reduce-scatter.25.cloned.1.call-start = ((), (), s32[]{:S(2)}) async-start(), calls=%async_computation.29 | async-start | bytes 4456448 | tf_op jit(solution)/shard_map/reduce_scatter | solution.py:358
  1652.8 503.9 %reduce-scatter.21.cloned.1.call-start = ((), (), s32[]{:S(2)}) async-start(), calls=%async_computation.27 | async-start | bytes 8912896 | tf_op jit(solution)/shard_map/reduce_scatter | solution.py:356
  1659.7 680.0 %reduce-scatter.29.cloned.1.call-start = ((), (), s32[]{:S(2)}) async-start(), calls=%async_computation.31 | async-start | bytes 8912896 | tf_op jit(solution)/shard_map/reduce_scatter | solution.py:360
  1667.4 1039.7 %reduce-scatter.31.cloned.1.call-start = ((), (), s32[]{:S(2)}) async-start(), calls=%async_computation.32 | async-start | bytes 26738688 | tf_op jit(solution)/shard_map/reduce_scatter | solution.py:272
  1682.7 1388.4 %reduce-scatter.33.cloned.1.call-start = ((), (), s32[]{:S(2)}) async-start(), calls=%async_computation.33 | async-start | bytes 26738688 | tf_op jit(solution)/shard_map/reduce_scatter | solution.py:273
  1696.7 1738.6 %reduce-scatter.35.cloned.1.call-start = ((), (), s32[]{:S(2)}) async-start(), calls=%async_computation.34 | async-start | bytes 26738688 | tf_op jit(solution)/shard_map/reduce_scatter | solution.py:274
  (130 other events, 6720.9 us)
Sparse Core Ops, SparseCore 0:
  57.0 10.4 all-gather.11
  70.3 61.7 all-gather.13
  134.8 59.1 all-gather.15
  196.7 74.3 all-gather.17
  273.6 117.1 all-gather.19
  552.1 87.7 reduce-scatter.12
  644.3 11.8 all-gather.21
  659.0 152.5 all-gather.23
  814.4 149.5 all-gather.25
  965.4 8.7 all-gather.29
  976.9 196.6 all-gather.27
  1216.7 7.9 reduce-scatter.16
  1229.9 11.8 all-gather.31
  1631.9 57.2 reduce-scatter.18
  1691.2 11.0 reduce-scatter.14
  1705.0 78.2 reduce-scatter.26
  1786.0 92.8 reduce-scatter.22
  1881.6 94.7 reduce-scatter.24
  1979.2 177.3 reduce-scatter.20
  2159.4 180.2 reduce-scatter.28
  2346.0 361.0 reduce-scatter.30
  2713.4 357.6 reduce-scatter.32
  3077.4 357.8 reduce-scatter.34
where the time goes:
time: 3450 us; the launch traced here: 3440 us
  waiting for transfers between devices  2640 us (77%)
  matrix products  216 us (6%)
  blocking collectives  172 us (5%)
  other arithmetic  138 us (4%)
  starting transfers between devices  114 us (3%)
  local copies, waits for them, and re-layouts  108 us (3%)
    reduce_scatter x1, waiting for transfers between devices, per_device(): lax.psum_scatter(gate_grad, 'dp', scatter_dimension=0, tiled=True)  367 us
    reduce_scatter x1, waiting for transfers between devices, per_device(): lax.psum_scatter(down_grad, 'dp', scatter_dimension=1, tiled=True)  364 us
    reduce_scatter x1, waiting for transfers between devices, per_device(): lax.psum_scatter(up_grad, 'dp', scatter_dimension=0, tiled=True)  364 us
    ppermute x28, waiting for transfers between devices, shifted(): lax.ppermute(value, axis, [(source, source + steps) for source in range(i...  282 us
    all_gather x1, waiting for transfers between devices, fetch_mlp(): lax.all_gather(down_weight, 'dp', axis=1, tiled=True)  198 us
    reduce_scatter x1, waiting for transfers between devices, per_device(): lax.psum_scatter(output_grad, 'dp', scatter_dimension=1, tiled=True)  183 us
    reduce_scatter x1, waiting for transfers between devices, per_device(): lax.psum_scatter(query_grad, 'dp', scatter_dimension=0, tiled=True)  180 us
    all_gather x1, waiting for transfers between devices, fetch_mlp(): lax.all_gather(gate_weight, 'dp', axis=0, tiled=True)  155 us
  transfers between devices with their start and end apart: 51, of which 44 were waited for; matrix products, arithmetic and copies ran while one was open for 8% of the time, Pallas kernels for 0%

commit v1 on v0

v1 whole, which is shorter than its diff:
```python
from functools import partial

import jax
import jax.numpy as jnp
from jax import lax
from jax.experimental import pallas as pl
from jax.experimental.pallas import tpu as pltpu
from jax.sharding import PartitionSpec as P

HEAD_SIZE = 128
TREE_TOKENS = 4096
EPS = 1e-06
THETA = 1000000.0
f32 = jnp.float32
bf = jnp.bfloat16

LOG2E=1.4426950408889634
BQ=256
BK=512
NT=(((1,),(1,)),((),()))
NN=(((1,),(0,)),((),()))
TN=(((0,),(0,)),((),()))
def dg(a,b,d): return lax.dot_general(a,b,d,preferred_element_type=f32)

def attn_forward_body(base, flags, q_ref, k_ref, v_ref, qbit_ref, kbit_ref, o_ref, l_ref, acc, tot):
    qb = pl.program_id(0)
    bq = q_ref.shape[0]
    nk, _, bk = kbit_ref.shape
    q = jnp.concatenate([q_ref[:, :HEAD_SIZE], q_ref[:, HEAD_SIZE:]], axis=0)
    acc[...] = jnp.zeros_like(acc)
    tot[...] = jnp.zeros_like(tot)
    factor = LOG2E * HEAD_SIZE ** (-0.5)
    def step(kb, masked):
        rows = pl.ds(pl.multiple_of(kb * bk, bk), bk)
        s = dg(q, k_ref[rows, :], NT) * factor
        if masked:
            seen = (qbit_ref[...] & kbit_ref[kb]) != 0
            at = lax.broadcasted_iota(jnp.int32, (bq, bk), 1) + kb * bk
            row = lax.broadcasted_iota(jnp.int32, (bq, bk), 0) + base + qb * bq
            seen = seen & (at <= row)
            s = jnp.where(jnp.concatenate([seen, seen], axis=0), s, -1e30)
        p = jnp.exp2(s)
        part = p[:, 0:128]
        for i in range(1, bk // 128):
            part = part + p[:, i * 128:(i + 1) * 128]
        tot[...] += part
        acc[...] += dg(p.astype(bf), v_ref[rows, :], NN)
    def body(kb, _):
        flag = flags[qb, kb]
        pl.when(flag == 1)(lambda: step(kb, True))
        pl.when(flag == 2)(lambda: step(kb, False))
        return 0
    lax.fori_loop(0, nk, body, 0)
    total = jnp.sum(tot[...], axis=1, keepdims=True)
    out = acc[...] / total
    o_ref[:, :HEAD_SIZE] = out[:bq]
    o_ref[:, HEAD_SIZE:] = out[bq:]
    lse = jnp.log2(total)
    l_ref[...] = jnp.concatenate([lse[:bq], lse[bq:]], axis=1)

def attn_forward(flags, q, k, v, qbit, kbit):
    T = q.shape[0]; N = k.shape[0]
    nk = N // BK
    return pl.pallas_call(
        partial(attn_forward_body, N - T),
        grid_spec=pltpu.PrefetchScalarGridSpec(
            num_scalar_prefetch=1, grid=(T // BQ,),
            in_specs=[
                pl.BlockSpec((BQ, 256), lambda i, f: (i, 0)),
                pl.BlockSpec((N, 128), lambda i, f: (0, 0)),
                pl.BlockSpec((N, 128), lambda i, f: (0, 0)),
                pl.BlockSpec((BQ, 1), lambda i, f: (i, 0)),
                pl.BlockSpec((nk, 1, BK), lambda i, f: (0, 0, 0)),
            ],
            out_specs=[pl.BlockSpec((BQ, 256), lambda i, f: (i, 0)), pl.BlockSpec((BQ, 2), lambda i, f: (i, 0))],
            scratch_shapes=[pltpu.VMEM((2 * BQ, 128), f32), pltpu.VMEM((2 * BQ, 128), f32)],
        ),
        out_shape=[jax.ShapeDtypeStruct((T, 256), f32), jax.ShapeDtypeStruct((T, 2), f32)],
        cost_estimate=pl.CostEstimate(flops=2*2*T*N*256*3//4, bytes_accessed=8<<20, transcendentals=T*N*3//2),
        name="attn_forward",
    )(flags, q, k, v, qbit, kbit)

def attn_backward_body(base, flags, q_ref, g_ref, k_ref, v_ref, qbit_ref, kbit_ref, lse_ref, del_ref, dq_ref, dk_ref, dv_ref):
    kb = pl.program_id(0)
    bk = k_ref.shape[0]
    T = q_ref.shape[0]
    bq = BQ
    factor = LOG2E * HEAD_SIZE ** (-0.5)
    @pl.when(kb == 0)
    def _():
        dq_ref[...] = jnp.zeros_like(dq_ref)
    dk_ref[...] = jnp.zeros_like(dk_ref)
    dv_ref[...] = jnp.zeros_like(dv_ref)
    def pair(ref, rows):
        return jnp.concatenate([ref[rows, :HEAD_SIZE], ref[rows, HEAD_SIZE:]], axis=0)
    def line(ref, rows):
        return jnp.concatenate([ref[0:1, rows], ref[1:2, rows]], axis=1)
    def step(qb, masked):
        rows = pl.ds(pl.multiple_of(qb * bq, bq), bq)
        q = pair(q_ref, rows)
        g = pair(g_ref, rows)
        k = k_ref[...]
        s = dg(k, q, NT) * factor - line(lse_ref, rows)
        if masked:
            seen = (kbit_ref[...] & qbit_ref[0:1, rows]) != 0
            at = lax.broadcasted_iota(jnp.int32, (bk, bq), 0) + kb * bk
            row = lax.broadcasted_iota(jnp.int32, (bk, bq), 1) + base + qb * bq
            seen = seen & (at <= row)
            s = jnp.where(jnp.concatenate([seen, seen], axis=1), s, -1e30)
        p = jnp.exp2(s)
        dv_ref[...] += dg(p.astype(bf), g, NN)
        dp = dg(v_ref[...], g, NT)
        ds = (p * (dp - line(del_ref, rows))).astype(bf)
        dk_ref[...] += dg(ds, q, NN)
        dq = dg(ds, k, TN)
        dq_ref[rows, :HEAD_SIZE] += dq[:bq]
        dq_ref[rows, HEAD_SIZE:] += dq[bq:]
    def body(qb, _):
        flag = flags[qb, kb]
        pl.when(flag == 1)(lambda: step(qb, True))
        pl.when(flag == 2)(lambda: step(qb, False))
        return 0
    lax.fori_loop(0, T // bq, body, 0)

def attn_backward(flags, q, g, k, v, qbit, kbit, lse, delta):
    T = q.shape[0]; N = k.shape[0]
    nk = N // BK
    whole = lambda *s: pl.BlockSpec(s, lambda i, f: (0,) * len(s))
    return pl.pallas_call(
        partial(attn_backward_body, N - T),
        grid_spec=pltpu.PrefetchScalarGridSpec(
            num_scalar_prefetch=1, grid=(nk,),
            in_specs=[whole(T, 256), whole(T, 256), pl.BlockSpec((BK, 128), lambda i, f: (i, 0)), pl.BlockSpec((BK, 128), lambda i, f: (i, 0)),
                whole(1, T), pl.BlockSpec((BK, 1), lambda i, f: (i, 0)), whole(2, T), whole(2, T)],
            out_specs=[whole(T, 256), pl.BlockSpec((BK, 128), lambda i, f: (i, 0)), pl.BlockSpec((BK, 128), lambda i, f: (i, 0))],
        ),
        out_shape=[jax.ShapeDtypeStruct((T, 256), f32), jax.ShapeDtypeStruct((N, 128), f32), jax.ShapeDtypeStruct((N, 128), f32)],
        cost_estimate=pl.CostEstimate(flops=5*2*T*N*256*3//4, bytes_accessed=12<<20, transcendentals=T*N*3//2),
        name="attn_backward",
    )(flags, q, g, k, v, qbit, kbit, lse, delta)


GROUP=4
MESH=pl.DeviceIdType.MESH

def places():
    dp = lax.axis_index("dp"); c = lax.axis_index("mp")
    t = dp % GROUP
    base = dp - t
    tx = t + 1 - 2 * (t % 2)
    ty = t + 2 - 4 * (t // 2)
    td = 3 - t
    return base, t, tx, ty, td, c

def greet(devices):
    barrier = pltpu.get_barrier_semaphore()
    for device in devices:
        pl.semaphore_signal(barrier, inc=1, device_id=device, device_id_type=MESH)
    pl.semaphore_wait(barrier, len(devices))

def gather_body(x_ref, out_ref, send, recv, local):
    base, t, tx, ty, td, c = places()
    share = x_ref.shape[0]
    half = share // 2
    xdev, ydev, mate = (base + tx, c), (base + ty, c), (base + t, 1 - c)
    greet([xdev, ydev, mate])
    def spot(who, part=None):
        start = (2 * who + c) * share
        if part is None:
            return out_ref.at[pl.ds(pl.multiple_of(start, share), share)]
        return out_ref.at[pl.ds(pl.multiple_of(start + part * half, half), half)]
    def copy(kind, src, dst, device):
        return pltpu.make_async_remote_copy(src_ref=src, dst_ref=dst, send_sem=send.at[kind], recv_sem=recv.at[kind], device_id=device, device_id_type=MESH)
    own = pltpu.make_async_copy(x_ref, spot(t), local)
    own.start()
    mine = [x_ref.at[pl.ds(0, half)], x_ref.at[pl.ds(half, half)]]
    k = {}
    k[2] = copy(2, mine[0], spot(t, 0), ydev); k[2].start()
    k[1] = copy(1, mine[1], spot(t, 1), xdev); k[1].start()
    k[3] = copy(3, mine[1], spot(t, 1), ydev); k[3].start()
    k[0] = copy(0, mine[0], spot(t, 0), xdev); k[0].start()
    k[6] = copy(6, x_ref, spot(t), mate); k[6].start()
    k[2].wait_recv()
    k[4] = copy(4, spot(ty, 0), spot(ty, 0), xdev); k[4].start()
    k[9] = copy(9, spot(ty, 0), spot(ty, 0), mate); k[9].start()
    k[1].wait_recv()
    k[5] = copy(5, spot(tx, 1), spot(tx, 1), ydev); k[5].start()
    k[8] = copy(8, spot(tx, 1), spot(tx, 1), mate); k[8].start()
    k[0].wait_recv()
    k[7] = copy(7, spot(tx, 0), spot(tx, 0), mate); k[7].start()
    k[3].wait_recv()
    k[10] = copy(10, spot(ty, 1), spot(ty, 1), mate); k[10].start()
    k[4].wait_recv()
    k[11] = copy(11, spot(td, 0), spot(td, 0), mate); k[11].start()
    k[5].wait_recv()
    k[12] = copy(12, spot(td, 1), spot(td, 1), mate); k[12].start()
    for kind in range(6, 13):
        k[kind].wait_recv()
    for kind in range(13):
        k[kind].wait_send()
    own.wait()

def gather_group(x):
    share, width = x.shape
    return pl.pallas_call(
        gather_body,
        out_shape=jax.ShapeDtypeStruct((share * GROUP * 2, width), x.dtype),
        in_specs=[pl.BlockSpec(memory_space=pltpu.VMEM)],
        out_specs=pl.BlockSpec(memory_space=pl.ANY),
        scratch_shapes=[pltpu.SemaphoreType.DMA((13,)), pltpu.SemaphoreType.DMA((13,)), pltpu.SemaphoreType.DMA],
        compiler_params=pltpu.CompilerParams(collective_id=1, has_side_effects=True),
        name="gather_group",
    )(x)

def reduce_body(p_ref, out_ref, near, mates, sums, xin, yin, zin, turn, load, send, recv):
    base, t, tx, ty, td, c = places()
    share = out_ref.shape[0]
    half = share // 2
    xdev, ydev, mate = (base + tx, c), (base + ty, c), (base + t, 1 - c)
    greet([xdev, ydev, mate])
    def spot(who, core):
        return p_ref.at[pl.ds(pl.multiple_of((2 * who + core) * share, share), share)]
    def copy(kind, src, dst, device):
        return pltpu.make_async_remote_copy(src_ref=src, dst_ref=dst, send_sem=send.at[kind], recv_sem=recv.at[kind], device_id=device, device_id_type=MESH)
    def add(dst, left, right):
        step = 16
        def go(i, _):
            rows = pl.ds(pl.multiple_of(i * step, step), step)
            dst[rows, :] = (left[rows, :].astype(f32) + right[rows, :].astype(f32)).astype(dst.dtype)
            return 0
        lax.fori_loop(0, dst.shape[0] // step, go, 0)
    order = [td, tx, ty, t]
    over, loads = [], []
    for i, who in enumerate(order):
        over.append(copy(i, spot(who, 1 - c), mates.at[i], mate)); over[i].start()
        loads.append(pltpu.make_async_copy(spot(who, c), near.at[i], load.at[i])); loads[i].start()
    A, B = pl.ds(0, half), pl.ds(half, half)
    k = {}
    for i in range(4):
        loads[i].wait()
        over[i].wait_recv()
        add(sums.at[i], near.at[i], mates.at[i])
        if i == 0:
            k[4] = copy(4, sums.at[0, A], xin.at[1], xdev); k[4].start()
            k[5] = copy(5, sums.at[0, B], yin.at[1], ydev); k[5].start()
        if i == 1:
            k[6] = copy(6, sums.at[1, A], xin.at[0], xdev); k[6].start()
        if i == 2:
            k[7] = copy(7, sums.at[2, B], yin.at[0], ydev); k[7].start()
    k[4].wait_recv()
    add(turn.at[0], sums.at[2, A], xin.at[1])
    k[8] = copy(8, turn.at[0], zin.at[0], ydev); k[8].start()
    k[5].wait_recv()
    add(turn.at[1], sums.at[1, B], yin.at[1])
    k[9] = copy(9, turn.at[1], zin.at[1], xdev); k[9].start()
    k[6].wait_recv()
    add(out_ref.at[A], sums.at[3, A], xin.at[0])
    k[7].wait_recv()
    add(out_ref.at[B], sums.at[3, B], yin.at[0])
    k[8].wait_recv()
    add(out_ref.at[A], out_ref.at[A], zin.at[0])
    k[9].wait_recv()
    add(out_ref.at[B], out_ref.at[B], zin.at[1])
    for i in range(4):
        over[i].wait_send()
    for kind in range(4, 10):
        k[kind].wait_send()

def reduce_group(p):
    rows, width = p.shape
    share = rows // (2 * GROUP)
    half = share // 2
    return pl.pallas_call(
        reduce_body,
        out_shape=jax.ShapeDtypeStruct((share, width), f32),
        in_specs=[pl.BlockSpec(memory_space=pl.ANY)],
        out_specs=pl.BlockSpec(memory_space=pltpu.VMEM),
        scratch_shapes=[pltpu.VMEM((4, share, width), bf), pltpu.VMEM((4, share, width), bf), pltpu.VMEM((4, share, width), bf),
            pltpu.VMEM((2, half, width), bf), pltpu.VMEM((2, half, width), bf), pltpu.VMEM((2, half, width), bf), pltpu.VMEM((2, half, width), bf),
            pltpu.SemaphoreType.DMA((4,)), pltpu.SemaphoreType.DMA((10,)), pltpu.SemaphoreType.DMA((10,))],
        compiler_params=pltpu.CompilerParams(collective_id=2, has_side_effects=True),
        name="reduce_group",
    )(p)

def trade_body(x_ref, out_ref, send, recv, local):
    base, t, tx, ty, td, c = places()
    partners = [td, tx, ty]
    greet([(base + who, c) for who in partners])
    own = pltpu.make_async_copy(x_ref.at[t], out_ref.at[t], local)
    copies = []
    for i, who in enumerate(partners):
        copies.append(pltpu.make_async_remote_copy(src_ref=x_ref.at[who], dst_ref=out_ref.at[t], send_sem=send.at[i], recv_sem=recv.at[i], device_id=(base + who, c), device_id_type=MESH))
        copies[i].start()
    own.start()
    for one in copies:
        one.wait()
    own.wait()

def trade_group(x, key):
    return pl.pallas_call(
        trade_body,
        out_shape=jax.ShapeDtypeStruct(x.shape, x.dtype),
        in_specs=[pl.BlockSpec(memory_space=pltpu.VMEM)],
        out_specs=pl.BlockSpec(memory_space=pl.ANY),
        scratch_shapes=[pltpu.SemaphoreType.DMA((3,)), pltpu.SemaphoreType.DMA((3,)), pltpu.SemaphoreType.DMA],
        compiler_params=pltpu.CompilerParams(collective_id=key, has_side_effects=True),
        name="trade_group",
    )(x)


def row_norm(values, gain):
    scale = lax.rsqrt(jnp.mean(values * values, axis=-1, keepdims=True) + EPS)
    return values * scale * gain


def rotate(values):
    half = values.shape[-1] // 2
    return jnp.concatenate([-values[..., half:], values[..., :half]], axis=-1)


def rope_tables(positions, width):
    half = width // 2
    freqs = THETA ** (-(jnp.arange(half, dtype=f32) / half))
    angle = positions.astype(f32)[:, None] * freqs[None, :]
    angle = jnp.concatenate([angle, angle], axis=-1)
    return (jnp.cos(angle)[:, None, :], jnp.sin(angle)[:, None, :])


def prepare_heads(raw, gain, cosine_table, sine_table):
    normed = row_norm(raw, gain)
    return normed * cosine_table + rotate(normed) * sine_table


def swiglu(gate, up):
    return jax.nn.silu(gate) * up


def gating(attn, logit):
    return attn * jax.nn.sigmoid(logit)[..., None]


def ancestors(parent_row, count):
    table = jnp.eye(count, dtype=jnp.int32)
    for seg_index in range(1, count):
        joined = jnp.maximum(table[seg_index], table[parent_row[seg_index]])
        table = table.at[seg_index].set(joined)
    return table


def segment_onehot(offsets, starts, count):
    segment = jnp.sum((offsets[:, None] >= starts[None, 1:]).astype(jnp.int32), axis=1)
    return (segment[:, None] == jnp.arange(count, dtype=jnp.int32)[None, :]).astype(jnp.int32)


def inner(left, right):
    return dg(left, right, TN)


def against(left, right):
    return dg(left, right, NT)


def by_member(weight, pieces):
    rows = weight.shape[0]
    return weight.reshape(rows, pieces, -1).transpose(1, 0, 2)


def from_members(pieces):
    return pieces.transpose(1, 0, 2).reshape(pieces.shape[1], -1)


def per_device(
    layer_in,
    out_grad,
    parents,
    lengths,
    attn_gain,
    mlp_gain,
    query_norm_gain,
    key_gain,
    query_weight,
    key_matrix,
    value_matrix,
    headgate_weight,
    output_weight,
    gate_weight,
    up_weight,
    down_weight,
):
    data_count = lax.axis_size("dp")
    model_count = lax.axis_size("mp")
    share, width = layer_in.shape
    rows_here = query_weight.shape[0]
    group_tokens = share * model_count * GROUP
    seg_count = parents.shape[1]
    far = [[member + GROUP * plane for plane in range(data_count // GROUP)] for member in range(GROUP)]
    planes = TREE_TOKENS // group_tokens

    pieces_attn = jnp.concatenate(
        [
            by_member(query_weight, GROUP),
            by_member(key_matrix, GROUP),
            by_member(value_matrix, GROUP),
            jnp.pad(by_member(headgate_weight, GROUP), ((0, 0), (0, 0), (0, HEAD_SIZE - headgate_weight.shape[1] // GROUP))),
        ],
        axis=-1,
    )
    pieces_out = by_member(output_weight.T, GROUP)
    pieces_glu = jnp.concatenate([by_member(gate_weight, GROUP), by_member(up_weight, GROUP)], axis=-1)
    pieces_down = by_member(down_weight.T, GROUP)

    def far_gather(pieces, key):
        mine = trade_group(pieces, key).reshape(GROUP * rows_here, -1)
        return lax.all_gather(mine, "dp", axis=0, tiled=True, axis_index_groups=far)

    full_attn = far_gather(pieces_attn, 3)
    full_out = far_gather(pieces_out, 4)
    full_glu = far_gather(pieces_glu, 5)
    full_down = far_gather(pieces_down, 6)

    def far_scatter(grad, key):
        mine = lax.psum_scatter(grad, "dp", scatter_dimension=0, tiled=True, axis_index_groups=far)
        return trade_group(mine.reshape(GROUP, rows_here, -1), key)

    sizes = [attn_gain.shape[0], mlp_gain.shape[0], query_norm_gain.shape[0], key_gain.shape[0]]
    cuts = [0, sizes[0], sizes[0] + sizes[1], sizes[0] + sizes[1] + sizes[2], sum(sizes)]
    gains = lax.all_gather(
        jnp.concatenate([attn_gain, mlp_gain, query_norm_gain, key_gain]), ("dp", "mp"), axis=0, tiled=False
    ).astype(f32)
    gain_one, gain_two, gain_query, gain_key = [
        gains[:, cuts[i] : cuts[i + 1]].reshape(-1) for i in range(4)
    ]

    group_index = lax.axis_index("dp") // GROUP
    first = group_index * group_tokens
    tree = first // TREE_TOKENS
    begin = first - tree * TREE_TOKENS
    later = begin // group_tokens
    parent_row = lax.dynamic_index_in_dim(parents, tree, 0, keepdims=False)
    length_row = lax.dynamic_index_in_dim(lengths, tree, 0, keepdims=False)
    starts = jnp.cumsum(length_row) - length_row
    table = ancestors(parent_row, seg_count)
    depth = jnp.sum(table * length_row[None, :], axis=1) - length_row
    offsets = begin + jnp.arange(group_tokens, dtype=jnp.int32)
    onehot = segment_onehot(offsets, starts, seg_count)
    positions = jnp.sum(onehot * (depth - starts)[None, :], axis=1) + offsets
    powers = 1 << jnp.arange(seg_count, dtype=jnp.int32)
    query_bits = jnp.sum(onehot * jnp.sum(table * powers[None, :], axis=1)[None, :], axis=1)
    key_count = planes * group_tokens
    key_offsets = begin - (key_count - group_tokens) + jnp.arange(key_count, dtype=jnp.int32)
    key_hot = segment_onehot(key_offsets, starts, seg_count) * (key_offsets >= 0).astype(jnp.int32)[:, None]
    key_bits = jnp.sum(key_hot * powers[None, :], axis=1)
    query_has = jnp.max(onehot.reshape(-1, BQ, seg_count), axis=1)
    key_has = jnp.max(key_hot.reshape(-1, BK, seg_count), axis=1)
    reached = jnp.dot(jnp.dot(query_has, table), key_has.T) > 0
    missed = jnp.dot(jnp.dot(query_has, 1 - table), key_has.T) > 0
    q_first = key_count - group_tokens + BQ * jnp.arange(query_has.shape[0], dtype=jnp.int32)[:, None]
    k_first = BK * jnp.arange(key_has.shape[0], dtype=jnp.int32)[None, :]
    some = reached & (k_first <= q_first + BQ - 1)
    every = ~missed & (k_first + BK - 1 <= q_first)
    flags = jnp.where(some, jnp.where(every, 2, 1), 0).astype(jnp.int32)
    cosine_table, sine_table = rope_tables(positions, HEAD_SIZE)

    rows = layer_in.astype(f32)
    normed_one, norm_one_back = jax.vjp(row_norm, rows, gain_one)
    hidden_first = gather_group(normed_one.astype(bf))
    grad_tokens = gather_group(out_grad)
    raw = jnp.dot(hidden_first, full_attn, preferred_element_type=f32)
    q_width = query_weight.shape[1] // GROUP
    k_width = key_matrix.shape[1] // GROUP
    heads = q_width // HEAD_SIZE
    query_unnormed = raw[:, :q_width].reshape(group_tokens, heads, HEAD_SIZE)
    key_unnormed = raw[:, q_width : q_width + k_width].reshape(group_tokens, 1, HEAD_SIZE)
    value_rows = raw[:, q_width + k_width : q_width + 2 * k_width].astype(bf)
    logit = raw[:, q_width + 2 * k_width : q_width + 2 * k_width + heads]
    prepare = partial(prepare_heads, cosine_table=cosine_table, sine_table=sine_table)
    query_f, query_back = jax.vjp(prepare, query_unnormed, gain_query)
    key_f, key_back = jax.vjp(prepare, key_unnormed, gain_key)
    query_rows = query_f.astype(bf).reshape(group_tokens, q_width)
    key_rows = key_f.astype(bf).reshape(group_tokens, k_width)
    ahead = [(s, s + GROUP) for s in range(data_count) if (s // GROUP) % planes == 0]
    back = [(d, s) for s, d in ahead]
    both = lax.ppermute(jnp.concatenate([key_rows, value_rows], axis=1), "dp", ahead)
    key_all = jnp.concatenate([both[:, :k_width], key_rows], axis=0)
    value_all = jnp.concatenate([both[:, k_width:], value_rows], axis=0)
    attn, lse = attn_forward(
        flags, query_rows, key_all, value_all, query_bits[:, None], key_bits.reshape(-1, 1, BK)
    )
    attn = attn.reshape(group_tokens, heads, HEAD_SIZE)
    mixed_f, gate_back = jax.vjp(gating, attn, logit)
    mixed = mixed_f.astype(bf).reshape(group_tokens, -1)
    middle = rows + reduce_group(against(mixed, full_out).astype(bf))

    normed_two, norm_two_back = jax.vjp(row_norm, middle, gain_two)
    h_two = gather_group(normed_two.astype(bf))
    both_glu = jnp.dot(h_two, full_glu, preferred_element_type=f32)
    units = full_down.shape[1]
    gate, up = both_glu[:, :units], both_glu[:, units:]
    hidden_f, glu_back = jax.vjp(swiglu, gate, up)
    hidden = hidden_f.astype(bf)
    layer_out = (middle + reduce_group(against(hidden, full_down).astype(bf))).astype(bf)

    down_grad = far_scatter(inner(grad_tokens, hidden).astype(bf), 7)
    grad_hidden = jnp.dot(grad_tokens, full_down, preferred_element_type=f32)
    grad_gate_f, grad_up_f = glu_back(grad_hidden)
    grad_glu = jnp.concatenate([grad_gate_f.astype(bf), grad_up_f.astype(bf)], axis=1)
    glu_grad = far_scatter(inner(h_two, grad_glu).astype(bf), 8)
    grad_h_two = reduce_group(against(grad_glu, full_glu).astype(bf))
    grad_mid_norm, gain_two_grad = norm_two_back(grad_h_two)
    grad_middle = out_grad.astype(f32) + grad_mid_norm

    grad_branch = gather_group(grad_middle.astype(bf))
    output_grad = far_scatter(inner(grad_branch, mixed).astype(bf), 9)
    grad_mixed = jnp.dot(grad_branch, full_out, preferred_element_type=f32).reshape(
        group_tokens, heads, HEAD_SIZE
    )
    grad_attn_f, grad_logit_f = gate_back(grad_mixed)
    grad_attn = grad_attn_f.astype(bf)
    delta = jnp.sum(grad_attn.astype(f32) * attn, axis=-1)
    grad_query, grad_key, grad_value = attn_backward(
        flags,
        query_rows,
        grad_attn.reshape(group_tokens, q_width),
        key_all,
        value_all,
        query_bits[None, :],
        key_bits[:, None],
        lse.T,
        delta.T,
    )
    early = key_count - group_tokens
    returned = lax.ppermute(
        jnp.concatenate([grad_key[:early], grad_value[:early]], axis=1).astype(bf), "dp", back
    ).astype(f32)
    score_scale = HEAD_SIZE ** (-0.5)
    grad_key = (grad_key[early:] + returned[:, :k_width]) * score_scale
    grad_value = grad_value[early:] + returned[:, k_width:]
    grad_q_raw, query_gain_grad = query_back((grad_query * score_scale).reshape(group_tokens, heads, HEAD_SIZE))
    grad_k_raw, key_gain_grad = key_back(grad_key.reshape(group_tokens, 1, HEAD_SIZE))
    grad_raw = jnp.concatenate(
        [
            grad_q_raw.reshape(group_tokens, -1),
            grad_k_raw.reshape(group_tokens, -1),
            grad_value,
            jnp.pad(grad_logit_f, ((0, 0), (0, HEAD_SIZE - heads))),
        ],
        axis=1,
    ).astype(bf)
    attn_grad = far_scatter(inner(hidden_first, grad_raw).astype(bf), 10)
    grad_h_one = reduce_group(against(grad_raw, full_attn).astype(bf))
    grad_in_norm, gain_one_grad = norm_one_back(grad_h_one)
    input_grad = (grad_middle + grad_in_norm).astype(bf)

    gain_parts = jnp.concatenate(
        [
            piece.reshape(data_count * model_count, -1)
            for piece in (gain_one_grad, gain_two_grad, query_gain_grad, key_gain_grad)
        ],
        axis=1,
    )
    gain_sums = lax.psum_scatter(gain_parts, ("dp", "mp"), scatter_dimension=0, tiled=True)[0]
    full = lambda pieces: from_members(pieces).astype(f32)
    return (
        layer_out,
        input_grad,
        gain_sums[cuts[0] : cuts[1]],
        gain_sums[cuts[1] : cuts[2]],
        gain_sums[cuts[2] : cuts[3]],
        gain_sums[cuts[3] : cuts[4]],
        full(attn_grad[:, :, :q_width]),
        full(attn_grad[:, :, q_width : q_width + k_width]),
        full(attn_grad[:, :, q_width + k_width : q_width + 2 * k_width]),
        full(attn_grad[:, :, q_width + 2 * k_width : q_width + 2 * k_width + heads]),
        full(output_grad).T,
        full(glu_grad[:, :, :units]),
        full(glu_grad[:, :, units:]),
        full(down_grad).T,
    )


def solution(mesh):
    in_specs = (
        P(("dp", "mp"), None),
        P(("dp", "mp"), None),
        P(),
        P(),
        P(("dp", "mp")),
        P(("dp", "mp")),
        P(("dp", "mp")),
        P(("dp", "mp")),
        P("dp", "mp"),
        P("dp", "mp"),
        P("dp", "mp"),
        P("dp", "mp"),
        P("mp", "dp"),
        P("dp", "mp"),
        P("dp", "mp"),
        P("mp", "dp"),
    )
    out_specs = (
        P(("dp", "mp"), None),
        P(("dp", "mp"), None),
        P(("dp", "mp")),
        P(("dp", "mp")),
        P(("dp", "mp")),
        P(("dp", "mp")),
        P("dp", "mp"),
        P("dp", "mp"),
        P("dp", "mp"),
        P("dp", "mp"),
        P("mp", "dp"),
        P("dp", "mp"),
        P("dp", "mp"),
        P("mp", "dp"),
    )
    return jax.shard_map(
        per_device, mesh=mesh, in_specs=in_specs, out_specs=out_specs, check_vma=False
    )
```

time: 3450 us -> 1090 us (0.32)
  waiting for transfers between devices: 2640 us -> 69.7 us
  Pallas kernels: 0 us -> 476 us
  starting transfers between devices: 114 us -> 6.74 us
  blocking collectives: 172 us -> 100 us
  matrix products: 216 us -> 150 us
    reduce_scatter x12 -> x4, waiting for transfers between devices: 1720 us -> 0.01 us  [far_scatter(): lax.psum_scatter(grad, 'dp', scatter_dimension=0, tiled=True, axis_index_...]
    all_gather x11 -> x4, waiting for transfers between devices: 637 us -> 0.03 us  [far_gather(): return lax.all_gather(mine, 'dp', axis=0, tiled=True, axis_index_groups=far)]
    pallas_call x0 -> x18, Pallas kernels: none -> 476 us  [the longest x4 165 us: reduce_group(): pl.pallas_call(reduce_body, out_shape=jax.ShapeDtypeStruct((share, width)...]
    ppermute x28 -> x2, waiting for transfers between devices: 282 us -> 69.6 us  [the longest x1 57.7 us: per_device(): lax.ppermute(jnp.concatenate([grad_key[:early], grad_value[:early]], axis...]
    ppermute x28 -> x2, starting transfers between devices: 113 us -> 6.41 us  [the longest x1 5.13 us: per_device(): lax.ppermute(jnp.concatenate([key_rows, value_rows], axis=1), 'dp', ahead)]
    dot_general x38 -> x14, matrix products: 216 us -> 150 us  [the longest x8 95.6 us: dg(): return lax.dot_general(a, b, d, preferred_element_type=f32)]
    add x24 -> x3, other arithmetic: 54.7 us -> 0.01 us  [the longest x1 0.01 us: per_device(): begin - (key_count - group_tokens) + jnp.arange(key_count, dtype=jnp.int32)]
    all_gather x1 -> x0, blocking collectives: 40 us -> none  [fetch_attention(): lax.all_gather(headgate_weight, 'dp', axis=0, tiled=True)]
  transfers between devices with their start and end apart: 51 -> 10, of which waited for: 44 -> 2; matrix products, arithmetic and copies ran while one was open for 8% -> 21% of each run, Pallas kernels for 0% -> 31%
where the time goes in v1:
time: 1090 us; the launch traced here: 1080 us
  Pallas kernels  476 us (44%)
  other arithmetic  167 us (15%)
  matrix products  150 us (14%)
  blocking collectives  100 us (9%)
  local copies, waits for them, and re-layouts  83.7 us (8%)
  waiting for transfers between devices  69.7 us (6%)
  between operations  27.8 us (3%)
    pallas_call x4, Pallas kernels, reduce_group(): pl.pallas_call(reduce_body, out_shape=jax.ShapeDtypeStruct((share, width)...  165 us
    pallas_call x4, Pallas kernels, gather_group(): pl.pallas_call(gather_body, out_shape=jax.ShapeDtypeStruct((share * GROUP...  164 us
    pallas_call x8, Pallas kernels, trade_group(): pl.pallas_call(trade_body, out_shape=jax.ShapeDtypeStruct(x.shape, x.dtyp...  105 us
    unnamed x2, blocking collectives  100 us
    dot_general x8, matrix products, dg(): return lax.dot_general(a, b, d, preferred_element_type=f32)  95.6 us
    ppermute x1, waiting for transfers between devices, per_device(): lax.ppermute(jnp.concatenate([grad_key[:early], grad_value[:early]], axis...  57.7 us
    reduce_sum x4, other arithmetic, row_norm(): return values * scale * gain  42.5 us
    reduce_sum x1, other arithmetic, per_device(): delta = jnp.sum(grad_attn.astype(f32) * attn, axis=-1)  34.1 us
  transfers between devices with their start and end apart: 10, of which 2 were waited for; matrix products, arithmetic and copies ran while one was open for 21% of the time, Pallas kernels for 31%

profile of v1, /device:TPU:0, one launch (start us, length us, event | category | flops | bytes accessed | tf_op | source)
XLA Modules:
  0.0 1081.1 jit_solution(5502516139301300614)
XLA Ops:
  12.0 13.2 %trade_group.8 = bf16[4,128,640]{2,1,0:T(8,128)(2,1)} custom-call(bf16[4,128,640]{2,1,0:T(8,128)(2,1)} %fusion.59.x_ref), custom_call_target="tpu_custom_call" | custom-call | tf_op jit(solution)/shard_map/trade_group/pallas_call | solution.py:300
  36.3 21.0 %trade_group.10 = bf16[4,128,1536]{2,1,0:T(8,128)(2,1)} custom-call(bf16[4,128,1536]{2,1,0:T(8,128)(2,1)} %pad_maximum_fusion.3.x_ref), custom_call_target="tpu_custom_call" | custom-call | tf_op jit(solution)/shard_map/trade_group/pallas_call | solution.py:300
  58.7 13.2 %trade_group.11 = bf16[4,128,768]{2,1,0:T(8,128)(2,1)} custom-call(bf16[4,128,768]{2,1,0:T(8,128)(2,1)} %bitcast.193), custom_call_target="tpu_custom_call" | custom-call | tf_op jit(solution)/shard_map/trade_group/pallas_call | solution.py:300
  80.8 41.0 %all-reduce.6 = bf16[4352]{0:T(1024)(128)(2,1)S(1)} all-reduce(bf16[4352]{0:T(1024)(128)(2,1)S(1)} %dynamic-update-slice.18), channel_id=2, replica_groups=mesh['dp'=16,'mp'=2] {'dp','mp'}, use_global_device_ids=true, to_apply=%add.6 | all-reduce | flops 4352 | bytes 17408
  128.9 41.5 %gather_group.4 = bf16[2048,2048]{1,0:T(8,128)(2,1)} custom-call(bf16[256,2048]{1,0:T(8,128)(2,1)} %fusion.9.x_ref), custom_call_target="tpu_custom_call" | custom-call | tf_op jit(solution)/shard_map/gather_group/pallas_call | solution.py:205
  172.6 40.9 %gather_group.6 = bf16[2048,2048]{1,0:T(8,128)(2,1)} custom-call(bf16[256,2048]{1,0:T(8,128)(2,1)} %x_ref.1), custom_call_target="tpu_custom_call" | custom-call | tf_op jit(solution)/shard_map/gather_group/pallas_call | solution.py:205
  298.2 16.0 %attn_forward.1 = (f32[2048,256]{1,0:T(8,128)}, f32[2048,2]{1,0:T(8,128)}) custom-call(s32[8,8]{1,0:T(8,128)} %fusion.37.flags, bf16[2048,256]{1,0:T(8,128)(2,1)} %fusion.19.q_ref, bf16[4096,128]{1,0:T(8,128)(2,1)} %pad_maximum_fusion.6.k_ref, bf16[4096,128]{1,0:T(8,128)(2,1)} %pad_maximum_fusion.7.v_ref, s32[2048,1]{1,0:T(8,128)} %copy.212.qbit_ref, ...), custom_call_target="tpu_custom_call" | custom-call | flops 6442450944 | bytes 8388608 | tf_op jit(solution)/shard_map/attn_forward/pallas_call | solution.py:64
  331.6 40.7 %reduce_group.4 = f32[256,2048]{1,0:T(8,128)} custom-call(bf16[2048,2048]{1,0:T(8,128)(2,1)} %convolution_convert_fusion.3.p_ref), custom_call_target="tpu_custom_call" | custom-call | tf_op jit(solution)/shard_map/reduce_group/pallas_call | solution.py:273
  375.6 40.9 %gather_group.5 = bf16[2048,2048]{1,0:T(8,128)(2,1)} custom-call(bf16[256,2048]{1,0:T(8,128)(2,1)} %multiply_convert_fusion.3.x_ref), custom_call_target="tpu_custom_call" | custom-call | tf_op jit(solution)/shard_map/gather_group/pallas_call | solution.py:205
  417.4 19.0 %fusion.100 = f32[2048,1536]{0,1:T(8,128)} fusion(bf16[2048,2048]{1,0:T(8,128)(2,1)} %gather_group.5, bf16[2048,1536]{1,0:T(8,128)(2,1)} %all-gather.10.cloned.1.call-done), kind=kOutput, calls=%fused_computation.208 | convolution fusion | flops 12884901888 | bytes 27262976 | tf_op jit(solution)/shard_map/dot_general | solution.py:496
  436.4 18.0 %fusion.2 = (bf16[2048,768]{0,1:T(8,128)(2,1)}, bf16[2048,768]{0,1:T(8,128)(2,1)}, bf16[2048,768]{0,1:T(8,128)(2,1)}) fusion(f32[2048,1536]{0,1:T(8,128)} %fusion.100, bf16[2048,2048]{1,0:T(8,128)(2,1)} %gather_group.6, bf16[2048,768]{1,0:T(8,128)(2,1)} %all-gather.12.cloned.1.call-done), kind=kOutput, calls=%fused_computation.8 | convolution fusion | flops 6467616768 | bytes 33554432 | tf_op jit(solution)/shard_map/dot_general | solution.py:504
  454.4 19.2 %convolution_convert_fusion.1.p_ref = bf16[2048,2048]{1,0:T(8,128)(2,1)} fusion(bf16[2048,1536]{1,0:T(8,128)(2,1)} %all-gather.10.cloned.1.call-done, bf16[2048,768]{0,1:T(8,128)(2,1)} %get-tuple-element.185, bf16[2048,768]{0,1:T(8,128)(2,1)} %get-tuple-element.184), kind=kOutput, calls=%fused_computation.2 | convolution fusion | flops 12901679104 | bytes 20971520 | tf_op jit(solution)/shard_map/dot_general | solution.py:23
  473.6 41.5 %reduce_group.6 = f32[256,2048]{1,0:T(8,128)} custom-call(bf16[2048,2048]{1,0:T(8,128)(2,1)} %convolution_convert_fusion.1.p_ref), custom_call_target="tpu_custom_call" | custom-call | tf_op jit(solution)/shard_map/reduce_group/pallas_call | solution.py:273
  519.4 40.4 %gather_group.7 = bf16[2048,2048]{1,0:T(8,128)(2,1)} custom-call(bf16[256,2048]{1,0:T(8,128)(2,1)} %fusion.92.x_ref), custom_call_target="tpu_custom_call" | custom-call | tf_op jit(solution)/shard_map/gather_group/pallas_call | solution.py:205
  577.6 34.1 %multiply_reduce_fusion.4 = (f32[2048,2]{1,0:T(8,128)}, f32[2048,2]{1,0:T(8,128)}) fusion(f32[2048,2,128]{2,1,0:T(2,128)} %reshape.575, f32[2048,2,128]{2,1,0:T(2,128)} %copy.222, f32[2048,2]{1,0:T(8,128)S(1)} %copy-done.15), kind=kLoop, calls=%fused_computation.56 | loop fusion | flops 3661824 | bytes 4243456 | tf_op jit(solution)/shard_map/reduce_sum | solution.py:519
  613.9 26.5 %attn_backward.1 = (f32[2048,256]{1,0:T(8,128)}, f32[4096,128]{1,0:T(8,128)}, f32[4096,128]{1,0:T(8,128)}) custom-call(s32[8,8]{1,0:T(8,128)} %fusion.37.flags, bf16[2048,256]{1,0:T(8,128)(2,1)} %fusion.19.q_ref, bf16[2048,256]{1,0:T(8,128)(2,1)} %fusion.18.g_ref, bf16[4096,128]{1,0:T(8,128)(2,1)} %pad_maximum_fusion.6.k_ref, ...), custom_call_target="tpu_custom_call" | custom-call | flops 16106127360 | bytes 12582912 | tf_op jit(solution)/shard_map/attn_backward/pallas_call | solution.py:129
  652.4 33.3 %multiply_reduce_fusion = (f32[128]{0:T(128)S(1)}, f32[2048,2]{1,0:T(8,128)}, f32[2048,2,128]{2,1,0:T(2,128)}) fusion(f32[2048,2,128]{2,1,0:T(2,128)S(1)} %copy-done.1, f32[2048,2]{1,0:T(8,128)S(1)} %copy-done.8, f32[128]{0:T(128)S(1)} %copy-done.58, f32[2048,2,128]{2,1,0:T(2,128)S(1)} %copy-done.11, f32[2048,128]{1,0:T(8,128)S(1)} %copy-done.20, ...), kind=kLoop, calls=%fused_computation.51 | loop fusion | flops 4714368 | bytes 9470976 | tf_op jit(solution)/shard_map/transpose(jvp())/reduce_sum | solution.py:313
  717.0 57.7 %collective-permute-done.1 = bf16[2048,256]{1,0:T(8,128)(2,1)} collective-permute-done((bf16[2048,256]{1,0:T(8,128)(2,1)}, bf16[2048,256]{1,0:T(8,128)(2,1)}, u32[]{:S(2)}, u32[]{:S(2)}) %collective-permute-start.1) | collective-permute-done | bytes 1048608 | tf_op jit(solution)/shard_map/ppermute | solution.py:532
  797.3 11.9 %fusion.5 = bf16[2048,768]{0,1:T(8,128)(2,1)} fusion(bf16[2048,768]{0,1:T(8,128)(2,1)} %get-tuple-element.186, bf16[2048,2048]{1,0:T(8,128)(2,1)} %gather_group.6), kind=kOutput, calls=%fused_computation.26 | convolution fusion | flops 6444023808 | bytes 14680064 | tf_op jit(solution)/shard_map/dot_general | solution.py:23
  809.3 19.4 %convolution_convert_fusion.4 = bf16[2048,1536]{1,0:T(8,128)(2,1)} fusion(bf16[2048,2048]{1,0:T(8,128)(2,1)} %gather_group.5, bf16[2048,768]{0,1:T(8,128)(2,1)} %get-tuple-element.185, bf16[2048,768]{0,1:T(8,128)(2,1)} %get-tuple-element.184), kind=kOutput, calls=%fused_computation.5 | convolution fusion | flops 12900630528 | bytes 20971520 | tf_op jit(solution)/shard_map/dot_general | solution.py:23
  840.4 40.9 %reduce_group.5 = f32[256,2048]{1,0:T(8,128)} custom-call(bf16[2048,2048]{1,0:T(8,128)(2,1)} %convolution_convert_fusion.2.p_ref), custom_call_target="tpu_custom_call" | custom-call | tf_op jit(solution)/shard_map/reduce_group/pallas_call | solution.py:273
  892.5 41.7 %reduce_group.7 = f32[256,2048]{1,0:T(8,128)} custom-call(bf16[2048,2048]{1,0:T(8,128)(2,1)} %convolution_convert_fusion.p_ref), custom_call_target="tpu_custom_call" | custom-call | tf_op jit(solution)/shard_map/reduce_group/pallas_call | solution.py:273
  936.8 59.5 %all-reduce.7 = f32[32,136]{1,0:T(8,128)S(1)} all-reduce(f32[32,136]{1,0:T(8,128)S(1)} %pad_maximum_fusion.9), channel_id=3, replica_groups=mesh['dp'=16,'mp'=2] {'dp','mp'}, use_global_device_ids=true, to_apply=%region_24.25.clone | all-reduce | flops 4352 | bytes 34816
  1043.5 21.9 %trade_group.14 = bf16[4,128,1536]{2,1,0:T(8,128)(2,1)} custom-call(bf16[4,128,1536]{2,1,0:T(8,128)(2,1)} %bitcast.198), custom_call_target="tpu_custom_call" | custom-call | tf_op jit(solution)/shard_map/trade_group/pallas_call | solution.py:300
  (340 shorter events, 299.7 us)
Async XLA Ops:
  7.2 210.2 %all-gather.6.cloned.1.call-start = ((), (), s32[]{:S(2)}) async-start(), calls=%async_computation.4 | async-start | bytes 3276800 | tf_op jit(solution)/shard_map/all_gather | solution.py:414
  25.2 299.2 %all-gather.8.cloned.1.call-start = ((), (), s32[]{:S(2)}) async-start(), calls=%async_computation.5 | async-start | bytes 1310720 | tf_op jit(solution)/shard_map/all_gather | solution.py:414
  33.6 383.8 %all-gather.10.cloned.1.call-start = ((), (), s32[]{:S(2)}) async-start(), calls=%async_computation.6 | async-start | bytes 7864320 | tf_op jit(solution)/shard_map/all_gather | solution.py:414
  57.4 379.0 %all-gather.12.cloned.1.call-start = ((), (), s32[]{:S(2)}) async-start(), calls=%async_computation.7 | async-start | bytes 3932160 | tf_op jit(solution)/shard_map/all_gather | solution.py:414
  57.5 69.8 %copy-start.5 = (bf16[256,2048]{1,0:T(8,128)(2,1)S(1)}, bf16[256,2048]{1,0:T(8,128)(2,1)}, u32[]{:S(2)}) copy-start(bf16[256,2048]{1,0:T(8,128)(2,1)} %param.28) | copy-start | bytes 3145732
  71.9 931.1 %reduce-scatter.7.cloned.1.call-start = ((), (), s32[]{:S(2)}) async-start(), calls=%async_computation.9 | async-start | bytes 1310720 | tf_op jit(solution)/shard_map/reduce_scatter | solution.py:422
  127.2 43.5 %copy-start.50 = (s32[2048]{0:T(1024)}, s32[2048]{0:T(1024)S(1)}, u32[]{:S(2)}) copy-start(s32[2048]{0:T(1024)S(1)} %get-tuple-element.176) | copy-start | bytes 24580
  127.3 43.1 %copy-start.45 = (f32[2048]{0:T(1024)}, f32[2048]{0:T(1024)S(1)}, u32[]{:S(2)}) copy-start(f32[2048]{0:T(1024)S(1)} %mul.497) | copy-start | bytes 24580
  127.6 42.9 %copy-start.55 = (f32[256]{0:T(256)}, f32[256]{0:T(256)S(1)}, u32[]{:S(2)}) copy-start(f32[256]{0:T(256)S(1)} %fusion.15) | copy-start | bytes 3076
  127.6 42.9 %copy-start.51 = (f32[256]{0:T(256)}, f32[256]{0:T(256)S(1)}, u32[]{:S(2)}) copy-start(f32[256]{0:T(256)S(1)} %fusion.74) | copy-start | bytes 3076
  170.6 65.1 %copy-start.53 = (f32[128]{0:T(128)}, f32[128]{0:T(128)S(1)}, u32[]{:S(2)}) copy-start(f32[128]{0:T(128)S(1)} %mul.529) | copy-start | bytes 1540
  170.7 90.9 %copy-start.57 = (f32[128]{0:T(128)}, f32[128]{0:T(128)S(1)}, u32[]{:S(2)}) copy-start(f32[128]{0:T(128)S(1)} %mul.504) | copy-start | bytes 1540
  244.9 49.9 %collective-permute-start = (bf16[2048,256]{1,0:T(8,128)(2,1)}, bf16[2048,256]{1,0:T(8,128)(2,1)}, u32[]{:S(2)}, u32[]{:S(2)}) collective-permute-start(bf16[2048,256]{1,0:T(8,128)(2,1)} %pad_maximum_fusion.5), channel_id=1, source_target_pairs={{0,8},{2,10},{4,12},{6,14},{16,24},{18,26},{20,28},{22,30},{1,9},{... | collective-permute-start | bytes 3145736 | tf_op jit(solution)/shard_map/ppermute | solution.py:483
  271.0 43.2 %copy-start.14 = (f32[2048,2]{1,0:T(8,128)}, f32[2048,2]{1,0:T(8,128)S(1)}, u32[]{:S(2)}) copy-start(f32[2048,2]{1,0:T(8,128)S(1)} %copy.213) | copy-start | bytes 49156
  705.2 69.5 %collective-permute-start.1 = (bf16[2048,256]{1,0:T(8,128)(2,1)}, bf16[2048,256]{1,0:T(8,128)(2,1)}, u32[]{:S(2)}, u32[]{:S(2)}) collective-permute-start(bf16[2048,256]{1,0:T(8,128)(2,1)} %pad_maximum_fusion.8), channel_id=1, source_target_pairs={{8,0},{10,2},{12,4},{14,6},{24,16},{26,18},{28,20},{30,22},{9,1},{... | collective-permute-start | bytes 3145736 | tf_op jit(solution)/shard_map/ppermute | solution.py:532
  716.9 59.3 %copy-start.13 = (f32[2048,64]{1,0:T(8,128)S(1)}, f32[2048,64]{1,0:T(8,128)}, u32[]{:S(2)}) copy-start(f32[2048,64]{1,0:T(8,128)} %copy-done.12) | copy-start | bytes 1572868
  716.9 296.0 %reduce-scatter.5.cloned.1.call-start = ((), (), s32[]{:S(2)}) async-start(), calls=%async_computation.8 | async-start | bytes 3276800 | tf_op jit(solution)/shard_map/reduce_scatter | solution.py:422
  717.0 59.3 %copy-start.29 = (f32[4096,128]{1,0:T(8,128)S(1)}, f32[4096,128]{1,0:T(8,128)}, u32[]{:S(2)}) copy-start(f32[4096,128]{1,0:T(8,128)} %get-tuple-element.94) | copy-start | bytes 6291460
  797.2 229.8 %reduce-scatter.11.cloned.1.call-start = ((), (), s32[]{:S(2)}) async-start(), calls=%async_computation.11 | async-start | bytes 3932160 | tf_op jit(solution)/shard_map/reduce_scatter | solution.py:422
  809.2 234.3 %reduce-scatter.9.cloned.1.call-start = ((), (), s32[]{:S(2)}) async-start(), calls=%async_computation.10 | async-start | bytes 7864320 | tf_op jit(solution)/shard_map/reduce_scatter | solution.py:422
  892.5 41.7 %copy-start.6 = (bf16[256,2048]{1,0:T(8,128)(2,1)S(1)}, bf16[256,2048]{1,0:T(8,128)(2,1)}, u32[]{:S(2)}) copy-start(bf16[256,2048]{1,0:T(8,128)(2,1)} %param.28) | copy-start | bytes 3145732
  892.5 41.7 %copy-start.46 = (f32[2048]{0:T(1024)S(1)}, f32[2048]{0:T(1024)}, u32[]{:S(2)}) copy-start(f32[2048]{0:T(1024)} %copy-done.45) | copy-start | bytes 24580
  892.5 41.7 %copy-start.52 = (f32[256]{0:T(256)S(1)}, f32[256]{0:T(256)}, u32[]{:S(2)}) copy-start(f32[256]{0:T(256)} %copy-done.51) | copy-start | bytes 3076
  934.2 63.3 %copy-start.56 = (f32[256]{0:T(256)S(1)}, f32[256]{0:T(256)}, u32[]{:S(2)}) copy-start(f32[256]{0:T(256)} %copy-done.55) | copy-start | bytes 3076
  (55 other events, 548.2 us)
Sparse Core Ops, SparseCore 0:
  25.3 54.9 all-gather.5
  82.0 27.4 all-gather.7
  111.1 114.9 all-gather.9
  227.4 80.0 all-gather.11
  717.0 85.2 reduce-scatter.6
  804.5 58.0 reduce-scatter.4
  864.9 59.9 reduce-scatter.10
  927.2 111.7 reduce-scatter.8

commit v2 on v1

--- a/solution.py
+++ b/solution.py
@@ -14,130 +14,309 @@
 f32 = jnp.float32
 bf = jnp.bfloat16
 
-LOG2E=1.4426950408889634
-BQ=256
-BK=512
-NT=(((1,),(1,)),((),()))
-NN=(((1,),(0,)),((),()))
-TN=(((0,),(0,)),((),()))
-def dg(a,b,d): return lax.dot_general(a,b,d,preferred_element_type=f32)
-
-def attn_forward_body(base, flags, q_ref, k_ref, v_ref, qbit_ref, kbit_ref, o_ref, l_ref, acc, tot):
+LOG2E = 1.4426950408889634
+SCORE_SCALE = HEAD_SIZE ** (-0.5)
+BQ = 256
+BK = 512
+NT = (((1,), (1,)), ((), ()))
+NN = (((1,), (0,)), ((), ()))
+TN = (((0,), (0,)), ((), ()))
+
+
+def dg(left, right, dims):
+    return lax.dot_general(left, right, dims, preferred_element_type=f32)
+
+
+def halves(ref, rows):
+    return jnp.concatenate([ref[rows, :HEAD_SIZE], ref[rows, HEAD_SIZE:]], axis=0)
+
+
+def as_rows(column):
+    return jnp.broadcast_to(column, (column.shape[0], HEAD_SIZE)).T[0:1, :]
+
+
+def attend_body(causal, last, flags, q_ref, kv_ref, qbit_ref, kbit_ref, *refs):
+    if last:
+        acc_in, tot_in, logit_ref, attn_ref, mixed_ref, lse_ref, acc, tot = refs
+    else:
+        acc_out, tot_out, acc, tot = refs
     qb = pl.program_id(0)
     bq = q_ref.shape[0]
     nk, _, bk = kbit_ref.shape
-    q = jnp.concatenate([q_ref[:, :HEAD_SIZE], q_ref[:, HEAD_SIZE:]], axis=0)
+    q = halves(q_ref, slice(None))
     acc[...] = jnp.zeros_like(acc)
     tot[...] = jnp.zeros_like(tot)
-    factor = LOG2E * HEAD_SIZE ** (-0.5)
+
     def step(kb, masked):
         rows = pl.ds(pl.multiple_of(kb * bk, bk), bk)
-        s = dg(q, k_ref[rows, :], NT) * factor
+        s = dg(q, kv_ref[rows, :HEAD_SIZE], NT) * (LOG2E * SCORE_SCALE)
         if masked:
             seen = (qbit_ref[...] & kbit_ref[kb]) != 0
-            at = lax.broadcasted_iota(jnp.int32, (bq, bk), 1) + kb * bk
-            row = lax.broadcasted_iota(jnp.int32, (bq, bk), 0) + base + qb * bq
-            seen = seen & (at <= row)
+            if causal:
+                at = lax.broadcasted_iota(jnp.int32, (bq, bk), 1) + kb * bk
+                row = lax.broadcasted_iota(jnp.int32, (bq, bk), 0) + qb * bq
+                seen = seen & (at <= row)
             s = jnp.where(jnp.concatenate([seen, seen], axis=0), s, -1e30)
         p = jnp.exp2(s)
         part = p[:, 0:128]
         for i in range(1, bk // 128):
-            part = part + p[:, i * 128:(i + 1) * 128]
+            part = part + p[:, i * 128 : (i + 1) * 128]
         tot[...] += part
-        acc[...] += dg(p.astype(bf), v_ref[rows, :], NN)
+        acc[...] += dg(p.astype(bf), kv_ref[rows, HEAD_SIZE:], NN)
+
     def body(kb, _):
         flag = flags[qb, kb]
         pl.when(flag == 1)(lambda: step(kb, True))
         pl.when(flag == 2)(lambda: step(kb, False))
         return 0
+
     lax.fori_loop(0, nk, body, 0)
     total = jnp.sum(tot[...], axis=1, keepdims=True)
-    out = acc[...] / total
-    o_ref[:, :HEAD_SIZE] = out[:bq]
-    o_ref[:, HEAD_SIZE:] = out[bq:]
-    lse = jnp.log2(total)
-    l_ref[...] = jnp.concatenate([lse[:bq], lse[bq:]], axis=1)
-
-def attn_forward(flags, q, k, v, qbit, kbit):
-    T = q.shape[0]; N = k.shape[0]
+    if not last:
+        acc_out[:, :HEAD_SIZE] = acc[:bq, :]
+        acc_out[:, HEAD_SIZE:] = acc[bq:, :]
+        tot_out[...] = jnp.concatenate([total[:bq], total[bq:]], axis=1)
+    else:
+        for h in range(2):
+            rows = slice(h * bq, (h + 1) * bq)
+            cols = slice(h * HEAD_SIZE, (h + 1) * HEAD_SIZE)
+            sums = total[rows] + tot_in[:, h : h + 1]
+            out = (acc[rows, :] + acc_in[:, cols]) / sums
+            attn_ref[:, cols] = out
+            mixed_ref[:, cols] = (out * jax.nn.sigmoid(logit_ref[:, h : h + 1])).astype(bf)
+            lse_ref[h : h + 1, :] = as_rows(jnp.log2(sums))
+
+
+def attend(causal, flags, q, kv, qbit, kbit, earlier=None):
+    T = q.shape[0]
+    N = kv.shape[0]
     nk = N // BK
-    return pl.pallas_call(
-        partial(attn_forward_body, N - T),
+    W = 2 * HEAD_SIZE
+    blk = lambda w, j=0: pl.BlockSpec((BQ, w), lambda i, f: (i, j))
+    last = earlier is not None
+    in_specs = [
+        blk(W),
+        pl.BlockSpec((N, W), lambda i, f: (0, 0)),
+        blk(1),
+        pl.BlockSpec((nk, 1, BK), lambda i, f: (0, 0, 0)),
+    ]
+    if last:
+        acc, tot, raw = earlier
+        extra = [acc, tot, raw]
+        in_specs += [blk(W), blk(2), blk(HEAD_SIZE, raw.shape[1] // HEAD_SIZE - 1)]
+        out_specs = [blk(W), blk(W), pl.BlockSpec((2, BQ), lambda i, f: (0, i))]
+        out_shape = [
+            jax.ShapeDtypeStruct((T, W), f32),
+            jax.ShapeDtypeStruct((T, W), bf),
+            jax.ShapeDtypeStruct((2, T), f32),
+        ]
+    else:
+        extra = []
+        out_specs = [blk(W), blk(2)]
+        out_shape = [jax.ShapeDtypeStruct((T, W), f32), jax.ShapeDtypeStruct((T, 2), f32)]
+    return pl.pallas_call(
+        partial(attend_body, causal, last),
         grid_spec=pltpu.PrefetchScalarGridSpec(
-            num_scalar_prefetch=1, grid=(T // BQ,),
-            in_specs=[
-                pl.BlockSpec((BQ, 256), lambda i, f: (i, 0)),
-                pl.BlockSpec((N, 128), lambda i, f: (0, 0)),
-                pl.BlockSpec((N, 128), lambda i, f: (0, 0)),
-                pl.BlockSpec((BQ, 1), lambda i, f: (i, 0)),
-                pl.BlockSpec((nk, 1, BK), lambda i, f: (0, 0, 0)),
-            ],
-            out_specs=[pl.BlockSpec((BQ, 256), lambda i, f: (i, 0)), pl.BlockSpec((BQ, 2), lambda i, f: (i, 0))],
-            scratch_shapes=[pltpu.VMEM((2 * BQ, 128), f32), pltpu.VMEM((2 * BQ, 128), f32)],
+            num_scalar_prefetch=1,
+            grid=(T // BQ,),
+            in_specs=in_specs,
+            out_specs=out_specs,
+            scratch_shapes=[pltpu.VMEM((2 * BQ, HEAD_SIZE), f32), pltpu.VMEM((2 * BQ, HEAD_SIZE), f32)],
         ),
-        out_shape=[jax.ShapeDtypeStruct((T, 256), f32), jax.ShapeDtypeStruct((T, 2), f32)],
-        cost_estimate=pl.CostEstimate(flops=2*2*T*N*256*3//4, bytes_accessed=8<<20, transcendentals=T*N*3//2),
-        name="attn_forward",
-    )(flags, q, k, v, qbit, kbit)
-
-def attn_backward_body(base, flags, q_ref, g_ref, k_ref, v_ref, qbit_ref, kbit_ref, lse_ref, del_ref, dq_ref, dk_ref, dv_ref):
+        out_shape=out_shape,
+        cost_estimate=pl.CostEstimate(
+            flops=(2 if causal else 4) * T * N * W, bytes_accessed=8 << 20, transcendentals=T * N * (1 if causal else 2)
+        ),
+        name="attend_own" if causal else "attend_earlier",
+    )(flags, q, kv, qbit, kbit, *extra)
+
+
+def attend_back_body(causal, flags, q_ref, g_ref, kv_ref, qbit_ref, kbit_ref, lse_ref, del_ref, *refs):
+    if causal:
+        dq_in, dq_ref, dkv_ref, dk_acc, dv_acc = refs
+    else:
+        dq_ref, dkv_ref, dk_acc, dv_acc = refs
     kb = pl.program_id(0)
-    bk = k_ref.shape[0]
+    bk = kv_ref.shape[0]
     T = q_ref.shape[0]
     bq = BQ
-    factor = LOG2E * HEAD_SIZE ** (-0.5)
+
     @pl.when(kb == 0)
     def _():
-        dq_ref[...] = jnp.zeros_like(dq_ref)
-    dk_ref[...] = jnp.zeros_like(dk_ref)
-    dv_ref[...] = jnp.zeros_like(dv_ref)
-    def pair(ref, rows):
-        return jnp.concatenate([ref[rows, :HEAD_SIZE], ref[rows, HEAD_SIZE:]], axis=0)
+        if causal:
+            dq_ref[...] = dq_in[...]
+        else:
+            dq_ref[...] = jnp.zeros_like(dq_ref)
+
+    dk_acc[...] = jnp.zeros_like(dk_acc)
+    dv_acc[...] = jnp.zeros_like(dv_acc)
+
     def line(ref, rows):
         return jnp.concatenate([ref[0:1, rows], ref[1:2, rows]], axis=1)
+
     def step(qb, masked):
         rows = pl.ds(pl.multiple_of(qb * bq, bq), bq)
-        q = pair(q_ref, rows)
-        g = pair(g_ref, rows)
-        k = k_ref[...]
-        s = dg(k, q, NT) * factor - line(lse_ref, rows)
+        q = halves(q_ref, rows)
+        g = halves(g_ref, rows)
+        k = kv_ref[:, :HEAD_SIZE]
+        s = dg(k, q, NT) * (LOG2E * SCORE_SCALE) - line(lse_ref, rows)
         if masked:
             seen = (kbit_ref[...] & qbit_ref[0:1, rows]) != 0
-            at = lax.broadcasted_iota(jnp.int32, (bk, bq), 0) + kb * bk
-            row = lax.broadcasted_iota(jnp.int32, (bk, bq), 1) + base + qb * bq
-            seen = seen & (at <= row)
+            if causal:
+                at = lax.broadcasted_iota(jnp.int32, (bk, bq), 0) + kb * bk
+                row = lax.broadcasted_iota(jnp.int32, (bk, bq), 1) + qb * bq
+                seen = seen & (at <= row)
             s = jnp.where(jnp.concatenate([seen, seen], axis=1), s, -1e30)
         p = jnp.exp2(s)
-        dv_ref[...] += dg(p.astype(bf), g, NN)
-        dp = dg(v_ref[...], g, NT)
+        dv_acc[...] += dg(p.astype(bf), g, NN)
+        dp = dg(kv_ref[:, HEAD_SIZE:], g, NT)
         ds = (p * (dp - line(del_ref, rows))).astype(bf)
-        dk_ref[...] += dg(ds, q, NN)
+        dk_acc[...] += dg(ds, q, NN)
         dq = dg(ds, k, TN)
         dq_ref[rows, :HEAD_SIZE] += dq[:bq]
         dq_ref[rows, HEAD_SIZE:] += dq[bq:]
+
     def body(qb, _):
         flag = flags[qb, kb]
         pl.when(flag == 1)(lambda: step(qb, True))
         pl.when(flag == 2)(lambda: step(qb, False))
         return 0
+
     lax.fori_loop(0, T // bq, body, 0)
-
-def attn_backward(flags, q, g, k, v, qbit, kbit, lse, delta):
-    T = q.shape[0]; N = k.shape[0]
-    nk = N // BK
+    dkv_ref[:, :HEAD_SIZE] = (dk_acc[...] * SCORE_SCALE).astype(dkv_ref.dtype)
+    dkv_ref[:, HEAD_SIZE:] = dv_acc[...].astype(dkv_ref.dtype)
+
+
+def attend_back(causal, flags, q, g, kv, qbit, kbit, lse, delta, dq=None):
+    T = q.shape[0]
+    N = kv.shape[0]
+    W = 2 * HEAD_SIZE
     whole = lambda *s: pl.BlockSpec(s, lambda i, f: (0,) * len(s))
-    return pl.pallas_call(
-        partial(attn_backward_body, N - T),
+    along = lambda w: pl.BlockSpec((BK, w), lambda i, f: (i, 0))
+    in_specs = [whole(T, W), whole(T, W), along(W), whole(1, T), along(1), whole(2, T), whole(2, T)]
+    extra = []
+    if causal:
+        in_specs.append(whole(T, W))
+        extra = [dq]
+    return pl.pallas_call(
+        partial(attend_back_body, causal),
         grid_spec=pltpu.PrefetchScalarGridSpec(
-            num_scalar_prefetch=1, grid=(nk,),
-            in_specs=[whole(T, 256), whole(T, 256), pl.BlockSpec((BK, 128), lambda i, f: (i, 0)), pl.BlockSpec((BK, 128), lambda i, f: (i, 0)),
-                whole(1, T), pl.BlockSpec((BK, 1), lambda i, f: (i, 0)), whole(2, T), whole(2, T)],
-            out_specs=[whole(T, 256), pl.BlockSpec((BK, 128), lambda i, f: (i, 0)), pl.BlockSpec((BK, 128), lambda i, f: (i, 0))],
+            num_scalar_prefetch=1,
+            grid=(N // BK,),
+            in_specs=in_specs,
+            out_specs=[whole(T, W), along(W)],
+            scratch_shapes=[pltpu.VMEM((BK, HEAD_SIZE), f32), pltpu.VMEM((BK, HEAD_SIZE), f32)],
         ),
-        out_shape=[jax.ShapeDtypeStruct((T, 256), f32), jax.ShapeDtypeStruct((N, 128), f32), jax.ShapeDtypeStruct((N, 128), f32)],
-        cost_estimate=pl.CostEstimate(flops=5*2*T*N*256*3//4, bytes_accessed=12<<20, transcendentals=T*N*3//2),
-        name="attn_backward",
-    )(flags, q, g, k, v, qbit, kbit, lse, delta)
+        out_shape=[jax.ShapeDtypeStruct((T, W), f32), jax.ShapeDtypeStruct((N, W), f32 if causal else bf)],
+        cost_estimate=pl.CostEstimate(
+            flops=(5 if causal else 10) * T * N * W, bytes_accessed=12 << 20, transcendentals=T * N * (1 if causal else 2)
+        ),
+        name="attend_own_back" if causal else "attend_earlier_back",
+    )(flags, q, g, kv, qbit, kbit, lse, delta, *extra)
+
+
+def turn(values):
+    return pltpu.roll(values, HEAD_SIZE // 2, 1)
+
+
+def prepare_body(raw_ref, cos_ref, sin_ref, gain_ref, q_ref, kv_ref):
+    for i in range(3):
+        cols = slice(i * HEAD_SIZE, (i + 1) * HEAD_SIZE)
+        u = raw_ref[:, cols]
+        r = lax.rsqrt(jnp.mean(u * u, axis=-1, keepdims=True) + EPS)
+        n = u * r * gain_ref[(1 if i == 2 else 0) : (2 if i == 2 else 1), :]
+        out = (n * cos_ref[...] + turn(n) * sin_ref[...]).astype(bf)
+        if i < 2:
+            q_ref[:, cols] = out
+        else:
+            kv_ref[:, :HEAD_SIZE] = out
+    kv_ref[:, HEAD_SIZE:] = raw_ref[:, 3 * HEAD_SIZE : 4 * HEAD_SIZE].astype(bf)
+
+
+def prepare(raw, cos, sin, gains):
+    T, width = raw.shape
+    blk = lambda w: pl.BlockSpec((BQ, w), lambda i: (i, 0))
+    return pl.pallas_call(
+        prepare_body,
+        grid=(T // BQ,),
+        in_specs=[blk(width), blk(HEAD_SIZE), blk(HEAD_SIZE), pl.BlockSpec((2, HEAD_SIZE), lambda i: (0, 0))],
+        out_specs=[blk(2 * HEAD_SIZE), blk(2 * HEAD_SIZE)],
+        out_shape=[jax.ShapeDtypeStruct((T, 2 * HEAD_SIZE), bf)] * 2,
+        cost_estimate=pl.CostEstimate(flops=T * 4000, bytes_accessed=T * 640 * 8, transcendentals=T),
+        name="prepare_heads",
+    )(raw, cos, sin, gains)
+
+
+def prepare_back_body(raw_ref, cos_ref, sin_ref, gain_ref, dq_ref, dkv_ref, back_ref, dlogit_ref, out_ref, sums_ref):
+    @pl.when(pl.program_id(0) == 0)
+    def _():
+        sums_ref[...] = jnp.zeros_like(sums_ref)
+
+    for i in range(3):
+        cols = slice(i * HEAD_SIZE, (i + 1) * HEAD_SIZE)
+        if i < 2:
+            w = dq_ref[:, cols] * SCORE_SCALE
+        else:
+            w = dkv_ref[:, :HEAD_SIZE] + back_ref[:, :HEAD_SIZE].astype(f32)
+        u = raw_ref[:, cols]
+        j = 1 if i == 2 else 0
+        r = lax.rsqrt(jnp.mean(u * u, axis=-1, keepdims=True) + EPS)
+        w = w * cos_ref[...] + turn(w * sin_ref[...])
+        sums_ref[j : j + 1, :] += jnp.sum(w * u * r, axis=0, keepdims=True)
+        w = w * gain_ref[j : j + 1, :]
+        out_ref[:, cols] = (r * w - u * (r * r * r * jnp.mean(w * u, axis=-1, keepdims=True))).astype(bf)
+    out_ref[:, 3 * HEAD_SIZE : 4 * HEAD_SIZE] = (dkv_ref[:, HEAD_SIZE:] + back_ref[:, HEAD_SIZE:].astype(f32)).astype(bf)
+    out_ref[:, 4 * HEAD_SIZE :] = dlogit_ref[...]
+
+
+def prepare_back(raw, cos, sin, gains, dq, dkv, back, dlogit):
+    T, width = raw.shape
+    W = 2 * HEAD_SIZE
+    blk = lambda w: pl.BlockSpec((BQ, w), lambda i: (i, 0))
+    flat = pl.BlockSpec((2, HEAD_SIZE), lambda i: (0, 0))
+    return pl.pallas_call(
+        prepare_back_body,
+        grid=(T // BQ,),
+        in_specs=[blk(width), blk(HEAD_SIZE), blk(HEAD_SIZE), flat, blk(W), blk(W), blk(W), blk(HEAD_SIZE)],
+        out_specs=[blk(width), flat],
+        out_shape=[jax.ShapeDtypeStruct((T, width), bf), jax.ShapeDtypeStruct((2, HEAD_SIZE), f32)],
+        cost_estimate=pl.CostEstimate(flops=T * 8000, bytes_accessed=T * 640 * 10, transcendentals=T),
+        name="prepare_heads_back",
+    )(raw, cos, sin, gains, dq, dkv, back, dlogit)
+
+
+def gate_back_body(gm_ref, attn_ref, logit_ref, ga_ref, dlogit_ref, del_ref):
+    lanes = lax.broadcasted_iota(jnp.int32, dlogit_ref.shape, 1)
+    grads = jnp.zeros(dlogit_ref.shape, f32)
+    for h in range(2):
+        cols = slice(h * HEAD_SIZE, (h + 1) * HEAD_SIZE)
+        g = jax.nn.sigmoid(logit_ref[:, h : h + 1])
+        gm = gm_ref[:, cols]
+        at = attn_ref[:, cols]
+        ga = (gm * g).astype(bf)
+        ga_ref[:, cols] = ga
+        slope = jnp.sum(gm * at, axis=-1, keepdims=True) * (g * (1 - g))
+        grads = jnp.where(lanes == h, slope, grads)
+        del_ref[h : h + 1, :] = as_rows(jnp.sum(ga.astype(f32) * at, axis=-1, keepdims=True))
+    dlogit_ref[...] = grads.astype(bf)
+
+
+def gate_back(grad_mixed, attn, raw):
+    T, W = attn.shape
+    blk = lambda w, j=0: pl.BlockSpec((BQ, w), lambda i: (i, j))
+    return pl.pallas_call(
+        gate_back_body,
+        grid=(T // BQ,),
+        in_specs=[blk(W), blk(W), blk(HEAD_SIZE, raw.shape[1] // HEAD_SIZE - 1)],
+        out_specs=[blk(W), blk(HEAD_SIZE), pl.BlockSpec((2, BQ), lambda i: (0, i))],
+        out_shape=[
+            jax.ShapeDtypeStruct((T, W), bf),
+            jax.ShapeDtypeStruct((T, HEAD_SIZE), bf),
+            jax.ShapeDtypeStruct((2, T), f32),
+        ],
+        cost_estimate=pl.CostEstimate(flops=T * 3000, bytes_accessed=T * 640 * 8, transcendentals=T),
+        name="gate_back",
+    )(grad_mixed, attn, raw)
 
 
 GROUP=4
@@ -307,36 +486,97 @@
         name="trade_group",
     )(x)
 
+def far_places():
+    dp = lax.axis_index("dp")
+    return dp // GROUP, lax.axis_size("dp") // GROUP
+
+def gather_all_body(x_ref, out_ref, send, recv, local):
+    base, t, tx, ty, td, c = places()
+    r, count = far_places()
+    mates = [td, tx, ty]
+    others = [(r + i) % count for i in range(1, count)]
+    greet([(z * GROUP + t, c) for z in others] + [(base + who, c) for who in mates] + [(base + t, 1 - c)])
+    def copy(kind, src, dst, device):
+        return pltpu.make_async_remote_copy(src_ref=src, dst_ref=dst, send_sem=send.at[kind], recv_sem=recv.at[kind], device_id=device, device_id_type=MESH)
+    own = pltpu.make_async_copy(x_ref, out_ref.at[c, t, r], local)
+    own.start()
+    stage = [copy(i, x_ref, out_ref.at[c, t, r], (z * GROUP + t, c)) for i, z in enumerate(others)]
+    for one in stage: one.start()
+    own.wait()
+    for one in stage: one.wait()
+    stage = [copy(count - 1 + i, out_ref.at[c, t], out_ref.at[c, t], (base + who, c)) for i, who in enumerate(mates)]
+    for one in stage: one.start()
+    for one in stage: one.wait()
+    last = copy(count + 2, out_ref.at[c], out_ref.at[c], (base + t, 1 - c))
+    last.start()
+    last.wait()
+
+def gather_all(x):
+    count = lax.axis_size("dp") // GROUP
+    return pl.pallas_call(
+        gather_all_body,
+        out_shape=jax.ShapeDtypeStruct((2, GROUP, count) + x.shape, x.dtype),
+        in_specs=[pl.BlockSpec(memory_space=pltpu.VMEM)],
+        out_specs=pl.BlockSpec(memory_space=pltpu.VMEM),
+        scratch_shapes=[pltpu.SemaphoreType.DMA((count + 3,)), pltpu.SemaphoreType.DMA((count + 3,)), pltpu.SemaphoreType.DMA],
+        compiler_params=pltpu.CompilerParams(collective_id=11, has_side_effects=True),
+        name="gather_all",
+    )(x)
+
+def reduce_all_body(x_ref, out_ref, one_in, one_sum, two_in, two_sum, far_in, send, recv):
+    base, t, tx, ty, td, c = places()
+    r, count = far_places()
+    mates = [td, tx, ty]
+    others = [(r + i) % count for i in range(1, count)]
+    greet([(z * GROUP + t, c) for z in others] + [(base + who, c) for who in mates] + [(base + t, 1 - c)])
+    def copy(kind, src, dst, device):
+        return pltpu.make_async_remote_copy(src_ref=src, dst_ref=dst, send_sem=send.at[kind], recv_sem=recv.at[kind], device_id=device, device_id_type=MESH)
+    first = copy(0, x_ref.at[1 - c], one_in, (base + t, 1 - c))
+    first.start()
+    first.wait()
+    one_sum[...] = x_ref[c] + one_in[...]
+    stage = [copy(1 + i, one_sum.at[who], two_in.at[i], (base + who, c)) for i, who in enumerate(mates)]
+    for one in stage: one.start()
+    for one in stage: one.wait()
+    two_sum[...] = one_sum[t] + two_in[0] + two_in[1] + two_in[2]
+    stage = [copy(4 + i, two_sum.at[z], far_in.at[i], (z * GROUP + t, c)) for i, z in enumerate(others)]
+    for one in stage: one.start()
+    for one in stage: one.wait()
+    total = two_sum[r]
+    for i in range(count - 1):
+        total = total + far_in[i]
+    out_ref[...] = total
+
+def reduce_all(x):
+    tile = x.shape[3:]
+    count = lax.axis_size("dp") // GROUP
+    return pl.pallas_call(
+        reduce_all_body,
+        out_shape=jax.ShapeDtypeStruct(tile, x.dtype),
+        in_specs=[pl.BlockSpec(memory_space=pltpu.VMEM)],
+        out_specs=pl.BlockSpec(memory_space=pltpu.VMEM),
+        scratch_shapes=[pltpu.VMEM((GROUP, count) + tile, f32), pltpu.VMEM((GROUP, count) + tile, f32), pltpu.VMEM((3, count) + tile, f32), pltpu.VMEM((count,) + tile, f32), pltpu.VMEM((count - 1,) + tile, f32),
+            pltpu.SemaphoreType.DMA((count + 3,)), pltpu.SemaphoreType.DMA((count + 3,))],
+        compiler_params=pltpu.CompilerParams(collective_id=12, has_side_effects=True),
+        name="reduce_all",
+    )(x)
+
 
 def row_norm(values, gain):
     scale = lax.rsqrt(jnp.mean(values * values, axis=-1, keepdims=True) + EPS)
     return values * scale * gain
-
-
-def rotate(values):
-    half = values.shape[-1] // 2
-    return jnp.concatenate([-values[..., half:], values[..., :half]], axis=-1)
 
 
 def rope_tables(positions, width):
     half = width // 2
     freqs = THETA ** (-(jnp.arange(half, dtype=f32) / half))
     angle = positions.astype(f32)[:, None] * freqs[None, :]
-    angle = jnp.concatenate([angle, angle], axis=-1)
-    return (jnp.cos(angle)[:, None, :], jnp.sin(angle)[:, None, :])
-
-
-def prepare_heads(raw, gain, cosine_table, sine_table):
-    normed = row_norm(raw, gain)
-    return normed * cosine_table + rotate(normed) * sine_table
+    cosine, sine = jnp.cos(angle), jnp.sin(angle)
+    return (jnp.concatenate([cosine, cosine], axis=-1), jnp.concatenate([-sine, sine], axis=-1))
 
 
 def swiglu(gate, up):
     return jax.nn.silu(gate) * up
-
-
-def gating(attn, logit):
-    return attn * jax.nn.sigmoid(logit)[..., None]
 
 
 def ancestors(parent_row, count):
@@ -358,6 +598,10 @@
 
 def against(left, right):
     return dg(left, right, NT)
+
+
+def after(value, *others):
+    return lax.optimization_barrier((value,) + others)[0]
 
 
 def by_member(weight, pieces):
@@ -409,27 +653,33 @@
     pieces_glu = jnp.concatenate([by_member(gate_weight, GROUP), by_member(up_weight, GROUP)], axis=-1)
     pieces_down = by_member(down_weight.T, GROUP)
 
-    def far_gather(pieces, key):
-        mine = trade_group(pieces, key).reshape(GROUP * rows_here, -1)
-        return lax.all_gather(mine, "dp", axis=0, tiled=True, axis_index_groups=far)
-
-    full_attn = far_gather(pieces_attn, 3)
-    full_out = far_gather(pieces_out, 4)
-    full_glu = far_gather(pieces_glu, 5)
-    full_down = far_gather(pieces_down, 6)
-
-    def far_scatter(grad, key):
+    def far_gather(mine):
+        return lax.all_gather(
+            mine.reshape(GROUP * rows_here, -1), "dp", axis=0, tiled=True, axis_index_groups=far
+        )
+
+    def far_scatter(grad):
         mine = lax.psum_scatter(grad, "dp", scatter_dimension=0, tiled=True, axis_index_groups=far)
-        return trade_group(mine.reshape(GROUP, rows_here, -1), key)
+        return mine.reshape(GROUP, rows_here, -1)
+
+    mine_attn = trade_group(pieces_attn, 3)
+    full_attn = far_gather(mine_attn)
 
     sizes = [attn_gain.shape[0], mlp_gain.shape[0], query_norm_gain.shape[0], key_gain.shape[0]]
-    cuts = [0, sizes[0], sizes[0] + sizes[1], sizes[0] + sizes[1] + sizes[2], sum(sizes)]
-    gains = lax.all_gather(
-        jnp.concatenate([attn_gain, mlp_gain, query_norm_gain, key_gain]), ("dp", "mp"), axis=0, tiled=False
-    ).astype(f32)
+    cuts = [sum(sizes[:i]) for i in range(5)]
+    tile = (8, 128)
+    spare = tile[0] * tile[1] - cuts[4]
+    gain_tile = jnp.pad(
+        jnp.concatenate([attn_gain, mlp_gain, query_norm_gain, key_gain]).astype(f32), (0, spare)
+    ).reshape(tile)
+    all_gains = gather_all(after(gain_tile, mine_attn))
+    gains = all_gains.transpose(2, 1, 0, 3, 4).reshape(data_count * model_count, -1)
     gain_one, gain_two, gain_query, gain_key = [
         gains[:, cuts[i] : cuts[i + 1]].reshape(-1) for i in range(4)
     ]
+    head_gains = jnp.stack([gain_query, gain_key])
+    mine_out = trade_group(after(pieces_out, all_gains), 4)
+    full_out = far_gather(mine_out)
 
     group_index = lax.axis_index("dp") // GROUP
     first = group_index * group_tokens
@@ -452,113 +702,99 @@
     key_bits = jnp.sum(key_hot * powers[None, :], axis=1)
     query_has = jnp.max(onehot.reshape(-1, BQ, seg_count), axis=1)
     key_has = jnp.max(key_hot.reshape(-1, BK, seg_count), axis=1)
+    early = key_count - group_tokens
     reached = jnp.dot(jnp.dot(query_has, table), key_has.T) > 0
     missed = jnp.dot(jnp.dot(query_has, 1 - table), key_has.T) > 0
-    q_first = key_count - group_tokens + BQ * jnp.arange(query_has.shape[0], dtype=jnp.int32)[:, None]
+    q_first = early + BQ * jnp.arange(query_has.shape[0], dtype=jnp.int32)[:, None]
     k_first = BK * jnp.arange(key_has.shape[0], dtype=jnp.int32)[None, :]
     some = reached & (k_first <= q_first + BQ - 1)
     every = ~missed & (k_first + BK - 1 <= q_first)
     flags = jnp.where(some, jnp.where(every, 2, 1), 0).astype(jnp.int32)
-    cosine_table, sine_table = rope_tables(positions, HEAD_SIZE)
+    cosine, sine = rope_tables(positions, HEAD_SIZE)
+    query_column, query_line = query_bits[:, None], query_bits[None, :]
+    key_lines = key_bits.reshape(-1, 1, BK)
+    key_column = key_bits[:, None]
+    key_cut = early // BK
 
     rows = layer_in.astype(f32)
     normed_one, norm_one_back = jax.vjp(row_norm, rows, gain_one)
-    hidden_first = gather_group(normed_one.astype(bf))
-    grad_tokens = gather_group(out_grad)
+    hidden_first = gather_group(after(normed_one.astype(bf), mine_out))
     raw = jnp.dot(hidden_first, full_attn, preferred_element_type=f32)
     q_width = query_weight.shape[1] // GROUP
     k_width = key_matrix.shape[1] // GROUP
     heads = q_width // HEAD_SIZE
-    query_unnormed = raw[:, :q_width].reshape(group_tokens, heads, HEAD_SIZE)
-    key_unnormed = raw[:, q_width : q_width + k_width].reshape(group_tokens, 1, HEAD_SIZE)
-    value_rows = raw[:, q_width + k_width : q_width + 2 * k_width].astype(bf)
-    logit = raw[:, q_width + 2 * k_width : q_width + 2 * k_width + heads]
-    prepare = partial(prepare_heads, cosine_table=cosine_table, sine_table=sine_table)
-    query_f, query_back = jax.vjp(prepare, query_unnormed, gain_query)
-    key_f, key_back = jax.vjp(prepare, key_unnormed, gain_key)
-    query_rows = query_f.astype(bf).reshape(group_tokens, q_width)
-    key_rows = key_f.astype(bf).reshape(group_tokens, k_width)
+    query, pair = prepare(raw, cosine, sine, head_gains)
     ahead = [(s, s + GROUP) for s in range(data_count) if (s // GROUP) % planes == 0]
     back = [(d, s) for s, d in ahead]
-    both = lax.ppermute(jnp.concatenate([key_rows, value_rows], axis=1), "dp", ahead)
-    key_all = jnp.concatenate([both[:, :k_width], key_rows], axis=0)
-    value_all = jnp.concatenate([both[:, k_width:], value_rows], axis=0)
-    attn, lse = attn_forward(
-        flags, query_rows, key_all, value_all, query_bits[:, None], key_bits.reshape(-1, 1, BK)
-    )
-    attn = attn.reshape(group_tokens, heads, HEAD_SIZE)
-    mixed_f, gate_back = jax.vjp(gating, attn, logit)
-    mixed = mixed_f.astype(bf).reshape(group_tokens, -1)
-    middle = rows + reduce_group(against(mixed, full_out).astype(bf))
+    pair_early = lax.ppermute(pair, "dp", ahead)
+    mine_glu = trade_group(after(pieces_glu, query), 5)
+    full_glu = far_gather(mine_glu)
+    own = attend(True, flags[:, key_cut:], query, pair, query_column, key_lines[key_cut:])
+    mine_down = trade_group(after(pieces_down, own[0], mine_glu), 6)
+    full_down = far_gather(mine_down)
+    attn, mixed, lse = attend(
+        False, flags[:, :key_cut], query, pair_early, query_column, key_lines[:key_cut], (own[0], own[1], raw)
+    )
+    branch = reduce_group(after(against(mixed, full_out).astype(bf), mine_down))
+    middle = rows + branch
 
     normed_two, norm_two_back = jax.vjp(row_norm, middle, gain_two)
     h_two = gather_group(normed_two.astype(bf))
+    grad_tokens = gather_group(after(out_grad, h_two))
     both_glu = jnp.dot(h_two, full_glu, preferred_element_type=f32)
     units = full_down.shape[1]
     gate, up = both_glu[:, :units], both_glu[:, units:]
     hidden_f, glu_back = jax.vjp(swiglu, gate, up)
     hidden = hidden_f.astype(bf)
-    layer_out = (middle + reduce_group(against(hidden, full_down).astype(bf))).astype(bf)
-
-    down_grad = far_scatter(inner(grad_tokens, hidden).astype(bf), 7)
-    grad_hidden = jnp.dot(grad_tokens, full_down, preferred_element_type=f32)
+
+    down_part = inner(grad_tokens, hidden).astype(bf)
+    down_rows = far_scatter(down_part)
+    grad_hidden = jnp.dot(after(grad_tokens, down_part), full_down, preferred_element_type=f32)
     grad_gate_f, grad_up_f = glu_back(grad_hidden)
     grad_glu = jnp.concatenate([grad_gate_f.astype(bf), grad_up_f.astype(bf)], axis=1)
-    glu_grad = far_scatter(inner(h_two, grad_glu).astype(bf), 8)
-    grad_h_two = reduce_group(against(grad_glu, full_glu).astype(bf))
+    glu_part = inner(h_two, grad_glu).astype(bf)
+    glu_rows = far_scatter(glu_part)
+    grad_h_two = reduce_group(against(after(grad_glu, glu_part), full_glu).astype(bf))
     grad_mid_norm, gain_two_grad = norm_two_back(grad_h_two)
     grad_middle = out_grad.astype(f32) + grad_mid_norm
 
     grad_branch = gather_group(grad_middle.astype(bf))
-    output_grad = far_scatter(inner(grad_branch, mixed).astype(bf), 9)
-    grad_mixed = jnp.dot(grad_branch, full_out, preferred_element_type=f32).reshape(
-        group_tokens, heads, HEAD_SIZE
-    )
-    grad_attn_f, grad_logit_f = gate_back(grad_mixed)
-    grad_attn = grad_attn_f.astype(bf)
-    delta = jnp.sum(grad_attn.astype(f32) * attn, axis=-1)
-    grad_query, grad_key, grad_value = attn_backward(
-        flags,
-        query_rows,
-        grad_attn.reshape(group_tokens, q_width),
-        key_all,
-        value_all,
-        query_bits[None, :],
-        key_bits[:, None],
-        lse.T,
-        delta.T,
-    )
-    early = key_count - group_tokens
-    returned = lax.ppermute(
-        jnp.concatenate([grad_key[:early], grad_value[:early]], axis=1).astype(bf), "dp", back
-    ).astype(f32)
-    score_scale = HEAD_SIZE ** (-0.5)
-    grad_key = (grad_key[early:] + returned[:, :k_width]) * score_scale
-    grad_value = grad_value[early:] + returned[:, k_width:]
-    grad_q_raw, query_gain_grad = query_back((grad_query * score_scale).reshape(group_tokens, heads, HEAD_SIZE))
-    grad_k_raw, key_gain_grad = key_back(grad_key.reshape(group_tokens, 1, HEAD_SIZE))
-    grad_raw = jnp.concatenate(
+    grad_mixed = jnp.dot(grad_branch, full_out, preferred_element_type=f32)
+    out_part = inner(after(grad_branch, grad_mixed), mixed).astype(bf)
+    out_rows = far_scatter(out_part)
+    grad_attn, grad_logit, delta = gate_back(grad_mixed, attn, raw)
+    query_grad, early_grad = attend_back(
+        False, flags[:, :key_cut], after(query, out_part), grad_attn, pair_early, query_line, key_column[:early], lse, delta
+    )
+    returned = lax.ppermute(early_grad, "dp", back)
+    query_grad, own_grad = attend_back(
+        True, flags[:, key_cut:], query, grad_attn, pair, query_line, key_column[early:], lse, delta, query_grad
+    )
+    down_grad = trade_group(after(down_rows, own_grad), 7)
+    last_branch = reduce_group(after(against(after(hidden, own_grad), full_down).astype(bf), down_grad))
+    layer_out = (middle + last_branch).astype(bf)
+    glu_grad = trade_group(after(glu_rows, last_branch), 8)
+    grad_raw, head_gain_grads = prepare_back(
+        raw, cosine, sine, head_gains, query_grad, own_grad, after(returned, glu_grad), grad_logit
+    )
+    attn_part = inner(hidden_first, grad_raw).astype(bf)
+    attn_rows = far_scatter(attn_part)
+    grad_h_one = reduce_group(against(after(grad_raw, attn_part), full_attn).astype(bf))
+    grad_in_norm, gain_one_grad = norm_one_back(grad_h_one)
+    input_grad = (grad_middle + grad_in_norm).astype(bf)
+
+    devices = data_count * model_count
+    gain_parts = jnp.concatenate(
         [
-            grad_q_raw.reshape(group_tokens, -1),
-            grad_k_raw.reshape(group_tokens, -1),
-            grad_value,
-            jnp.pad(grad_logit_f, ((0, 0), (0, HEAD_SIZE - heads))),
+            piece.reshape(devices, -1)
+            for piece in (gain_one_grad, gain_two_grad, head_gain_grads[0], head_gain_grads[1], jnp.zeros((devices, spare), f32))
         ],
         axis=1,
-    ).astype(bf)
-    attn_grad = far_scatter(inner(hidden_first, grad_raw).astype(bf), 10)
-    grad_h_one = reduce_group(against(grad_raw, full_attn).astype(bf))
-    grad_in_norm, gain_one_grad = norm_one_back(grad_h_one)
-    input_grad = (grad_middle + grad_in_norm).astype(bf)
-
-    gain_parts = jnp.concatenate(
-        [
-            piece.reshape(data_count * model_count, -1)
-            for piece in (gain_one_grad, gain_two_grad, query_gain_grad, key_gain_grad)
-        ],
-        axis=1,
-    )
-    gain_sums = lax.psum_scatter(gain_parts, ("dp", "mp"), scatter_dimension=0, tiled=True)[0]
+    )
+    gain_parts = gain_parts.reshape((data_count // GROUP, GROUP, model_count) + tile).transpose(2, 1, 0, 3, 4)
+    gain_sums = reduce_all(gain_parts).reshape(-1)
+    out_weight_grad = trade_group(after(out_rows, gain_sums), 9)
+    attn_grad = trade_group(after(attn_rows, out_weight_grad), 10)
     full = lambda pieces: from_members(pieces).astype(f32)
     return (
         layer_out,
@@ -571,7 +807,7 @@
         full(attn_grad[:, :, q_width : q_width + k_width]),
         full(attn_grad[:, :, q_width + k_width : q_width + 2 * k_width]),
         full(attn_grad[:, :, q_width + 2 * k_width : q_width + 2 * k_width + heads]),
-        full(output_grad).T,
+        full(out_weight_grad).T,
         full(glu_grad[:, :, :units]),
         full(glu_grad[:, :, units:]),
         full(down_grad).T,

time: 1090 us -> 920 us (0.84)
  Pallas kernels: 476 us -> 608 us
  other arithmetic: 167 us -> 43 us
  blocking collectives: 100 us -> 0 us
  waiting for transfers between devices: 69.7 us -> 13.3 us
  local copies, waits for them, and re-layouts: 83.7 us -> 58.1 us
    pallas_call x2 -> x9, Pallas kernels: 42.4 us -> 174 us  [the longest x1 82.1 us: reduce_all(): pl.pallas_call(reduce_all_body, out_shape=jax.ShapeDtypeStruct(tile, x.dt...]
    unnamed x2 -> x0, blocking collectives: 100 us -> none
    ppermute x2, waiting for transfers between devices: 69.6 us -> 13 us  [the longest x1 13 us: per_device(): pair_early = lax.ppermute(pair, 'dp', ahead)]
    reduce_sum x4 -> x2, other arithmetic: 42.5 us -> 4.59 us  [row_norm(): return values * scale * gain]
    reduce_sum x1 -> x0, other arithmetic: 34.1 us -> none  [per_device(): delta = jnp.sum(grad_attn.astype(f32) * attn, axis=-1)]
    mul x7 -> x0, other arithmetic: 20.9 us -> none  [the longest x3 11.8 us: prepare_heads(): return normed * cosine_table + rotate(normed) * sine_table]
    convert_element_type x6 -> x2, other arithmetic: 17.1 us -> 3.3 us  [the longest x1 2.02 us: per_device(): hidden = hidden_f.astype(bf)]
    another operation x3 -> x2, other arithmetic: 12.9 us -> 0.76 us  [the longest x1 0.58 us: per_device(): head_gains = jnp.stack([gain_query, gain_key])]
  transfers between devices with their start and end apart: 10 -> 10, of which waited for: 2 -> 1; matrix products, arithmetic and copies ran while one was open for 21% -> 25% of each run, Pallas kernels for 31% -> 65%
where the time goes in v2:
time: 920 us; the launch traced here: 908 us
  Pallas kernels  608 us (66%)
  matrix products  153 us (17%)
  local copies, waits for them, and re-layouts  58.1 us (6%)
  other arithmetic  43 us (5%)
  between operations  27 us (3%)
  waiting for transfers between devices  13.3 us (1%)
    pallas_call x4, Pallas kernels, reduce_group(): pl.pallas_call(reduce_body, out_shape=jax.ShapeDtypeStruct((share, width)...  164 us
    pallas_call x4, Pallas kernels, gather_group(): pl.pallas_call(gather_body, out_shape=jax.ShapeDtypeStruct((share * GROUP...  163 us
    pallas_call x8, Pallas kernels, trade_group(): pl.pallas_call(trade_body, out_shape=jax.ShapeDtypeStruct(x.shape, x.dtyp...  106 us
    dot_general x8, matrix products, dg(): return lax.dot_general(left, right, dims, preferred_element_type=f32)  99.4 us
    pallas_call x1, Pallas kernels, reduce_all(): pl.pallas_call(reduce_all_body, out_shape=jax.ShapeDtypeStruct(tile, x.dt...  82.1 us
    pallas_call x2, Pallas kernels, attend_back(): pl.pallas_call(partial(attend_back_body, causal), grid_spec=pltpu.Prefetc...  30.2 us
    unnamed x82, local copies, waits for them, and re-layouts  28 us
    pallas_call x2, Pallas kernels, attend(): pl.pallas_call(partial(attend_body, causal, last), grid_spec=pltpu.Prefet...  24.4 us
  transfers between devices with their start and end apart: 10, of which 1 were waited for; matrix products, arithmetic and copies ran while one was open for 25% of the time, Pallas kernels for 65%

profile of v2, /device:TPU:0, one launch (start us, length us, event | category | flops | bytes accessed | tf_op | source)
XLA Modules:
  0.0 907.8 jit_solution(13063578177166361915)
XLA Ops:
  12.7 13.2 %trade_group.8 = bf16[4,128,640]{2,1,0:T(8,128)(2,1)} custom-call(bf16[4,128,640]{2,1,0:T(8,128)(2,1)} %fusion.41.x_ref), custom_call_target="tpu_custom_call" | custom-call | tf_op jit(solution)/shard_map/trade_group/pallas_call | solution.py:479
  26.7 12.4 %gather_all.1 = f32[2,4,4,8,128]{4,3,2,1,0:T(8,128)} custom-call(f32[8,128]{1,0:T(8,128)} %fusion.55.x_ref), custom_call_target="tpu_custom_call" | custom-call | tf_op jit(solution)/shard_map/gather_all/pallas_call | solution.py:516
  68.9 40.4 %gather_group.4 = bf16[2048,2048]{1,0:T(8,128)(2,1)} custom-call(bf16[256,2048]{1,0:T(8,128)(2,1)} %fusion.6.x_ref), custom_call_target="tpu_custom_call" | custom-call | tf_op jit(solution)/shard_map/gather_group/pallas_call | solution.py:384
  141.2 22.0 %trade_group.10 = bf16[4,128,1536]{2,1,0:T(8,128)(2,1)} custom-call(bf16[4,128,1536]{2,1,0:T(8,128)(2,1)} %pad_maximum_fusion.1.x_ref), custom_call_target="tpu_custom_call" | custom-call | tf_op jit(solution)/shard_map/trade_group/pallas_call | solution.py:479
  172.3 14.9 %attend_own.1 = (f32[2048,256]{1,0:T(8,128)}, f32[2048,2]{1,0:T(8,128)}) custom-call(s32[8,4]{1,0:T(8,128)} %get-tuple-element.217.flags, bf16[2048,256]{1,0:T(8,128)(2,1)} %get-tuple-element.140.q_ref, bf16[2048,256]{1,0:T(8,128)(2,1)} %get-tuple-element.125.kv_ref, s32[2048,1]{1,0:T(8,128)} %copy.72.qbit_ref, s32[4,1,512]{2,1,0:T(1,128)} %bitcast.171), custom_call_target="tpu_custom_call" | custom-call | flops 2147483648 | bytes 8388608 | tf_op jit(solution)/shard_map/attend_own/pallas_call | solution.py:117
  187.2 12.2 %trade_group.11 = bf16[4,128,768]{2,1,0:T(8,128)(2,1)} custom-call(bf16[4,128,768]{2,1,0:T(8,128)(2,1)} %bitcast.135), custom_call_target="tpu_custom_call" | custom-call | tf_op jit(solution)/shard_map/trade_group/pallas_call | solution.py:479
  199.5 13.0 %collective-permute-done.kv_ref = bf16[2048,256]{1,0:T(8,128)(2,1)} collective-permute-done((bf16[2048,256]{1,0:T(8,128)(2,1)S(1)}, bf16[2048,256]{1,0:T(8,128)(2,1)}, u32[]{:S(2)}, u32[]{:S(2)}) %collective-permute-start) | collective-permute-done | bytes 1048608 | tf_op jit(solution)/shard_map/ppermute | solution.py:729
  229.2 39.8 %reduce_group.4 = f32[256,2048]{1,0:T(8,128)} custom-call(bf16[2048,2048]{1,0:T(8,128)(2,1)} %convolution_convert_fusion.3.p_ref), custom_call_target="tpu_custom_call" | custom-call | tf_op jit(solution)/shard_map/reduce_group/pallas_call | solution.py:452
  272.3 41.6 %gather_group.5 = bf16[2048,2048]{1,0:T(8,128)(2,1)} custom-call(bf16[256,2048]{1,0:T(8,128)(2,1)} %multiply_convert_fusion.2.x_ref), custom_call_target="tpu_custom_call" | custom-call | tf_op jit(solution)/shard_map/gather_group/pallas_call | solution.py:384
  313.8 41.0 %gather_group.6 = bf16[2048,2048]{1,0:T(8,128)(2,1)} custom-call(bf16[256,2048]{1,0:T(8,128)(2,1)} %x_ref), custom_call_target="tpu_custom_call" | custom-call | tf_op jit(solution)/shard_map/gather_group/pallas_call | solution.py:384
  354.8 17.7 %fusion.81 = f32[2048,1536]{0,1:T(8,128)S(1)} fusion(bf16[2048,2048]{1,0:T(8,128)(2,1)} %gather_group.5, bf16[2048,1536]{1,0:T(8,128)(2,1)} %all-gather.9.cloned.1.call-done), kind=kOutput, calls=%fused_computation.146 | convolution fusion | flops 12884901888 | bytes 27262976 | tf_op jit(solution)/shard_map/dot_general | solution.py:744
  381.6 18.8 %convolution_convert_fusion.5 = bf16[2048,768]{1,0:T(8,128)(2,1)} fusion(bf16[2048,2048]{1,0:T(8,128)(2,1)S(1)} %copy-done.5, bf16[2048,768]{0,1:T(8,128)(2,1)S(1)} %multiply_convert_fusion.1), kind=kOutput, calls=%fused_computation.19 | convolution fusion | flops 6444023808 | bytes 14680064 | tf_op jit(solution)/shard_map/dot_general | solution.py:27
  400.5 16.4 %fusion.2 = (bf16[2048,768]{0,1:T(8,128)(2,1)S(1)}, bf16[2048,768]{0,1:T(8,128)(2,1)}) fusion(f32[2048,1536]{0,1:T(8,128)} %copy-done.3, bf16[2048,2048]{1,0:T(8,128)(2,1)} %gather_group.6, bf16[2048,768]{1,0:T(8,128)(2,1)} %all-gather.11.cloned.1.call-done), kind=kOutput, calls=%fused_computation.8 | convolution fusion | flops 6464471040 | bytes 30408704 | tf_op jit(solution)/shard_map/dot_general | solution.py:752
  418.6 18.3 %convolution_convert_fusion.4 = bf16[2048,1536]{1,0:T(8,128)(2,1)} fusion(bf16[2048,2048]{1,0:T(8,128)(2,1)} %gather_group.5, bf16[2048,768]{0,1:T(8,128)(2,1)} %get-tuple-element.197, bf16[2048,768]{0,1:T(8,128)(2,1)S(1)} %get-tuple-element.196), kind=kOutput, calls=%fused_computation.5 | convolution fusion | flops 12900630528 | bytes 20971520 | tf_op jit(solution)/shard_map/dot_general | solution.py:27
  444.2 17.6 %convolution_convert_fusion.2.p_ref = bf16[2048,2048]{1,0:T(8,128)(2,1)} fusion(bf16[2048,1536]{0,1:T(8,128)(2,1)S(1)} %pad_maximum_fusion, bf16[2048,1536]{1,0:T(8,128)(2,1)} %all-gather.9.cloned.1.call-done), kind=kOutput, calls=%fused_computation.3 | convolution fusion | flops 12889096192 | bytes 20971520 | tf_op jit(solution)/shard_map/dot_general | solution.py:27
  461.8 42.0 %reduce_group.5 = f32[256,2048]{1,0:T(8,128)} custom-call(bf16[2048,2048]{1,0:T(8,128)(2,1)} %convolution_convert_fusion.2.p_ref), custom_call_target="tpu_custom_call" | custom-call | tf_op jit(solution)/shard_map/reduce_group/pallas_call | solution.py:452
  508.1 40.5 %gather_group.7 = bf16[2048,2048]{1,0:T(8,128)(2,1)} custom-call(bf16[256,2048]{1,0:T(8,128)(2,1)} %fusion.72.x_ref), custom_call_target="tpu_custom_call" | custom-call | tf_op jit(solution)/shard_map/gather_group/pallas_call | solution.py:384
  573.5 24.0 %attend_own_back.1 = (f32[2048,256]{1,0:T(8,128)}, f32[2048,256]{1,0:T(8,128)}) custom-call(s32[8,4]{1,0:T(8,128)} %get-tuple-element.217.flags, bf16[2048,256]{1,0:T(8,128)(2,1)} %get-tuple-element.140.q_ref, bf16[2048,256]{1,0:T(8,128)(2,1)} %get-tuple-element.136.g_ref, bf16[2048,256]{1,0:T(8,128)(2,1)} %get-tuple-element.125.kv_ref, ...), custom_call_target="tpu_custom_call" | custom-call | flops 5368709120 | bytes 12582912 | tf_op jit(solution)/shard_map/attend_own_back/pallas_call | solution.py:201
  598.9 11.7 %convolution_convert_fusion.1.p_ref = bf16[2048,2048]{1,0:T(8,128)(2,1)} fusion(bf16[2048,768]{0,1:T(8,128)(2,1)} %copy-done.11, bf16[2048,768]{1,0:T(8,128)(2,1)} %all-gather.11.cloned.1.call-done), kind=kOutput, calls=%fused_computation.2 | convolution fusion | flops 6446645248 | bytes 14680064 | tf_op jit(solution)/shard_map/dot_general | solution.py:27
  610.5 13.4 %trade_group.12 = bf16[4,128,768]{2,1,0:T(8,128)(2,1)} custom-call(bf16[4,128,768]{2,1,0:T(8,128)(2,1)} %bitcast.151), custom_call_target="tpu_custom_call" | custom-call | tf_op jit(solution)/shard_map/trade_group/pallas_call | solution.py:479
  623.9 40.9 %reduce_group.6 = f32[256,2048]{1,0:T(8,128)} custom-call(bf16[2048,2048]{1,0:T(8,128)(2,1)} %convolution_convert_fusion.1.p_ref), custom_call_target="tpu_custom_call" | custom-call | tf_op jit(solution)/shard_map/reduce_group/pallas_call | solution.py:452
  664.9 22.0 %trade_group.13 = bf16[4,128,1536]{2,1,0:T(8,128)(2,1)} custom-call(bf16[4,128,1536]{2,1,0:T(8,128)(2,1)} %bitcast.143), custom_call_target="tpu_custom_call" | custom-call | tf_op jit(solution)/shard_map/trade_group/pallas_call | solution.py:479
  725.4 41.1 %reduce_group.7 = f32[256,2048]{1,0:T(8,128)} custom-call(bf16[2048,2048]{1,0:T(8,128)(2,1)} %convolution_convert_fusion.p_ref), custom_call_target="tpu_custom_call" | custom-call | tf_op jit(solution)/shard_map/reduce_group/pallas_call | solution.py:452
  769.9 82.1 %reduce_all.1 = f32[8,128]{1,0:T(8,128)} custom-call(f32[2,4,4,8,128]{4,3,2,1,0:T(8,128)} %bitcast.161), custom_call_target="tpu_custom_call" | custom-call | tf_op jit(solution)/shard_map/reduce_all/pallas_call | solution.py:553
  (227 shorter events, 223.9 us)
Async XLA Ops:
  7.2 31.9 %copy-start.16 = (bf16[1024,128]{1,0:T(8,128)(2,1)S(1)}, bf16[1024,128]{1,0:T(8,128)(2,1)}, u32[]{:S(2)}) copy-start(bf16[1024,128]{1,0:T(8,128)(2,1)} %param.40) | copy-start | bytes 786436
  7.2 114.6 %all-gather.5.cloned.1.call-start = ((), (), s32[]{:S(2)}) async-start(), calls=%async_computation.4 | async-start | bytes 3276800 | tf_op jit(solution)/shard_map/all_gather | solution.py:657
  8.4 39.3 %copy-start.32 = (s32[2,7]{1,0:T(2,128)S(1)}, s32[2,7]{1,0:T(2,128)}, u32[]{:S(2)}) copy-start(s32[2,7]{1,0:T(2,128)} %param.30) | copy-start | bytes 172
  8.5 39.3 %copy-start.33 = (s32[2,7]{1,0:T(2,128)S(1)}, s32[2,7]{1,0:T(2,128)}, u32[]{:S(2)}) copy-start(s32[2,7]{1,0:T(2,128)} %param.31) | copy-start | bytes 172
  26.0 196.0 %all-gather.7.cloned.1.call-start = ((), (), s32[]{:S(2)}) async-start(), calls=%async_computation.5 | async-start | bytes 1310720 | tf_op jit(solution)/shard_map/all_gather | solution.py:657
  47.6 19.7 %copy-start.1 = (bf16[256,2048]{1,0:T(8,128)(2,1)S(1)}, bf16[256,2048]{1,0:T(8,128)(2,1)}, u32[]{:S(2)}) copy-start(bf16[256,2048]{1,0:T(8,128)(2,1)} %param.28) | copy-start | bytes 3145732
  47.6 307.2 %all-gather.9.cloned.1.call-start = ((), (), s32[]{:S(2)}) async-start(), calls=%async_computation.6 | async-start | bytes 7864320 | tf_op jit(solution)/shard_map/all_gather | solution.py:657
  62.1 101.5 %copy-start.19 = (s32[2048]{0:T(1024)}, s32[2048]{0:T(1024)S(1)}, u32[]{:S(2)}) copy-start(s32[2048]{0:T(1024)S(1)} %get-tuple-element.188) | copy-start | bytes 24580
  67.3 42.0 %copy-start.17 = (f32[2048]{0:T(1024)}, f32[2048]{0:T(1024)S(1)}, u32[]{:S(2)}) copy-start(f32[2048]{0:T(1024)S(1)} %mul.247) | copy-start | bytes 24580
  67.6 41.7 %copy-start.24 = (f32[256]{0:T(256)}, f32[256]{0:T(256)S(1)}, u32[]{:S(2)}) copy-start(f32[256]{0:T(256)S(1)} %fusion.11) | copy-start | bytes 3076
  67.6 41.7 %copy-start.22 = (f32[256]{0:T(256)}, f32[256]{0:T(256)S(1)}, u32[]{:S(2)}) copy-start(f32[256]{0:T(256)S(1)} %fusion.58) | copy-start | bytes 3076
  141.2 23.9 %copy-start.15 = (bf16[3072,128]{1,0:T(8,128)(2,1)S(1)}, bf16[3072,128]{1,0:T(8,128)(2,1)}, u32[]{:S(2)}) copy-start(bf16[3072,128]{1,0:T(8,128)(2,1)} %param.43) | copy-start | bytes 2359300
  141.2 25.7 %copy-start.34 = (bf16[2048,256]{1,0:T(8,128)(2,1)S(1)}, bf16[2048,256]{1,0:T(8,128)(2,1)}, u32[]{:S(2)}) copy-start(bf16[2048,256]{1,0:T(8,128)(2,1)} %get-tuple-element.125.kv_ref) | copy-start | bytes 3145732
  163.2 237.3 %all-gather.11.cloned.1.call-start = ((), (), s32[]{:S(2)}) async-start(), calls=%async_computation.7 | async-start | bytes 3932160 | tf_op jit(solution)/shard_map/all_gather | solution.py:657
  166.9 45.7 %collective-permute-start = (bf16[2048,256]{1,0:T(8,128)(2,1)S(1)}, bf16[2048,256]{1,0:T(8,128)(2,1)}, u32[]{:S(2)}, u32[]{:S(2)}) collective-permute-start(bf16[2048,256]{1,0:T(8,128)(2,1)S(1)} %copy-done.34), channel_id=1, source_target_pairs={{0,8},{2,10},{4,12},{6,14},{16,24},{18,26},{20,28},{22,30},{1,9},{... | collective-permute-start | bytes 3145736 | tf_op jit(solution)/shard_map/ppermute | solution.py:729
  199.5 411.1 %reduce-scatter.5.cloned.1.call-start = ((), (), s32[]{:S(2)}) async-start(), calls=%async_computation.8 | async-start | bytes 3932160 | tf_op jit(solution)/shard_map/reduce_scatter | solution.py:662
  400.4 264.5 %reduce-scatter.7.cloned.1.call-start = ((), (), s32[]{:S(2)}) async-start(), calls=%async_computation.9 | async-start | bytes 7864320 | tf_op jit(solution)/shard_map/reduce_scatter | solution.py:662
  436.9 415.2 %reduce-scatter.11.cloned.1.call-start = ((), (), s32[]{:S(2)}) async-start(), calls=%async_computation.11 | async-start | bytes 1310720 | tf_op jit(solution)/shard_map/reduce_scatter | solution.py:662
  508.1 40.5 %copy-start.13 = (bf16[2048,256]{1,0:T(8,128)(2,1)S(1)}, bf16[2048,256]{1,0:T(8,128)(2,1)}, u32[]{:S(2)}) copy-start(bf16[2048,256]{1,0:T(8,128)(2,1)} %all-gather.7.cloned.1.call-done) | copy-start | bytes 3145732
  597.5 89.4 %collective-permute-start.1 = (bf16[2048,256]{1,0:T(8,128)(2,1)}, bf16[2048,256]{1,0:T(8,128)(2,1)S(1)}, u32[]{:S(2)}, u32[]{:S(2)}) collective-permute-start(bf16[2048,256]{1,0:T(8,128)(2,1)} %get-tuple-element.147), channel_id=1, source_target_pairs={{8,0},{10,2},{12,4},{14,6},{24,16},{26,18},{28,20},{30,22},{9,1},{... | collective-permute-start | bytes 3145736 | tf_op jit(solution)/shard_map/ppermute | solution.py:769
  598.8 286.1 %reduce-scatter.9.cloned.1.call-start = ((), (), s32[]{:S(2)}) async-start(), calls=%async_computation.10 | async-start | bytes 3276800 | tf_op jit(solution)/shard_map/reduce_scatter | solution.py:662
  725.4 41.1 %copy-start.2 = (bf16[256,2048]{1,0:T(8,128)(2,1)S(1)}, bf16[256,2048]{1,0:T(8,128)(2,1)}, u32[]{:S(2)}) copy-start(bf16[256,2048]{1,0:T(8,128)(2,1)} %param.28) | copy-start | bytes 3145732
  725.4 41.1 %copy-start.18 = (f32[2048]{0:T(1024)S(1)}, f32[2048]{0:T(1024)}, u32[]{:S(2)}) copy-start(f32[2048]{0:T(1024)} %copy-done.17) | copy-start | bytes 24580
  725.4 41.1 %copy-start.23 = (f32[256]{0:T(256)S(1)}, f32[256]{0:T(256)}, u32[]{:S(2)}) copy-start(f32[256]{0:T(256)} %copy-done.22) | copy-start | bytes 3076
  (21 other events, 137.1 us)
Sparse Core Ops, SparseCore 0:
  26.1 54.9 all-gather.4
  82.7 26.7 all-gather.6
  163.3 129.6 all-gather.8
  294.4 64.3 all-gather.10
  400.5 112.9 reduce-scatter.4
  515.7 110.6 reduce-scatter.6
  628.7 83.2 reduce-scatter.10
  714.3 116.2 reduce-scatter.8

commit v3 on v2

--- a/solution.py
+++ b/solution.py
@@ -319,8 +319,9 @@
     )(grad_mixed, attn, raw)
 
 
-GROUP=4
-MESH=pl.DeviceIdType.MESH
+GROUP = 4
+MESH = pl.DeviceIdType.MESH
+QUICK = pl.CostEstimate(flops=0, bytes_accessed=1 << 16, transcendentals=0)
 
 def places():
     dp = lax.axis_index("dp"); c = lax.axis_index("mp")
@@ -388,50 +389,94 @@
         out_specs=pl.BlockSpec(memory_space=pl.ANY),
         scratch_shapes=[pltpu.SemaphoreType.DMA((13,)), pltpu.SemaphoreType.DMA((13,)), pltpu.SemaphoreType.DMA],
         compiler_params=pltpu.CompilerParams(collective_id=1, has_side_effects=True),
+        cost_estimate=QUICK,
         name="gather_group",
     )(x)
 
-def reduce_body(p_ref, out_ref, near, mates, sums, xin, yin, zin, turn, load, send, recv):
+def reduce_body(left_ref, right_ref, out_ref, left, right, fars, near, mates, sums, xin, yin, zin, turned, fetch, send, recv):
     base, t, tx, ty, td, c = places()
     share = out_ref.shape[0]
     half = share // 2
+    chunk = right.shape[0] // 4
     xdev, ydev, mate = (base + tx, c), (base + ty, c), (base + t, 1 - c)
+    order = [td, tx, ty, t]
+    lefts, rights = [], []
+    for i, who in enumerate(order):
+        for side, core in enumerate((1 - c, c)):
+            rows = pl.ds(pl.multiple_of((2 * who + core) * share, share), share)
+            n = 2 * i + side
+            lefts.append(pltpu.make_async_copy(left_ref.at[rows], left.at[n], fetch.at[n]))
+    for j in range(4):
+        rows = pl.ds(j * chunk, chunk)
+        rights.append(pltpu.make_async_copy(right_ref.at[rows], right.at[rows], fetch.at[8 + j]))
+    for one in lefts[:2] + rights + lefts[2:]:
+        one.start()
     greet([xdev, ydev, mate])
-    def spot(who, core):
-        return p_ref.at[pl.ds(pl.multiple_of((2 * who + core) * share, share), share)]
+
     def copy(kind, src, dst, device):
-        return pltpu.make_async_remote_copy(src_ref=src, dst_ref=dst, send_sem=send.at[kind], recv_sem=recv.at[kind], device_id=device, device_id_type=MESH)
-    def add(dst, left, right):
+        return pltpu.make_async_remote_copy(
+            src_ref=src, dst_ref=dst, send_sem=send.at[kind], recv_sem=recv.at[kind], device_id=device, device_id_type=MESH
+        )
+
+    def product(n, dst):
+        lefts[n].wait()
+
+        def go(j, _):
+            rows = pl.ds(pl.multiple_of(j * chunk, chunk), chunk)
+            dst[:, rows] = dg(left[n], right[rows, :], NT).astype(dst.dtype)
+            return 0
+
+        if n == 0:
+            for j in range(4):
+                rights[j].wait()
+                go(j, 0)
+        else:
+            lax.fori_loop(0, 4, go, 0)
+
+    def add(dst, one, two):
         step = 16
+
         def go(i, _):
             rows = pl.ds(pl.multiple_of(i * step, step), step)
-            dst[rows, :] = (left[rows, :].astype(f32) + right[rows, :].astype(f32)).astype(dst.dtype)
+            dst[rows, :] = (one[rows, :].astype(f32) + two[rows, :].astype(f32)).astype(dst.dtype)
             return 0
+
         lax.fori_loop(0, dst.shape[0] // step, go, 0)
-    order = [td, tx, ty, t]
-    over, loads = [], []
-    for i, who in enumerate(order):
-        over.append(copy(i, spot(who, 1 - c), mates.at[i], mate)); over[i].start()
-        loads.append(pltpu.make_async_copy(spot(who, c), near.at[i], load.at[i])); loads[i].start()
+
     A, B = pl.ds(0, half), pl.ds(half, half)
-    k = {}
-    for i in range(4):
-        loads[i].wait()
+    over, k = [], {}
+
+    def join(i):
         over[i].wait_recv()
         add(sums.at[i], near.at[i], mates.at[i])
         if i == 0:
-            k[4] = copy(4, sums.at[0, A], xin.at[1], xdev); k[4].start()
-            k[5] = copy(5, sums.at[0, B], yin.at[1], ydev); k[5].start()
+            k[4] = copy(4, sums.at[0, A], xin.at[1], xdev)
+            k[5] = copy(5, sums.at[0, B], yin.at[1], ydev)
+            k[4].start()
+            k[5].start()
         if i == 1:
-            k[6] = copy(6, sums.at[1, A], xin.at[0], xdev); k[6].start()
+            k[6] = copy(6, sums.at[1, A], xin.at[0], xdev)
+            k[6].start()
         if i == 2:
-            k[7] = copy(7, sums.at[2, B], yin.at[0], ydev); k[7].start()
+            k[7] = copy(7, sums.at[2, B], yin.at[0], ydev)
+            k[7].start()
+
+    for i in range(4):
+        product(2 * i, fars.at[i])
+        over.append(copy(i, fars.at[i], mates.at[i], mate))
+        over[i].start()
+        product(2 * i + 1, near.at[i])
+        if i:
+            join(i - 1)
+    join(3)
     k[4].wait_recv()
-    add(turn.at[0], sums.at[2, A], xin.at[1])
-    k[8] = copy(8, turn.at[0], zin.at[0], ydev); k[8].start()
+    add(turned.at[0], sums.at[2, A], xin.at[1])
+    k[8] = copy(8, turned.at[0], zin.at[0], ydev)
+    k[8].start()
     k[5].wait_recv()
-    add(turn.at[1], sums.at[1, B], yin.at[1])
-    k[9] = copy(9, turn.at[1], zin.at[1], xdev); k[9].start()
+    add(turned.at[1], sums.at[1, B], yin.at[1])
+    k[9] = copy(9, turned.at[1], zin.at[1], xdev)
+    k[9].start()
     k[6].wait_recv()
     add(out_ref.at[A], sums.at[3, A], xin.at[0])
     k[7].wait_recv()
@@ -445,46 +490,303 @@
     for kind in range(4, 10):
         k[kind].wait_send()
 
-def reduce_group(p):
-    rows, width = p.shape
+
+def product_reduce(left, right, key):
+    rows, depth = left.shape
+    width = right.shape[0]
     share = rows // (2 * GROUP)
     half = share // 2
+    block = lambda n, r: pltpu.VMEM((n, r, width), bf)
     return pl.pallas_call(
         reduce_body,
         out_shape=jax.ShapeDtypeStruct((share, width), f32),
-        in_specs=[pl.BlockSpec(memory_space=pl.ANY)],
+        in_specs=[pl.BlockSpec(memory_space=pl.ANY)] * 2,
         out_specs=pl.BlockSpec(memory_space=pltpu.VMEM),
-        scratch_shapes=[pltpu.VMEM((4, share, width), bf), pltpu.VMEM((4, share, width), bf), pltpu.VMEM((4, share, width), bf),
-            pltpu.VMEM((2, half, width), bf), pltpu.VMEM((2, half, width), bf), pltpu.VMEM((2, half, width), bf), pltpu.VMEM((2, half, width), bf),
-            pltpu.SemaphoreType.DMA((4,)), pltpu.SemaphoreType.DMA((10,)), pltpu.SemaphoreType.DMA((10,))],
-        compiler_params=pltpu.CompilerParams(collective_id=2, has_side_effects=True),
-        name="reduce_group",
-    )(p)
-
-def trade_body(x_ref, out_ref, send, recv, local):
+        scratch_shapes=[
+            pltpu.VMEM((2 * GROUP, share, depth), bf),
+            pltpu.VMEM((width, depth), bf),
+            block(4, share),
+            block(4, share),
+            block(4, share),
+            block(4, share),
+            block(2, half),
+            block(2, half),
+            block(2, half),
+            block(2, half),
+            pltpu.SemaphoreType.DMA((12,)),
+            pltpu.SemaphoreType.DMA((10,)),
+            pltpu.SemaphoreType.DMA((10,)),
+        ],
+        compiler_params=pltpu.CompilerParams(collective_id=key, has_side_effects=True, vmem_limit_bytes=56 << 20),
+        cost_estimate=QUICK,
+        name="product_reduce",
+    )(left, right)
+
+
+def gather_product_body(glu, x_ref, w_ref, full_ref, y_ref, *refs):
+    if glu:
+        hidden_ref, refs = refs[0], refs[1:]
+        hs, refs = refs[0], refs[1:]
+    buf, w, ys, fetch, put_x, put_y, send, recv = refs
+    base, t, tx, ty, td, c = places()
+    share = x_ref.shape[0]
+    half = share // 2
+    width = w.shape[1]
+    xdev, ydev, mate = (base + tx, c), (base + ty, c), (base + t, 1 - c)
+    weights = pltpu.make_async_copy(w_ref, w, fetch)
+    weights.start()
+    greet([xdev, ydev, mate])
+
+    def unit(who, core):
+        return pl.ds(pl.multiple_of((2 * who + core) * share, share), share)
+
+    def spot(who, part):
+        start = (2 * who + c) * share + part * half
+        return buf.at[pl.ds(pl.multiple_of(start, half), half)]
+
+    def copy(kind, src, dst, device):
+        one = pltpu.make_async_remote_copy(
+            src_ref=src, dst_ref=dst, send_sem=send.at[kind], recv_sem=recv.at[kind], device_id=device, device_id_type=MESH
+        )
+        one.start()
+        return one
+
+    mine = [x_ref.at[pl.ds(0, half)], x_ref.at[pl.ds(half, half)]]
+    k, puts = {}, []
+    k[2] = copy(2, mine[0], spot(t, 0), ydev)
+    k[1] = copy(1, mine[1], spot(t, 1), xdev)
+    k[3] = copy(3, mine[1], spot(t, 1), ydev)
+    k[0] = copy(0, mine[0], spot(t, 0), xdev)
+    k[6] = copy(6, x_ref, buf.at[unit(t, c)], mate)
+    weights.wait()
+
+    def work(n, src, who, core):
+        rows = unit(who, core)
+        slot = n % 2
+        one = pltpu.make_async_copy(src, full_ref.at[rows], put_x.at[n])
+        one.start()
+        if n >= 2:
+            for old in puts[n - 2][1:]:
+                old.wait()
+        if glu:
+            chunk = 256
+
+            def go(j, _):
+                left = pl.ds(pl.multiple_of(j * chunk, chunk), chunk)
+                right = pl.ds(pl.multiple_of(width // 2 + j * chunk, chunk), chunk)
+                gate = dg(src[...], w[:, left], NN)
+                up = dg(src[...], w[:, right], NN)
+                ys[slot, :, left] = gate
+                ys[slot, :, right] = up
+                hs[slot, :, left] = (gate * jax.nn.sigmoid(gate) * up).astype(bf)
+                return 0
+
+            lax.fori_loop(0, width // 2 // chunk, go, 0)
+        else:
+            chunk = 128 if width % 256 else 256
+
+            def go(j, _):
+                cols = pl.ds(pl.multiple_of(j * chunk, chunk), chunk)
+                ys[slot, :, cols] = dg(src[...], w[:, cols], NN)
+                return 0
+
+            lax.fori_loop(0, width // chunk, go, 0)
+        outs = [one, pltpu.make_async_copy(ys.at[slot], y_ref.at[rows], put_y.at[n])]
+        if glu:
+            outs.append(pltpu.make_async_copy(hs.at[slot], hidden_ref.at[rows], put_y.at[8 + n]))
+        for out in outs[1:]:
+            out.start()
+        puts.append(outs)
+
+    def landed(who, core):
+        return buf.at[unit(who, core)]
+
+    work(0, x_ref, t, c)
+    k[6].wait_recv()
+    work(1, landed(t, 1 - c), t, 1 - c)
+    k[2].wait_recv()
+    k[4] = copy(4, spot(ty, 0), spot(ty, 0), xdev)
+    k[9] = copy(9, spot(ty, 0), spot(ty, 0), mate)
+    k[1].wait_recv()
+    k[5] = copy(5, spot(tx, 1), spot(tx, 1), ydev)
+    k[8] = copy(8, spot(tx, 1), spot(tx, 1), mate)
+    k[0].wait_recv()
+    k[7] = copy(7, spot(tx, 0), spot(tx, 0), mate)
+    k[3].wait_recv()
+    k[10] = copy(10, spot(ty, 1), spot(ty, 1), mate)
+    work(2, landed(tx, c), tx, c)
+    work(3, landed(ty, c), ty, c)
+    k[7].wait_recv()
+    k[8].wait_recv()
+    work(4, landed(tx, 1 - c), tx, 1 - c)
+    k[9].wait_recv()
+    k[10].wait_recv()
+    work(5, landed(ty, 1 - c), ty, 1 - c)
+    k[4].wait_recv()
+    k[11] = copy(11, spot(td, 0), spot(td, 0), mate)
+    k[5].wait_recv()
+    k[12] = copy(12, spot(td, 1), spot(td, 1), mate)
+    work(6, landed(td, c), td, c)
+    k[11].wait_recv()
+    k[12].wait_recv()
+    work(7, landed(td, 1 - c), td, 1 - c)
+    for kind in range(13):
+        k[kind].wait_send()
+    for n, outs in enumerate(puts):
+        outs[0].wait()
+        if n >= 6:
+            for out in outs[1:]:
+                out.wait()
+
+
+def gather_product(x, w, key, glu=False):
+    share, depth = x.shape
+    width = w.shape[1]
+    rows = share * GROUP * 2
+    anywhere = pl.BlockSpec(memory_space=pl.ANY)
+    outs = [jax.ShapeDtypeStruct((rows, depth), bf), jax.ShapeDtypeStruct((rows, width), f32)]
+    extra = []
+    if glu:
+        outs.append(jax.ShapeDtypeStruct((rows, width // 2), bf))
+        extra = [pltpu.VMEM((2, share, width // 2), bf)]
+    return pl.pallas_call(
+        partial(gather_product_body, glu),
+        out_shape=outs,
+        in_specs=[pl.BlockSpec(memory_space=pltpu.VMEM), anywhere],
+        out_specs=[anywhere] * len(outs),
+        scratch_shapes=extra
+        + [
+            pltpu.VMEM((rows, depth), bf),
+            pltpu.VMEM((depth, width), bf),
+            pltpu.VMEM((2, share, width), f32),
+            pltpu.SemaphoreType.DMA,
+            pltpu.SemaphoreType.DMA((8,)),
+            pltpu.SemaphoreType.DMA((16,)),
+            pltpu.SemaphoreType.DMA((13,)),
+            pltpu.SemaphoreType.DMA((13,)),
+        ],
+        compiler_params=pltpu.CompilerParams(collective_id=key, has_side_effects=True, vmem_limit_bytes=48 << 20),
+        cost_estimate=QUICK,
+        name="gather_product",
+    )(x, w)
+
+
+def trade_body(widths, kv, out_side, *refs):
+    count = len(widths)
     base, t, tx, ty, td, c = places()
     partners = [td, tx, ty]
-    greet([(base + who, c) for who in partners])
-    own = pltpu.make_async_copy(x_ref.at[t], out_ref.at[t], local)
+    friends = [(base + who, c) for who in partners]
+    if kv:
+        ins, refs = refs[: count + 1], refs[count + 1 :]
+        outs, refs = refs[:2], refs[2:]
+        send, recv, local = refs
+        plane = lax.axis_index("dp") // GROUP
+        late = plane % kv
+        friends.append((lax.axis_index("dp") + (GROUP - 2 * GROUP * late), c))
+    elif out_side:
+        ins, outs, (send, recv, local) = refs[:1], refs[1 : 1 + count], refs[1 + count :]
+    else:
+        ins, outs, (send, recv, local) = refs[:count], refs[count : count + 1], refs[count + 1 :]
+    greet(friends)
+    starts = [sum(widths[:i]) for i in range(count)]
+
+    def column(who, width):
+        return pl.ds(pl.multiple_of(who * width, width), width)
+
+    def source(i, who):
+        if out_side:
+            return ins[0].at[who, :, pl.ds(starts[i], widths[i])]
+        return ins[i].at[:, column(who, widths[i])]
+
+    def target(i):
+        if out_side:
+            return outs[i].at[:, column(t, widths[i])]
+        return outs[0].at[t, :, pl.ds(starts[i], widths[i])]
+
     copies = []
-    for i, who in enumerate(partners):
-        copies.append(pltpu.make_async_remote_copy(src_ref=x_ref.at[who], dst_ref=out_ref.at[t], send_sem=send.at[i], recv_sem=recv.at[i], device_id=(base + who, c), device_id_type=MESH))
-        copies[i].start()
-    own.start()
+    for j, who in enumerate(partners):
+        for i in range(count):
+            kind = j * count + i
+            one = pltpu.make_async_remote_copy(
+                src_ref=source(i, who),
+                dst_ref=target(i),
+                send_sem=send.at[kind],
+                recv_sem=recv.at[kind],
+                device_id=(base + who, c),
+                device_id_type=MESH,
+            )
+            one.start()
+            copies.append(one)
+    if kv:
+        pair = pltpu.make_async_remote_copy(
+            src_ref=ins[count],
+            dst_ref=outs[1],
+            send_sem=send.at[3 * count],
+            recv_sem=recv.at[3 * count],
+            device_id=friends[-1],
+            device_id_type=MESH,
+        )
+        keep = pltpu.make_async_copy(ins[count], outs[1], local.at[count])
+
+        @pl.when(late == 0)
+        def _():
+            pair.start()
+            keep.start()
+
+    owns = [pltpu.make_async_copy(source(i, t), target(i), local.at[i]) for i in range(count)]
+    for own in owns:
+        own.start()
     for one in copies:
         one.wait()
-    own.wait()
-
-def trade_group(x, key):
+    for own in owns:
+        own.wait()
+    if kv:
+
+        @pl.when(late == 0)
+        def _():
+            pair.wait_send()
+            keep.wait()
+
+        @pl.when(late == 1)
+        def _():
+            pair.wait_recv()
+
+
+def trade_call(ins, outs, widths, key, kv, out_side):
+    vmem = pl.BlockSpec(memory_space=pltpu.VMEM)
+    anywhere = pl.BlockSpec(memory_space=pl.ANY)
+    kinds = 3 * len(widths) + 1
     return pl.pallas_call(
-        trade_body,
-        out_shape=jax.ShapeDtypeStruct(x.shape, x.dtype),
-        in_specs=[pl.BlockSpec(memory_space=pltpu.VMEM)],
-        out_specs=pl.BlockSpec(memory_space=pl.ANY),
-        scratch_shapes=[pltpu.SemaphoreType.DMA((3,)), pltpu.SemaphoreType.DMA((3,)), pltpu.SemaphoreType.DMA],
+        partial(trade_body, widths, kv, out_side),
+        out_shape=outs,
+        in_specs=[vmem] * len(ins),
+        out_specs=[anywhere] * len(outs),
+        scratch_shapes=[
+            pltpu.SemaphoreType.DMA((kinds,)),
+            pltpu.SemaphoreType.DMA((kinds,)),
+            pltpu.SemaphoreType.DMA((len(widths) + 1,)),
+        ],
         compiler_params=pltpu.CompilerParams(collective_id=key, has_side_effects=True),
+        cost_estimate=QUICK,
         name="trade_group",
-    )(x)
+    )(*ins)
+
+
+def trade_group(weights, key, pair=None, planes=2):
+    rows = weights[0].shape[0]
+    widths = tuple(w.shape[1] // GROUP for w in weights)
+    outs = [jax.ShapeDtypeStruct((GROUP, rows, sum(widths)), bf)]
+    if pair is None:
+        return trade_call(weights, outs, widths, key, 0, False)[0]
+    outs.append(jax.ShapeDtypeStruct(pair.shape, bf))
+    return trade_call(list(weights) + [pair], outs, widths, key, planes, False)
+
+
+def trade_back(grad, widths, key):
+    rows = grad.shape[1]
+    outs = [jax.ShapeDtypeStruct((rows, GROUP * w), bf) for w in widths]
+    return trade_call([grad], outs, tuple(widths), key, 0, True)
+
 
 def far_places():
     dp = lax.axis_index("dp")
@@ -520,6 +822,7 @@
         out_specs=pl.BlockSpec(memory_space=pltpu.VMEM),
         scratch_shapes=[pltpu.SemaphoreType.DMA((count + 3,)), pltpu.SemaphoreType.DMA((count + 3,)), pltpu.SemaphoreType.DMA],
         compiler_params=pltpu.CompilerParams(collective_id=11, has_side_effects=True),
+        cost_estimate=QUICK,
         name="gather_all",
     )(x)
 
@@ -558,6 +861,7 @@
         scratch_shapes=[pltpu.VMEM((GROUP, count) + tile, f32), pltpu.VMEM((GROUP, count) + tile, f32), pltpu.VMEM((3, count) + tile, f32), pltpu.VMEM((count,) + tile, f32), pltpu.VMEM((count - 1,) + tile, f32),
             pltpu.SemaphoreType.DMA((count + 3,)), pltpu.SemaphoreType.DMA((count + 3,))],
         compiler_params=pltpu.CompilerParams(collective_id=12, has_side_effects=True),
+        cost_estimate=QUICK,
         name="reduce_all",
     )(x)
 
@@ -569,48 +873,109 @@
 
 def rope_tables(positions, width):
     half = width // 2
-    freqs = THETA ** (-(jnp.arange(half, dtype=f32) / half))
-    angle = positions.astype(f32)[:, None] * freqs[None, :]
-    cosine, sine = jnp.cos(angle), jnp.sin(angle)
-    return (jnp.concatenate([cosine, cosine], axis=-1), jnp.concatenate([-sine, sine], axis=-1))
-
-
-def swiglu(gate, up):
-    return jax.nn.silu(gate) * up
-
-
-def ancestors(parent_row, count):
-    table = jnp.eye(count, dtype=jnp.int32)
-    for seg_index in range(1, count):
-        joined = jnp.maximum(table[seg_index], table[parent_row[seg_index]])
-        table = table.at[seg_index].set(joined)
-    return table
-
-
-def segment_onehot(offsets, starts, count):
-    segment = jnp.sum((offsets[:, None] >= starts[None, 1:]).astype(jnp.int32), axis=1)
-    return (segment[:, None] == jnp.arange(count, dtype=jnp.int32)[None, :]).astype(jnp.int32)
+    lanes = jnp.arange(width, dtype=jnp.int32)
+    freqs = THETA ** (-((lanes % half).astype(f32) / half))
+    angle = positions.astype(f32) * freqs[None, :]
+    return jnp.cos(angle), jnp.sin(angle) * jnp.where(lanes < half, -1.0, 1.0)[None, :]
+
+
+def tables_body(group_tokens, early, seg_count, parents, lengths, pos_ref, qcol_ref, qline_ref, kline_ref, kcol_ref, flags, key_any):
+    step = pl.program_id(0)
+    first = lax.axis_index("dp") // GROUP * group_tokens
+    tree = first // TREE_TOKENS
+    begin = first - tree * TREE_TOKENS
+    size = [lengths[tree, seg] for seg in range(seg_count)]
+    starts, bits, depth = [jnp.int32(0)], [jnp.int32(1)], [jnp.int32(0)]
+    for seg in range(1, seg_count):
+        starts.append(starts[-1] + size[seg - 1])
+        parent = parents[tree, seg]
+        above, deep = bits[0], depth[0] + size[0]
+        for p in range(1, seg):
+            above = jnp.where(parent == p, bits[p], above)
+            deep = jnp.where(parent == p, depth[p] + size[p], deep)
+        bits.append(above | (1 << seg))
+        depth.append(deep)
+    powers = [jnp.int32(1 << seg) for seg in range(seg_count)]
+
+    def by_segment(offsets, values):
+        out = jnp.zeros_like(offsets) + values[0]
+        for start, value in zip(starts[1:], values[1:]):
+            out = jnp.where(offsets >= start, value, out)
+        return out
+
+    q_first = begin + step * BQ
+    k_first = begin - early + step * BK
+    column = lax.broadcasted_iota(jnp.int32, (BQ, 1), 0) + q_first
+    pos_ref[...] = by_segment(column, [d - s for d, s in zip(depth, starts)]) + column
+    qcol_ref[...] = by_segment(column, bits)
+    qline_ref[...] = by_segment(lax.broadcasted_iota(jnp.int32, (1, BQ), 1) + q_first, bits)
+    column = lax.broadcasted_iota(jnp.int32, (BK, 1), 0) + k_first
+    kcol_ref[...] = jnp.where(column >= 0, by_segment(column, powers), 0)
+    line = lax.broadcasted_iota(jnp.int32, (1, BK), 1) + k_first
+    kline_ref[0] = jnp.where(line >= 0, by_segment(line, powers), 0)
+
+    def touches(begins, seg, span):
+        return (starts[seg] <= begins + span - 1) & (starts[seg] + size[seg] > begins)
+
+    @pl.when(step == 0)
+    def _():
+        for k in range(key_any.shape[0]):
+            seen = jnp.int32(0)
+            for seg in range(seg_count):
+                seen = jnp.where(touches(begin - early + k * BK, seg, BK), seen | powers[seg], seen)
+            key_any[k] = seen
+
+    query_any, query_all = jnp.int32(0), jnp.int32(-1)
+    for seg in range(seg_count):
+        inside = touches(q_first, seg, BQ)
+        query_any = jnp.where(inside, query_any | bits[seg], query_any)
+        query_all = jnp.where(inside, query_all & bits[seg], query_all)
+    for k in range(key_any.shape[0]):
+        keys_at = begin - early + k * BK
+        some = ((query_any & key_any[k]) != 0) & (keys_at <= q_first + BQ - 1)
+        every = ((key_any[k] & ~query_all) == 0) & (keys_at + BK - 1 <= q_first)
+        flags[step, k] = jnp.where(some, jnp.where(every, 2, 1), 0)
+
+
+def tables(parents, lengths, group_tokens, planes):
+    seg_count = parents.shape[1]
+    early = (planes - 1) * group_tokens
+    steps = group_tokens // BQ
+    blocks = planes * group_tokens // BK
+    i32 = lambda *shape: jax.ShapeDtypeStruct(shape, jnp.int32)
+    smem = pl.BlockSpec(memory_space=pltpu.SMEM)
+    return pl.pallas_call(
+        partial(tables_body, group_tokens, early, seg_count),
+        grid=(steps,),
+        in_specs=[smem, smem],
+        out_specs=[
+            pl.BlockSpec((BQ, 1), lambda i: (i, 0)),
+            pl.BlockSpec((BQ, 1), lambda i: (i, 0)),
+            pl.BlockSpec((1, BQ), lambda i: (0, i)),
+            pl.BlockSpec((1, 1, BK), lambda i: (i, 0, 0)),
+            pl.BlockSpec((BK, 1), lambda i: (i, 0)),
+            smem,
+        ],
+        out_shape=[
+            i32(group_tokens, 1),
+            i32(group_tokens, 1),
+            i32(1, group_tokens),
+            i32(blocks, 1, BK),
+            i32(blocks * BK, 1),
+            i32(steps, blocks),
+        ],
+        scratch_shapes=[pltpu.SMEM((blocks,), jnp.int32)],
+        cost_estimate=QUICK,
+        name="tables",
+    )(parents, lengths)
 
 
 def inner(left, right):
     return dg(left, right, TN)
 
 
-def against(left, right):
-    return dg(left, right, NT)
-
-
 def after(value, *others):
     return lax.optimization_barrier((value,) + others)[0]
-
-
-def by_member(weight, pieces):
-    rows = weight.shape[0]
-    return weight.reshape(rows, pieces, -1).transpose(1, 0, 2)
-
-
-def from_members(pieces):
-    return pieces.transpose(1, 0, 2).reshape(pieces.shape[1], -1)
 
 
 def per_device(
@@ -640,18 +1005,10 @@
     far = [[member + GROUP * plane for plane in range(data_count // GROUP)] for member in range(GROUP)]
     planes = TREE_TOKENS // group_tokens
 
-    pieces_attn = jnp.concatenate(
-        [
-            by_member(query_weight, GROUP),
-            by_member(key_matrix, GROUP),
-            by_member(value_matrix, GROUP),
-            jnp.pad(by_member(headgate_weight, GROUP), ((0, 0), (0, 0), (0, HEAD_SIZE - headgate_weight.shape[1] // GROUP))),
-        ],
-        axis=-1,
-    )
-    pieces_out = by_member(output_weight.T, GROUP)
-    pieces_glu = jnp.concatenate([by_member(gate_weight, GROUP), by_member(up_weight, GROUP)], axis=-1)
-    pieces_down = by_member(down_weight.T, GROUP)
+    gates = headgate_weight.shape[1] // GROUP
+    pieces_gates = jnp.pad(
+        headgate_weight.reshape(rows_here, GROUP, gates), ((0, 0), (0, 0), (0, HEAD_SIZE - gates))
+    ).reshape(rows_here, GROUP * HEAD_SIZE)
 
     def far_gather(mine):
         return lax.all_gather(
@@ -662,7 +1019,7 @@
         mine = lax.psum_scatter(grad, "dp", scatter_dimension=0, tiled=True, axis_index_groups=far)
         return mine.reshape(GROUP, rows_here, -1)
 
-    mine_attn = trade_group(pieces_attn, 3)
+    mine_attn = trade_group([query_weight, key_matrix, value_matrix, pieces_gates], 3)
     full_attn = far_gather(mine_attn)
 
     sizes = [attn_gain.shape[0], mlp_gain.shape[0], query_norm_gain.shape[0], key_gain.shape[0]]
@@ -678,42 +1035,12 @@
         gains[:, cuts[i] : cuts[i + 1]].reshape(-1) for i in range(4)
     ]
     head_gains = jnp.stack([gain_query, gain_key])
-    mine_out = trade_group(after(pieces_out, all_gains), 4)
+    mine_out = trade_group([after(output_weight.T, all_gains)], 4)
     full_out = far_gather(mine_out)
 
-    group_index = lax.axis_index("dp") // GROUP
-    first = group_index * group_tokens
-    tree = first // TREE_TOKENS
-    begin = first - tree * TREE_TOKENS
-    later = begin // group_tokens
-    parent_row = lax.dynamic_index_in_dim(parents, tree, 0, keepdims=False)
-    length_row = lax.dynamic_index_in_dim(lengths, tree, 0, keepdims=False)
-    starts = jnp.cumsum(length_row) - length_row
-    table = ancestors(parent_row, seg_count)
-    depth = jnp.sum(table * length_row[None, :], axis=1) - length_row
-    offsets = begin + jnp.arange(group_tokens, dtype=jnp.int32)
-    onehot = segment_onehot(offsets, starts, seg_count)
-    positions = jnp.sum(onehot * (depth - starts)[None, :], axis=1) + offsets
-    powers = 1 << jnp.arange(seg_count, dtype=jnp.int32)
-    query_bits = jnp.sum(onehot * jnp.sum(table * powers[None, :], axis=1)[None, :], axis=1)
-    key_count = planes * group_tokens
-    key_offsets = begin - (key_count - group_tokens) + jnp.arange(key_count, dtype=jnp.int32)
-    key_hot = segment_onehot(key_offsets, starts, seg_count) * (key_offsets >= 0).astype(jnp.int32)[:, None]
-    key_bits = jnp.sum(key_hot * powers[None, :], axis=1)
-    query_has = jnp.max(onehot.reshape(-1, BQ, seg_count), axis=1)
-    key_has = jnp.max(key_hot.reshape(-1, BK, seg_count), axis=1)
-    early = key_count - group_tokens
-    reached = jnp.dot(jnp.dot(query_has, table), key_has.T) > 0
-    missed = jnp.dot(jnp.dot(query_has, 1 - table), key_has.T) > 0
-    q_first = early + BQ * jnp.arange(query_has.shape[0], dtype=jnp.int32)[:, None]
-    k_first = BK * jnp.arange(key_has.shape[0], dtype=jnp.int32)[None, :]
-    some = reached & (k_first <= q_first + BQ - 1)
-    every = ~missed & (k_first + BK - 1 <= q_first)
-    flags = jnp.where(some, jnp.where(every, 2, 1), 0).astype(jnp.int32)
+    positions, query_column, query_line, key_lines, key_column, flags = tables(parents, lengths, group_tokens, planes)
     cosine, sine = rope_tables(positions, HEAD_SIZE)
-    query_column, query_line = query_bits[:, None], query_bits[None, :]
-    key_lines = key_bits.reshape(-1, 1, BK)
-    key_column = key_bits[:, None]
+    early = (planes - 1) * group_tokens
     key_cut = early // BK
 
     rows = layer_in.astype(f32)
@@ -726,40 +1053,38 @@
     query, pair = prepare(raw, cosine, sine, head_gains)
     ahead = [(s, s + GROUP) for s in range(data_count) if (s // GROUP) % planes == 0]
     back = [(d, s) for s, d in ahead]
-    pair_early = lax.ppermute(pair, "dp", ahead)
-    mine_glu = trade_group(after(pieces_glu, query), 5)
+    mine_glu, pair_early = trade_group([gate_weight, up_weight], 5, pair, planes)
     full_glu = far_gather(mine_glu)
+    query = after(query, mine_glu)
     own = attend(True, flags[:, key_cut:], query, pair, query_column, key_lines[key_cut:])
-    mine_down = trade_group(after(pieces_down, own[0], mine_glu), 6)
+    mine_down = trade_group([after(down_weight.T, own[0])], 6)
     full_down = far_gather(mine_down)
+    grad_tokens = gather_group(after(out_grad, mine_down))
     attn, mixed, lse = attend(
-        False, flags[:, :key_cut], query, pair_early, query_column, key_lines[:key_cut], (own[0], own[1], raw)
+        False, flags[:, :key_cut], after(query, grad_tokens), pair_early, query_column, key_lines[:key_cut], (own[0], own[1], raw)
     )
-    branch = reduce_group(after(against(mixed, full_out).astype(bf), mine_down))
+    branch = product_reduce(mixed, full_out, 2)
     middle = rows + branch
 
     normed_two, norm_two_back = jax.vjp(row_norm, middle, gain_two)
-    h_two = gather_group(normed_two.astype(bf))
-    grad_tokens = gather_group(after(out_grad, h_two))
-    both_glu = jnp.dot(h_two, full_glu, preferred_element_type=f32)
+    h_two, both_glu, hidden = gather_product(normed_two.astype(bf), full_glu, 14, True)
     units = full_down.shape[1]
     gate, up = both_glu[:, :units], both_glu[:, units:]
-    hidden_f, glu_back = jax.vjp(swiglu, gate, up)
-    hidden = hidden_f.astype(bf)
 
     down_part = inner(grad_tokens, hidden).astype(bf)
     down_rows = far_scatter(down_part)
     grad_hidden = jnp.dot(after(grad_tokens, down_part), full_down, preferred_element_type=f32)
-    grad_gate_f, grad_up_f = glu_back(grad_hidden)
-    grad_glu = jnp.concatenate([grad_gate_f.astype(bf), grad_up_f.astype(bf)], axis=1)
+    open_gate = jax.nn.sigmoid(gate)
+    grad_gate = grad_hidden * up * open_gate * (1 + gate * (1 - open_gate))
+    grad_up = grad_hidden * gate * open_gate
+    grad_glu = jnp.concatenate([grad_gate.astype(bf), grad_up.astype(bf)], axis=1)
     glu_part = inner(h_two, grad_glu).astype(bf)
     glu_rows = far_scatter(glu_part)
-    grad_h_two = reduce_group(against(after(grad_glu, glu_part), full_glu).astype(bf))
+    grad_h_two = product_reduce(after(grad_glu, glu_part), full_glu, 15)
     grad_mid_norm, gain_two_grad = norm_two_back(grad_h_two)
     grad_middle = out_grad.astype(f32) + grad_mid_norm
 
-    grad_branch = gather_group(grad_middle.astype(bf))
-    grad_mixed = jnp.dot(grad_branch, full_out, preferred_element_type=f32)
+    grad_branch, grad_mixed = gather_product(grad_middle.astype(bf), full_out, 16)
     out_part = inner(after(grad_branch, grad_mixed), mixed).astype(bf)
     out_rows = far_scatter(out_part)
     grad_attn, grad_logit, delta = gate_back(grad_mixed, attn, raw)
@@ -770,18 +1095,18 @@
     query_grad, own_grad = attend_back(
         True, flags[:, key_cut:], query, grad_attn, pair, query_line, key_column[early:], lse, delta, query_grad
     )
-    down_grad = trade_group(after(down_rows, own_grad), 7)
-    last_branch = reduce_group(after(against(after(hidden, own_grad), full_down).astype(bf), down_grad))
-    layer_out = (middle + last_branch).astype(bf)
-    glu_grad = trade_group(after(glu_rows, last_branch), 8)
+    (down_grad,) = trade_back(after(down_rows, own_grad), [units], 7)
+    gate_grad, up_grad = trade_back(after(glu_rows, down_grad), [units, units], 8)
     grad_raw, head_gain_grads = prepare_back(
-        raw, cosine, sine, head_gains, query_grad, own_grad, after(returned, glu_grad), grad_logit
+        raw, cosine, sine, head_gains, query_grad, own_grad, after(returned, gate_grad), grad_logit
     )
     attn_part = inner(hidden_first, grad_raw).astype(bf)
     attn_rows = far_scatter(attn_part)
-    grad_h_one = reduce_group(against(after(grad_raw, attn_part), full_attn).astype(bf))
+    grad_h_one = product_reduce(after(grad_raw, attn_part), full_attn, 17)
     grad_in_norm, gain_one_grad = norm_one_back(grad_h_one)
     input_grad = (grad_middle + grad_in_norm).astype(bf)
+    last_branch = product_reduce(after(hidden, grad_h_one), full_down, 18)
+    layer_out = (middle + last_branch).astype(bf)
 
     devices = data_count * model_count
     gain_parts = jnp.concatenate(
@@ -792,10 +1117,12 @@
         axis=1,
     )
     gain_parts = gain_parts.reshape((data_count // GROUP, GROUP, model_count) + tile).transpose(2, 1, 0, 3, 4)
-    gain_sums = reduce_all(gain_parts).reshape(-1)
-    out_weight_grad = trade_group(after(out_rows, gain_sums), 9)
-    attn_grad = trade_group(after(attn_rows, out_weight_grad), 10)
-    full = lambda pieces: from_members(pieces).astype(f32)
+    (out_weight_grad,) = trade_back(after(out_rows, last_branch), [q_width], 9)
+    gain_sums = reduce_all(after(gain_parts, out_weight_grad)).reshape(-1)
+    q_grad, k_grad, v_grad, gates_grad = trade_back(
+        after(attn_rows, gain_sums), [q_width, k_width, k_width, HEAD_SIZE], 10
+    )
+    gates_grad = gates_grad.reshape(rows_here, GROUP, HEAD_SIZE)[:, :, :heads].reshape(rows_here, -1)
     return (
         layer_out,
         input_grad,
@@ -803,14 +1130,14 @@
         gain_sums[cuts[1] : cuts[2]],
         gain_sums[cuts[2] : cuts[3]],
         gain_sums[cuts[3] : cuts[4]],
-        full(attn_grad[:, :, :q_width]),
-        full(attn_grad[:, :, q_width : q_width + k_width]),
-        full(attn_grad[:, :, q_width + k_width : q_width + 2 * k_width]),
-        full(attn_grad[:, :, q_width + 2 * k_width : q_width + 2 * k_width + heads]),
-        full(out_weight_grad).T,
-        full(glu_grad[:, :, :units]),
-        full(glu_grad[:, :, units:]),
-        full(down_grad).T,
+        q_grad.astype(f32),
+        k_grad.astype(f32),
+        v_grad.astype(f32),
+        gates_grad.astype(f32),
+        out_weight_grad.astype(f32).T,
+        gate_grad.astype(f32),
+        up_grad.astype(f32),
+        down_grad.astype(f32).T,
     )
 
 

time: 920 us -> 775 us (0.84)
  matrix products: 153 us -> 72.8 us
  local copies, waits for them, and re-layouts: 58.1 us -> 30.7 us
  Pallas kernels: 608 us -> 586 us
  between operations: 27 us -> 15.2 us
  waiting for transfers between devices: 13.3 us -> 23.6 us
    pallas_call x12 -> x15, Pallas kernels: 270 us -> 384 us  [the longest x4 185 us: product_reduce(): pl.pallas_call(reduce_body, out_shape=jax.ShapeDtypeStruct((share, width)...]
    pallas_call x4 -> x2, Pallas kernels: 163 us -> 80.7 us  [gather_group(): pl.pallas_call(gather_body, out_shape=jax.ShapeDtypeStruct((share * GROUP...]
    pallas_call x1, Pallas kernels: 82.1 us -> 27.5 us  [reduce_all(): pl.pallas_call(reduce_all_body, out_shape=jax.ShapeDtypeStruct(tile, x.dt...]
    dot_general x8 -> x4, matrix products: 99.4 us -> 46.9 us  [dg(): return lax.dot_general(left, right, dims, preferred_element_type=f32)]
    dot_general x4 -> x0, matrix products: 25.8 us -> none  [the longest x1 17.7 us: per_device(): both_glu = jnp.dot(h_two, full_glu, preferred_element_type=f32)]
    ppermute x1, waiting for transfers between devices: 0.01 us -> 23.4 us  [per_device(): returned = lax.ppermute(early_grad, 'dp', back)]
    ppermute x1 -> x0, waiting for transfers between devices: 13 us -> none  [per_device(): pair_early = lax.ppermute(pair, 'dp', ahead)]
    unnamed x82 -> x78, local copies, waits for them, and re-layouts: 28 us -> 15.9 us
  transfers between devices with their start and end apart: 10 -> 9, of which waited for: 1 -> 1; matrix products, arithmetic and copies ran while one was open for 25% -> 16% of each run, Pallas kernels for 65% -> 73%
where the time goes in v3:
time: 775 us; the launch traced here: 769 us
  Pallas kernels  586 us (76%)
  matrix products  72.8 us (9%)
  other arithmetic  39.2 us (5%)
  local copies, waits for them, and re-layouts  30.7 us (4%)
  waiting for transfers between devices  23.6 us (3%)
  between operations  15.2 us (2%)
    pallas_call x4, Pallas kernels, product_reduce(): pl.pallas_call(reduce_body, out_shape=jax.ShapeDtypeStruct((share, width)...  185 us
    pallas_call x8, Pallas kernels, trade_call(): pl.pallas_call(partial(trade_body, widths, kv, out_side), out_shape=outs,...  112 us
    pallas_call x2, Pallas kernels, gather_product(): pl.pallas_call(partial(gather_product_body, glu), out_shape=outs, in_spec...  81.5 us
    pallas_call x2, Pallas kernels, gather_group(): pl.pallas_call(gather_body, out_shape=jax.ShapeDtypeStruct((share * GROUP...  80.7 us
    dot_general x4, matrix products, dg(): return lax.dot_general(left, right, dims, preferred_element_type=f32)  46.9 us
    pallas_call x2, Pallas kernels, attend_back(): pl.pallas_call(partial(attend_back_body, causal), grid_spec=pltpu.Prefetc...  31 us
    pallas_call x1, Pallas kernels, reduce_all(): pl.pallas_call(reduce_all_body, out_shape=jax.ShapeDtypeStruct(tile, x.dt...  27.5 us
    pallas_call x2, Pallas kernels, attend(): pl.pallas_call(partial(attend_body, causal, last), grid_spec=pltpu.Prefet...  25.5 us
  transfers between devices with their start and end apart: 9, of which 1 were waited for; matrix products, arithmetic and copies ran while one was open for 16% of the time, Pallas kernels for 73%

profile of v3, /device:TPU:0, one launch (start us, length us, event | category | flops | bytes accessed | tf_op | source)
XLA Modules:
  0.0 769.2 jit_solution(9192622362034640657)
XLA Ops:
  9.0 13.5 %trade_group.8 = bf16[4,128,640]{2,1,0:T(8,128)(2,1)} custom-call(bf16[128,1024]{1,0:T(8,128)(2,1)} %refs_0_.2, bf16[128,512]{1,0:T(8,128)(2,1)} %refs_1_.2, bf16[128,512]{1,0:T(8,128)(2,1)} %refs_2_.1, bf16[128,512]{1,0:T(8,128)(2,1)} %bitcast.59), custom_call_target="tpu_custom_call" | custom-call | bytes 65536 | tf_op jit(solution)/shard_map/trade_group/pallas_call | solution.py:759
  23.3 12.4 %gather_all.1 = f32[2,4,4,8,128]{4,3,2,1,0:T(8,128)} custom-call(f32[8,128]{1,0:T(8,128)} %fusion.18.x_ref), custom_call_target="tpu_custom_call" | custom-call | bytes 65536 | tf_op jit(solution)/shard_map/gather_all/pallas_call | solution.py:818
  47.0 40.3 %gather_group.2 = bf16[2048,2048]{1,0:T(8,128)(2,1)} custom-call(bf16[256,2048]{1,0:T(8,128)(2,1)} %fusion.2.x_ref), custom_call_target="tpu_custom_call" | custom-call | bytes 65536 | tf_op jit(solution)/shard_map/gather_group/pallas_call | solution.py:385
  100.9 11.3 %fusion.33.raw_ref.refs_2_.logit_ref = f32[2048,640]{1,0:T(8,128)} fusion(bf16[2048,2048]{1,0:T(8,128)(2,1)} %gather_group.2, bf16[2048,640]{1,0:T(8,128)(2,1)} %all-gather.5.cloned.1.call-done.right_ref), kind=kOutput, calls=%fused_computation.71 | convolution fusion | flops 5368709120 | bytes 16252928 | tf_op jit(solution)/shard_map/dot_general | solution.py:1049
  120.4 26.4 %trade_group.10 = (bf16[4,128,1536]{2,1,0:T(8,128)(2,1)}, bf16[2048,256]{1,0:T(8,128)(2,1)}) custom-call(bf16[128,3072]{1,0:T(8,128)(2,1)} %refs_0_.3, bf16[128,3072]{1,0:T(8,128)(2,1)} %refs_1_.3, bf16[2048,256]{1,0:T(8,128)(2,1)} %get-tuple-element.74.refs_2_.kv_ref), custom_call_target="tpu_custom_call" | custom-call | bytes 65536 | tf_op jit(solution)/shard_map/trade_group/pallas_call | solution.py:759
  149.3 15.7 %attend_own.1 = (f32[2048,256]{1,0:T(8,128)}, f32[2048,2]{1,0:T(8,128)}) custom-call(s32[8,4]{1,0:T(8,128)} %get-tuple-element.203.flags, bf16[2048,256]{1,0:T(8,128)(2,1)} %get-tuple-element.99.q_ref, bf16[2048,256]{1,0:T(8,128)(2,1)} %get-tuple-element.74.refs_2_.kv_ref, s32[2048,1]{1,0:T(8,128)} %get-tuple-element.77.qbit_ref, ...), custom_call_target="tpu_custom_call" | custom-call | flops 2147483648 | bytes 8388608 | tf_op jit(solution)/shard_map/attend_own/pallas_call | solution.py:117
  165.0 12.3 %trade_group.11 = bf16[4,128,768]{2,1,0:T(8,128)(2,1)} custom-call(bf16[128,3072]{1,0:T(8,128)(2,1)} %bitcast.51), custom_call_target="tpu_custom_call" | custom-call | bytes 65536 | tf_op jit(solution)/shard_map/trade_group/pallas_call | solution.py:759
  177.5 40.3 %gather_group.3 = bf16[2048,2048]{1,0:T(8,128)(2,1)} custom-call(bf16[256,2048]{1,0:T(8,128)(2,1)} %x_ref), custom_call_target="tpu_custom_call" | custom-call | bytes 65536 | tf_op jit(solution)/shard_map/gather_group/pallas_call | solution.py:385
  227.6 43.5 %product_reduce.4 = f32[256,2048]{1,0:T(8,128)} custom-call(bf16[2048,256]{1,0:T(8,128)(2,1)} %get-tuple-element.85.left_ref, bf16[2048,256]{1,0:T(8,128)(2,1)} %all-gather.7.cloned.1.call-done.right_ref.w_ref), custom_call_target="tpu_custom_call" | custom-call | bytes 65536 | tf_op jit(solution)/shard_map/product_reduce/pallas_call | solution.py:500
  273.4 42.6 %gather_product.2 = (bf16[2048,2048]{1,0:T(8,128)(2,1)}, f32[2048,1536]{1,0:T(8,128)}, bf16[2048,768]{1,0:T(8,128)(2,1)S(1)}) custom-call(bf16[256,2048]{1,0:T(8,128)(2,1)S(1)} %multiply_convert_fusion.2.x_ref, bf16[2048,1536]{1,0:T(8,128)(2,1)} %all-gather.9.cloned.1.call-done.w_ref.right_ref), custom_call_target="tpu_custom_call" | custom-call | bytes 65536 | tf_op jit(solution)/shard_map/gather_product/pallas_call | solution.py:652
  317.6 10.5 %convolution_convert_fusion.1 = bf16[2048,768]{1,0:T(8,128)(2,1)} fusion(bf16[2048,2048]{1,0:T(8,128)(2,1)} %gather_group.3, bf16[2048,768]{1,0:T(8,128)(2,1)S(1)} %get-tuple-element.111.left_ref), kind=kOutput, calls=%fused_computation.10 | convolution fusion | flops 6444023808 | bytes 14680064 | tf_op jit(solution)/shard_map/dot_general | solution.py:27
  328.1 14.5 %multiply_convert_fusion.1 = (bf16[2048,768]{1,0:T(8,128)(2,1)S(1)}, bf16[2048,768]{1,0:T(8,128)(2,1)S(1)}) fusion(f32[2048,1536]{1,0:T(8,128)} %get-tuple-element.88, bf16[2048,2048]{1,0:T(8,128)(2,1)} %gather_group.3, bf16[2048,768]{1,0:T(8,128)(2,1)} %all-gather.11.cloned.1.call-done.right_ref), kind=kOutput, calls=%fused_computation.3 | convolution fusion | flops 6462898176 | bytes 30408704 | tf_op jit(solution)/shard_map/dot_general | solution.py:1076
  345.3 18.3 %convolution_convert_fusion = bf16[2048,1536]{1,0:T(8,128)(2,1)} fusion(bf16[2048,2048]{1,0:T(8,128)(2,1)} %get-tuple-element.89, bf16[2048,768]{1,0:T(8,128)(2,1)S(1)} %get-tuple-element.186, bf16[2048,768]{1,0:T(8,128)(2,1)S(1)} %get-tuple-element.185), kind=kOutput, calls=%fused_computation | convolution fusion | flops 12900630528 | bytes 20971520 | tf_op jit(solution)/shard_map/dot_general | solution.py:27
  371.9 49.8 %product_reduce.5 = f32[256,2048]{1,0:T(8,128)} custom-call(bf16[2048,1536]{1,0:T(8,128)(2,1)} %pad_maximum_fusion.left_ref, bf16[2048,1536]{1,0:T(8,128)(2,1)} %all-gather.9.cloned.1.call-done.w_ref.right_ref), custom_call_target="tpu_custom_call" | custom-call | bytes 65536 | tf_op jit(solution)/shard_map/product_reduce/pallas_call | solution.py:500
  425.4 38.9 %gather_product.3 = (bf16[2048,2048]{1,0:T(8,128)(2,1)}, f32[2048,256]{1,0:T(8,128)S(1)}) custom-call(bf16[256,2048]{1,0:T(8,128)(2,1)S(1)} %fusion.25.x_ref, bf16[2048,256]{1,0:T(8,128)(2,1)S(1)} %copy-done), custom_call_target="tpu_custom_call" | custom-call | bytes 65536 | tf_op jit(solution)/shard_map/gather_product/pallas_call | solution.py:652
  488.0 24.8 %attend_own_back.1 = (f32[2048,256]{1,0:T(8,128)}, f32[2048,256]{1,0:T(8,128)}) custom-call(s32[8,4]{1,0:T(8,128)} %get-tuple-element.203.flags, bf16[2048,256]{1,0:T(8,128)(2,1)} %get-tuple-element.99.q_ref, bf16[2048,256]{1,0:T(8,128)(2,1)} %get-tuple-element.93.g_ref, bf16[2048,256]{1,0:T(8,128)(2,1)} %get-tuple-element.74.refs_2_.kv_ref, ...), custom_call_target="tpu_custom_call" | custom-call | flops 5368709120 | bytes 12582912 | tf_op jit(solution)/shard_map/attend_own_back/pallas_call | solution.py:201
  512.7 13.6 %trade_group.12 = bf16[128,3072]{1,0:T(8,128)(2,1)} custom-call(bf16[4,128,768]{2,1,0:T(8,128)(2,1)} %bitcast.57), custom_call_target="tpu_custom_call" | custom-call | bytes 65536 | tf_op jit(solution)/shard_map/trade_group/pallas_call | solution.py:759
  526.4 21.7 %trade_group.13 = (bf16[128,3072]{1,0:T(8,128)(2,1)}, bf16[128,3072]{1,0:T(8,128)(2,1)}) custom-call(bf16[4,128,1536]{2,1,0:T(8,128)(2,1)} %bitcast.53), custom_call_target="tpu_custom_call" | custom-call | bytes 65536 | tf_op jit(solution)/shard_map/trade_group/pallas_call | solution.py:759
  548.1 23.4 %collective-permute-done.back_ref = bf16[2048,256]{1,0:T(8,128)(2,1)S(1)} collective-permute-done((bf16[2048,256]{1,0:T(8,128)(2,1)}, bf16[2048,256]{1,0:T(8,128)(2,1)S(1)}, u32[]{:S(2)}, u32[]{:S(2)}) %collective-permute-start) | collective-permute-done | bytes 1048608 | tf_op jit(solution)/shard_map/ppermute | solution.py:1094
  582.1 11.1 %convolution_convert_fusion.2 = bf16[2048,640]{1,0:T(8,128)(2,1)} fusion(bf16[2048,2048]{1,0:T(8,128)(2,1)} %gather_group.2, bf16[2048,640]{1,0:T(8,128)(2,1)} %get-tuple-element.110.left_ref), kind=kOutput, calls=%fused_computation.11 | convolution fusion | flops 5370019840 | bytes 13631488 | tf_op jit(solution)/shard_map/dot_general | solution.py:27
  600.1 45.7 %product_reduce.6 = f32[256,2048]{1,0:T(8,128)} custom-call(bf16[2048,640]{1,0:T(8,128)(2,1)} %get-tuple-element.110.left_ref, bf16[2048,640]{1,0:T(8,128)(2,1)} %all-gather.5.cloned.1.call-done.right_ref), custom_call_target="tpu_custom_call" | custom-call | bytes 65536 | tf_op jit(solution)/shard_map/product_reduce/pallas_call | solution.py:500
  645.8 45.8 %product_reduce.7 = f32[256,2048]{1,0:T(8,128)} custom-call(bf16[2048,768]{1,0:T(8,128)(2,1)} %copy-done.1, bf16[2048,768]{1,0:T(8,128)(2,1)} %all-gather.11.cloned.1.call-done.right_ref), custom_call_target="tpu_custom_call" | custom-call | bytes 65536 | tf_op jit(solution)/shard_map/product_reduce/pallas_call | solution.py:500
  705.6 27.5 %reduce_all.1 = f32[8,128]{1,0:T(8,128)} custom-call(f32[2,4,4,8,128]{4,3,2,1,0:T(8,128)} %bitcast.65), custom_call_target="tpu_custom_call" | custom-call | bytes 65536 | tf_op jit(solution)/shard_map/reduce_all/pallas_call | solution.py:856
  744.8 10.4 %trade_group.15 = (bf16[128,1024]{1,0:T(8,128)(2,1)}, bf16[128,512]{1,0:T(8,128)(2,1)}, bf16[128,512]{1,0:T(8,128)(2,1)}, bf16[128,512]{1,0:T(8,128)(2,1)}) custom-call(bf16[4,128,640]{2,1,0:T(8,128)(2,1)} %bitcast.58), custom_call_target="tpu_custom_call" | custom-call | bytes 65536 | tf_op jit(solution)/shard_map/trade_group/pallas_call | solution.py:759
  (161 shorter events, 139.7 us)
Async XLA Ops:
  7.2 28.4 %copy-start.17 = (bf16[1024,128]{1,0:T(8,128)(2,1)S(1)}, bf16[1024,128]{1,0:T(8,128)(2,1)}, u32[]{:S(2)}) copy-start(bf16[1024,128]{1,0:T(8,128)(2,1)} %param.28) | copy-start | bytes 786436
  7.2 38.2 %copy-start.5 = (bf16[256,2048]{1,0:T(8,128)(2,1)S(1)}, bf16[256,2048]{1,0:T(8,128)(2,1)}, u32[]{:S(2)}) copy-start(bf16[256,2048]{1,0:T(8,128)(2,1)} %param.16) | copy-start | bytes 3145732
  7.2 93.7 %all-gather.5.cloned.1.call-start = ((), (), s32[]{:S(2)}) async-start(), calls=%async_computation.4 | async-start | bytes 3276800 | tf_op jit(solution)/shard_map/all_gather | solution.py:1014
  22.5 205.1 %all-gather.7.cloned.1.call-start = ((), (), s32[]{:S(2)}) async-start(), calls=%async_computation.5 | async-start | bytes 1310720 | tf_op jit(solution)/shard_map/all_gather | solution.py:1014
  44.2 229.2 %all-gather.9.cloned.1.call-start = ((), (), s32[]{:S(2)}) async-start(), calls=%async_computation.6 | async-start | bytes 7864320 | tf_op jit(solution)/shard_map/all_gather | solution.py:1014
  45.7 41.7 %copy-start.26 = (f32[256]{0:T(256)}, f32[256]{0:T(256)S(1)}, u32[]{:S(2)}) copy-start(f32[256]{0:T(256)S(1)} %fusion.7) | copy-start | bytes 3076
  45.7 652.3 %copy-start.20 = (f32[256]{0:T(256)}, f32[256]{0:T(256)S(1)}, u32[]{:S(2)}) copy-start(f32[256]{0:T(256)S(1)} %fusion.19) | copy-start | bytes 3076
  120.4 27.6 %copy-start.23 = (s32[8,8]{1,0:T(8,128)S(1)}, s32[8,8]{1,0:T(8,128)}, u32[]{:S(2)}) copy-start(s32[8,8]{1,0:T(8,128)} %get-tuple-element.68) | copy-start | bytes 772
  120.4 28.3 %copy-start.22 = (s32[8,1,512]{2,1,0:T(1,128)S(1)}, s32[8,1,512]{2,1,0:T(1,128)}, u32[]{:S(2)}) copy-start(s32[8,1,512]{2,1,0:T(1,128)} %get-tuple-element.78) | copy-start | bytes 49156
  146.8 181.4 %all-gather.11.cloned.1.call-start = ((), (), s32[]{:S(2)}) async-start(), calls=%async_computation.7 | async-start | bytes 3932160 | tf_op jit(solution)/shard_map/all_gather | solution.py:1014
  177.4 335.4 %reduce-scatter.7.cloned.1.call-start = ((), (), s32[]{:S(2)}) async-start(), calls=%async_computation.9 | async-start | bytes 3932160 | tf_op jit(solution)/shard_map/reduce_scatter | solution.py:1019
  273.1 150.9 %copy-start.18 = (f32[256]{0:T(256)}, f32[256]{0:T(256)S(1)}, u32[]{:S(2)}) copy-start(f32[256]{0:T(256)S(1)} %fusion.20) | copy-start | bytes 3076
  328.0 198.3 %reduce-scatter.5.cloned.1.call-start = ((), (), s32[]{:S(2)}) async-start(), calls=%async_computation.8 | async-start | bytes 7864320 | tf_op jit(solution)/shard_map/reduce_scatter | solution.py:1019
  363.6 328.0 %reduce-scatter.9.cloned.1.call-start = ((), (), s32[]{:S(2)}) async-start(), calls=%async_computation.10 | async-start | bytes 1310720 | tf_op jit(solution)/shard_map/reduce_scatter | solution.py:1019
  424.2 41.6 %copy-start.13 = (bf16[2048,256]{1,0:T(8,128)(2,1)S(1)}, bf16[2048,256]{1,0:T(8,128)(2,1)}, u32[]{:S(2)}) copy-start(bf16[2048,256]{1,0:T(8,128)(2,1)} %get-tuple-element.85.left_ref) | copy-start | bytes 3145732
  486.6 84.8 %collective-permute-start = (bf16[2048,256]{1,0:T(8,128)(2,1)}, bf16[2048,256]{1,0:T(8,128)(2,1)S(1)}, u32[]{:S(2)}, u32[]{:S(2)}) collective-permute-start(bf16[2048,256]{1,0:T(8,128)(2,1)} %get-tuple-element.103), channel_id=1, source_target_pairs={{8,0},{10,2},{12,4},{14,6},{24,16},{26,18},{28,20},{30,22},{9,1},{... | collective-permute-start | bytes 3145736 | tf_op jit(solution)/shard_map/ppermute | solution.py:1094
  487.9 256.8 %reduce-scatter.11.cloned.1.call-start = ((), (), s32[]{:S(2)}) async-start(), calls=%async_computation.11 | async-start | bytes 3276800 | tf_op jit(solution)/shard_map/reduce_scatter | solution.py:1019
  645.8 52.3 %copy-start.6 = (bf16[256,2048]{1,0:T(8,128)(2,1)S(1)}, bf16[256,2048]{1,0:T(8,128)(2,1)}, u32[]{:S(2)}) copy-start(bf16[256,2048]{1,0:T(8,128)(2,1)} %param.16) | copy-start | bytes 3145732
  698.1 35.0 %copy-start.12 = (bf16[128,1024]{1,0:T(8,128)(2,1)S(1)}, bf16[128,1024]{1,0:T(8,128)(2,1)}, u32[]{:S(2)}) copy-start(bf16[128,1024]{1,0:T(8,128)(2,1)} %trade_group.14) | copy-start | bytes 786436
  704.9 33.7 %copy-start.27 = (f32[256]{0:T(256)S(1)}, f32[256]{0:T(256)}, u32[]{:S(2)}) copy-start(f32[256]{0:T(256)} %copy-done.26) | copy-start | bytes 3076
  704.9 33.7 %copy-start.29 = (f32[256]{0:T(256)S(1)}, f32[256]{0:T(256)}, u32[]{:S(2)}) copy-start(f32[256]{0:T(256)} %get-tuple-element.180) | copy-start | bytes 3076
  704.9 34.8 %copy-start.19 = (f32[256]{0:T(256)S(1)}, f32[256]{0:T(256)}, u32[]{:S(2)}) copy-start(f32[256]{0:T(256)} %copy-done.18) | copy-start | bytes 3076
  704.9 34.8 %copy-start.21 = (f32[256]{0:T(256)S(1)}, f32[256]{0:T(256)}, u32[]{:S(2)}) copy-start(f32[256]{0:T(256)} %copy-done.20) | copy-start | bytes 3076
  704.9 34.8 %copy-start.25 = (f32[256]{0:T(256)S(1)}, f32[256]{0:T(256)}, u32[]{:S(2)}) copy-start(f32[256]{0:T(256)} %copy-done.24) | copy-start | bytes 3076
  (20 other events, 129.7 us)
Sparse Core Ops, SparseCore 0:
  22.6 55.0 all-gather.4
  79.2 26.7 all-gather.6
  146.9 115.5 all-gather.8
  263.9 61.6 all-gather.10
  328.2 71.9 reduce-scatter.6
  402.3 110.6 reduce-scatter.4
  515.3 55.0 reduce-scatter.8
  593.4 68.0 reduce-scatter.10

commit v4 on v3

--- a/solution.py
+++ b/solution.py
@@ -252,12 +252,14 @@
     def _():
         sums_ref[...] = jnp.zeros_like(sums_ref)
 
+    sent = lax.axis_index("dp") // GROUP % 2 == 0
+    back = jnp.where(sent, back_ref[...].astype(f32), 0.0)
     for i in range(3):
         cols = slice(i * HEAD_SIZE, (i + 1) * HEAD_SIZE)
         if i < 2:
             w = dq_ref[:, cols] * SCORE_SCALE
         else:
-            w = dkv_ref[:, :HEAD_SIZE] + back_ref[:, :HEAD_SIZE].astype(f32)
+            w = dkv_ref[:, :HEAD_SIZE] + back[:, :HEAD_SIZE]
         u = raw_ref[:, cols]
         j = 1 if i == 2 else 0
         r = lax.rsqrt(jnp.mean(u * u, axis=-1, keepdims=True) + EPS)
@@ -265,7 +267,7 @@
         sums_ref[j : j + 1, :] += jnp.sum(w * u * r, axis=0, keepdims=True)
         w = w * gain_ref[j : j + 1, :]
         out_ref[:, cols] = (r * w - u * (r * r * r * jnp.mean(w * u, axis=-1, keepdims=True))).astype(bf)
-    out_ref[:, 3 * HEAD_SIZE : 4 * HEAD_SIZE] = (dkv_ref[:, HEAD_SIZE:] + back_ref[:, HEAD_SIZE:].astype(f32)).astype(bf)
+    out_ref[:, 3 * HEAD_SIZE : 4 * HEAD_SIZE] = (dkv_ref[:, HEAD_SIZE:] + back[:, HEAD_SIZE:]).astype(bf)
     out_ref[:, 4 * HEAD_SIZE :] = dlogit_ref[...]
 
 
@@ -285,13 +287,13 @@
     )(raw, cos, sin, gains, dq, dkv, back, dlogit)
 
 
-def gate_back_body(gm_ref, attn_ref, logit_ref, ga_ref, dlogit_ref, del_ref):
+def gate_back_rows(grad_mixed, attn_ref, logit_ref, ga_ref, dlogit_ref, del_ref):
     lanes = lax.broadcasted_iota(jnp.int32, dlogit_ref.shape, 1)
     grads = jnp.zeros(dlogit_ref.shape, f32)
     for h in range(2):
         cols = slice(h * HEAD_SIZE, (h + 1) * HEAD_SIZE)
         g = jax.nn.sigmoid(logit_ref[:, h : h + 1])
-        gm = gm_ref[:, cols]
+        gm = grad_mixed[:, cols]
         at = attn_ref[:, cols]
         ga = (gm * g).astype(bf)
         ga_ref[:, cols] = ga
@@ -301,22 +303,32 @@
     dlogit_ref[...] = grads.astype(bf)
 
 
-def gate_back(grad_mixed, attn, raw):
-    T, W = attn.shape
-    blk = lambda w, j=0: pl.BlockSpec((BQ, w), lambda i: (i, j))
+def hidden_back_body(dout_ref, down_ref, both_ref, out_ref):
+    units = down_ref.shape[1]
+    chunk = 256
+    for j in range(units // chunk):
+        left = slice(j * chunk, (j + 1) * chunk)
+        right = slice(units + j * chunk, units + (j + 1) * chunk)
+        grad = dg(dout_ref[...], down_ref[:, left], NN)
+        gate = both_ref[:, left]
+        s = jax.nn.sigmoid(gate)
+        out_ref[:, left] = (grad * both_ref[:, right] * s * (1 + gate * (1 - s))).astype(bf)
+        out_ref[:, right] = (grad * (gate * s)).astype(bf)
+
+
+def hidden_back(dout, down, both):
+    T, width = dout.shape
+    units = down.shape[1]
+    blk = lambda w: pl.BlockSpec((2 * BQ, w), lambda i: (i, 0))
     return pl.pallas_call(
-        gate_back_body,
-        grid=(T // BQ,),
-        in_specs=[blk(W), blk(W), blk(HEAD_SIZE, raw.shape[1] // HEAD_SIZE - 1)],
-        out_specs=[blk(W), blk(HEAD_SIZE), pl.BlockSpec((2, BQ), lambda i: (0, i))],
-        out_shape=[
-            jax.ShapeDtypeStruct((T, W), bf),
-            jax.ShapeDtypeStruct((T, HEAD_SIZE), bf),
-            jax.ShapeDtypeStruct((2, T), f32),
-        ],
-        cost_estimate=pl.CostEstimate(flops=T * 3000, bytes_accessed=T * 640 * 8, transcendentals=T),
-        name="gate_back",
-    )(grad_mixed, attn, raw)
+        hidden_back_body,
+        grid=(T // (2 * BQ),),
+        in_specs=[blk(width), pl.BlockSpec((width, units), lambda i: (0, 0)), blk(2 * units)],
+        out_specs=blk(2 * units),
+        out_shape=jax.ShapeDtypeStruct((T, 2 * units), bf),
+        cost_estimate=pl.CostEstimate(flops=2 * T * width * units, bytes_accessed=T * units * 30, transcendentals=T * units),
+        name="hidden_back",
+    )(dout, down, both)
 
 
 GROUP = 4
@@ -393,25 +405,54 @@
         name="gather_group",
     )(x)
 
-def reduce_body(left_ref, right_ref, out_ref, left, right, fars, near, mates, sums, xin, yin, zin, turned, fetch, send, recv):
+def reduce_body(side, back, left_ref, right_ref, *refs):
+    if side:
+        tall_ref, out_ref, grad_ref, tall, grad, refs = *refs[:5], refs[5:]
+    elif back:
+        pair_ref, out_ref, pair_out, refs = *refs[:3], refs[3:]
+    else:
+        out_ref, refs = refs[0], refs[1:]
+    left, right, fars, near, mates, sums, xin, yin, zin, turned, fetch, send, recv = refs
     base, t, tx, ty, td, c = places()
     share = out_ref.shape[0]
     half = share // 2
     chunk = right.shape[0] // 4
     xdev, ydev, mate = (base + tx, c), (base + ty, c), (base + t, 1 - c)
     order = [td, tx, ty, t]
-    lefts, rights = [], []
+    lefts, rights, talls = [], [], []
     for i, who in enumerate(order):
-        for side, core in enumerate((1 - c, c)):
+        for j, core in enumerate((1 - c, c)):
             rows = pl.ds(pl.multiple_of((2 * who + core) * share, share), share)
-            n = 2 * i + side
-            lefts.append(pltpu.make_async_copy(left_ref.at[rows], left.at[n], fetch.at[n]))
+            n = 2 * i + j
+            place = pl.ds(n * share, share)
+            lefts.append(pltpu.make_async_copy(left_ref.at[rows], left.at[place], fetch.at[n]))
+            if side:
+                talls.append(pltpu.make_async_copy(tall_ref.at[rows], tall.at[place], fetch.at[12 + n]))
     for j in range(4):
         rows = pl.ds(j * chunk, chunk)
         rights.append(pltpu.make_async_copy(right_ref.at[rows], right.at[rows], fetch.at[8 + j]))
-    for one in lefts[:2] + rights + lefts[2:]:
+    for one in lefts[:2] + rights + lefts[2:] + talls:
         one.start()
-    greet([xdev, ydev, mate])
+    friends = [xdev, ydev, mate]
+    if back:
+        late = lax.axis_index("dp") // GROUP % 2
+        friends.append((lax.axis_index("dp") + (GROUP - 2 * GROUP * late), c))
+    greet(friends)
+    if back:
+        pair = pltpu.make_async_remote_copy(
+            src_ref=pair_ref,
+            dst_ref=pair_out,
+            send_sem=send.at[10],
+            recv_sem=recv.at[10],
+            device_id=friends[-1],
+            device_id_type=MESH,
+        )
+        keep = pltpu.make_async_copy(pair_ref, pair_out, fetch.at[12])
+
+        @pl.when(late == 1)
+        def _():
+            pair.start()
+            keep.start()
 
     def copy(kind, src, dst, device):
         return pltpu.make_async_remote_copy(
@@ -423,7 +464,7 @@
 
         def go(j, _):
             rows = pl.ds(pl.multiple_of(j * chunk, chunk), chunk)
-            dst[:, rows] = dg(left[n], right[rows, :], NT).astype(dst.dtype)
+            dst[:, rows] = dg(left[n * share : (n + 1) * share, :], right[rows, :], NT).astype(dst.dtype)
             return 0
 
         if n == 0:
@@ -477,6 +518,18 @@
     add(turned.at[1], sums.at[1, B], yin.at[1])
     k[9] = copy(9, turned.at[1], zin.at[1], xdev)
     k[9].start()
+    if side:
+        for one in talls:
+            one.wait()
+
+        def inner_product(j, _):
+            cols = pl.ds(pl.multiple_of(j * 256, 256), 256)
+            grad[cols, :] = dg(tall[:, cols], left[...], TN).astype(bf)
+            return 0
+
+        lax.fori_loop(0, tall.shape[1] // 256, inner_product, 0)
+        put = pltpu.make_async_copy(grad, grad_ref, fetch.at[20])
+        put.start()
     k[6].wait_recv()
     add(out_ref.at[A], sums.at[3, A], xin.at[0])
     k[7].wait_recv()
@@ -489,21 +542,50 @@
         over[i].wait_send()
     for kind in range(4, 10):
         k[kind].wait_send()
-
-
-def product_reduce(left, right, key):
+    if side:
+        put.wait()
+    if back:
+
+        @pl.when(late == 1)
+        def _():
+            pair.wait_send()
+            keep.wait()
+
+        @pl.when(late == 0)
+        def _():
+            pair.wait_recv()
+
+
+def product_reduce(left, right, key, tall=None, pair=None):
     rows, depth = left.shape
+    side = tall is not None
+    back = pair is not None
     width = right.shape[0]
     share = rows // (2 * GROUP)
     half = share // 2
     block = lambda n, r: pltpu.VMEM((n, r, width), bf)
-    return pl.pallas_call(
-        reduce_body,
-        out_shape=jax.ShapeDtypeStruct((share, width), f32),
-        in_specs=[pl.BlockSpec(memory_space=pl.ANY)] * 2,
-        out_specs=pl.BlockSpec(memory_space=pltpu.VMEM),
-        scratch_shapes=[
-            pltpu.VMEM((2 * GROUP, share, depth), bf),
+    anywhere = pl.BlockSpec(memory_space=pl.ANY)
+    outs, out_specs = [jax.ShapeDtypeStruct((share, width), f32)], [pl.BlockSpec(memory_space=pltpu.VMEM)]
+    ins, extra = [left, right], []
+    if side:
+        ins.append(tall)
+        outs.append(jax.ShapeDtypeStruct((tall.shape[1], depth), bf))
+        out_specs.append(anywhere)
+        extra = [pltpu.VMEM(tall.shape, bf), pltpu.VMEM((tall.shape[1], depth), bf)]
+    in_specs = [anywhere] * len(ins)
+    if back:
+        ins.append(pair)
+        in_specs.append(pl.BlockSpec(memory_space=pltpu.VMEM))
+        outs.append(jax.ShapeDtypeStruct(pair.shape, bf))
+        out_specs.append(anywhere)
+    result = pl.pallas_call(
+        partial(reduce_body, side, back),
+        out_shape=outs,
+        in_specs=in_specs,
+        out_specs=out_specs,
+        scratch_shapes=extra
+        + [
+            pltpu.VMEM((rows, depth), bf),
             pltpu.VMEM((width, depth), bf),
             block(4, share),
             block(4, share),
@@ -513,28 +595,35 @@
             block(2, half),
             block(2, half),
             block(2, half),
-            pltpu.SemaphoreType.DMA((12,)),
-            pltpu.SemaphoreType.DMA((10,)),
-            pltpu.SemaphoreType.DMA((10,)),
+            pltpu.SemaphoreType.DMA((21,)),
+            pltpu.SemaphoreType.DMA((11,)),
+            pltpu.SemaphoreType.DMA((11,)),
         ],
-        compiler_params=pltpu.CompilerParams(collective_id=key, has_side_effects=True, vmem_limit_bytes=56 << 20),
+        compiler_params=pltpu.CompilerParams(collective_id=key, has_side_effects=True, vmem_limit_bytes=60 << 20),
         cost_estimate=QUICK,
         name="product_reduce",
-    )(left, right)
-
-
-def gather_product_body(glu, x_ref, w_ref, full_ref, y_ref, *refs):
+    )(*ins)
+    return result if side or back else result[0]
+
+
+def gather_product_body(glu, x_ref, w_ref, *refs):
     if glu:
-        hidden_ref, refs = refs[0], refs[1:]
-        hs, refs = refs[0], refs[1:]
-    buf, w, ys, fetch, put_x, put_y, send, recv = refs
+        full_ref, y_ref, hidden_ref, hs, ys, refs = *refs[:5], refs[5:]
+    else:
+        attn_ref, raw_ref, full_ref, ga_ref, dlogit_ref, del_ref, attn, logit, gs, ds, es, refs = *refs[:11], refs[11:]
+    buf, w, fetch, put_x, put_y, send, recv = refs
     base, t, tx, ty, td, c = places()
     share = x_ref.shape[0]
     half = share // 2
     width = w.shape[1]
     xdev, ydev, mate = (base + tx, c), (base + ty, c), (base + t, 1 - c)
-    weights = pltpu.make_async_copy(w_ref, w, fetch)
-    weights.start()
+    weights = [pltpu.make_async_copy(w_ref, w, fetch.at[0])]
+    if not glu:
+        edge = raw_ref.shape[1] - HEAD_SIZE
+        weights.append(pltpu.make_async_copy(attn_ref, attn, fetch.at[1]))
+        weights.append(pltpu.make_async_copy(raw_ref.at[:, pl.ds(edge, HEAD_SIZE)], logit, fetch.at[2]))
+    for one in weights:
+        one.start()
     greet([xdev, ydev, mate])
 
     def unit(who, core):
@@ -558,7 +647,8 @@
     k[3] = copy(3, mine[1], spot(t, 1), ydev)
     k[0] = copy(0, mine[0], spot(t, 0), xdev)
     k[6] = copy(6, x_ref, buf.at[unit(t, c)], mate)
-    weights.wait()
+    for one in weights:
+        one.wait()
 
     def work(n, src, who, core):
         rows = unit(who, core)
@@ -582,18 +672,20 @@
                 return 0
 
             lax.fori_loop(0, width // 2 // chunk, go, 0)
+            outs = [
+                one,
+                pltpu.make_async_copy(ys.at[slot], y_ref.at[rows], put_y.at[n]),
+                pltpu.make_async_copy(hs.at[slot], hidden_ref.at[rows], put_y.at[8 + n]),
+            ]
         else:
-            chunk = 128 if width % 256 else 256
-
-            def go(j, _):
-                cols = pl.ds(pl.multiple_of(j * chunk, chunk), chunk)
-                ys[slot, :, cols] = dg(src[...], w[:, cols], NN)
-                return 0
-
-            lax.fori_loop(0, width // chunk, go, 0)
-        outs = [one, pltpu.make_async_copy(ys.at[slot], y_ref.at[rows], put_y.at[n])]
-        if glu:
-            outs.append(pltpu.make_async_copy(hs.at[slot], hidden_ref.at[rows], put_y.at[8 + n]))
+            gm = dg(src[...], w[...], NN)
+            gate_back_rows(gm, attn.at[rows], logit.at[rows], gs.at[slot], ds.at[slot], es.at[slot])
+            outs = [
+                one,
+                pltpu.make_async_copy(gs.at[slot], ga_ref.at[rows], put_y.at[n]),
+                pltpu.make_async_copy(ds.at[slot], dlogit_ref.at[rows], put_y.at[8 + n]),
+                pltpu.make_async_copy(es.at[slot], del_ref.at[:, rows], put_y.at[16 + n]),
+            ]
         for out in outs[1:]:
             out.start()
         puts.append(outs)
@@ -639,77 +731,169 @@
                 out.wait()
 
 
-def gather_product(x, w, key, glu=False):
+def gather_product(x, w, key, gated=None):
     share, depth = x.shape
     width = w.shape[1]
     rows = share * GROUP * 2
     anywhere = pl.BlockSpec(memory_space=pl.ANY)
-    outs = [jax.ShapeDtypeStruct((rows, depth), bf), jax.ShapeDtypeStruct((rows, width), f32)]
-    extra = []
-    if glu:
-        outs.append(jax.ShapeDtypeStruct((rows, width // 2), bf))
-        extra = [pltpu.VMEM((2, share, width // 2), bf)]
+    shape = jax.ShapeDtypeStruct
+    if gated is None:
+        gated = []
+        outs = [shape((rows, width), f32), shape((rows, width // 2), bf)]
+        extra = [pltpu.VMEM((2, share, width // 2), bf), pltpu.VMEM((2, share, width), f32)]
+    else:
+        outs = [shape((rows, width), bf), shape((rows, HEAD_SIZE), bf), shape((2, rows), f32)]
+        extra = [
+            pltpu.VMEM((rows, width), f32),
+            pltpu.VMEM((rows, HEAD_SIZE), f32),
+            pltpu.VMEM((2, share, width), bf),
+            pltpu.VMEM((2, share, HEAD_SIZE), bf),
+            pltpu.VMEM((2, 2, share), f32),
+        ]
+    outs = [shape((rows, depth), bf)] + outs
     return pl.pallas_call(
-        partial(gather_product_body, glu),
+        partial(gather_product_body, not gated),
         out_shape=outs,
-        in_specs=[pl.BlockSpec(memory_space=pltpu.VMEM), anywhere],
+        in_specs=[pl.BlockSpec(memory_space=pltpu.VMEM)] + [anywhere] * (1 + len(gated)),
         out_specs=[anywhere] * len(outs),
         scratch_shapes=extra
         + [
             pltpu.VMEM((rows, depth), bf),
             pltpu.VMEM((depth, width), bf),
-            pltpu.VMEM((2, share, width), f32),
-            pltpu.SemaphoreType.DMA,
+            pltpu.SemaphoreType.DMA((3,)),
             pltpu.SemaphoreType.DMA((8,)),
-            pltpu.SemaphoreType.DMA((16,)),
+            pltpu.SemaphoreType.DMA((24,)),
             pltpu.SemaphoreType.DMA((13,)),
             pltpu.SemaphoreType.DMA((13,)),
         ],
         compiler_params=pltpu.CompilerParams(collective_id=key, has_side_effects=True, vmem_limit_bytes=48 << 20),
         cost_estimate=QUICK,
         name="gather_product",
-    )(x, w)
-
-
-def trade_body(widths, kv, out_side, *refs):
-    count = len(widths)
+    )(x, w, *gated)
+
+
+def far_places():
+    dp = lax.axis_index("dp")
+    return dp // GROUP, lax.axis_size("dp") // GROUP
+
+
+def far_friends():
+    base, t, tx, ty, td, c = places()
+    r, count = far_places()
+    return [((r + i) % count * GROUP + t, c) for i in range(1, count)] + [(base + t, 1 - c)]
+
+
+def small_copy(send, recv):
+    def copy(kind, src, dst, device):
+        one = pltpu.make_async_remote_copy(
+            src_ref=src, dst_ref=dst, send_sem=send.at[kind], recv_sem=recv.at[kind], device_id=device, device_id_type=MESH
+        )
+        one.start()
+        return one
+
+    return copy
+
+
+def spread(x_ref, out_ref, send, recv, local):
+    base, t, tx, ty, td, c = places()
+    r, count = far_places()
+    copy = small_copy(send, recv)
+    own = pltpu.make_async_copy(x_ref, out_ref.at[c, t, r], local)
+    own.start()
+    others = [(r + i) % count for i in range(1, count)]
+    stage = [copy(i, x_ref, out_ref.at[c, t, r], (z * GROUP + t, c)) for i, z in enumerate(others)]
+    own.wait()
+    for one in stage:
+        one.wait()
+    stage = [copy(count - 1 + i, out_ref.at[c, t], out_ref.at[c, t], (base + who, c)) for i, who in enumerate([td, tx, ty])]
+    yield
+    for one in stage:
+        one.wait()
+    copy(count + 2, out_ref.at[c], out_ref.at[c], (base + t, 1 - c)).wait()
+    yield
+
+
+def collect(x_ref, out_ref, one_in, one_sum, two_in, two_sum, far_in, send, recv):
+    base, t, tx, ty, td, c = places()
+    r, count = far_places()
+    copy = small_copy(send, recv)
+    copy(0, x_ref.at[1 - c], one_in, (base + t, 1 - c)).wait()
+    one_sum[...] = x_ref[c] + one_in[...]
+    stage = [copy(1 + i, one_sum.at[who], two_in.at[i], (base + who, c)) for i, who in enumerate([td, tx, ty])]
+    yield
+    for one in stage:
+        one.wait()
+    two_sum[...] = one_sum[t] + two_in[0] + two_in[1] + two_in[2]
+    others = [(r + i) % count for i in range(1, count)]
+    stage = [copy(4 + i, two_sum.at[z], far_in.at[i], (z * GROUP + t, c)) for i, z in enumerate(others)]
+    for one in stage:
+        one.wait()
+    total = two_sum[r]
+    for i in range(count - 1):
+        total = total + far_in[i]
+    out_ref[...] = total
+    yield
+
+
+def small_scratch(tile, inward):
+    count = lax.axis_size("dp") // GROUP
+    sems = [pltpu.SemaphoreType.DMA((count + 3,)), pltpu.SemaphoreType.DMA((count + 3,))]
+    if inward:
+        return sems + [pltpu.SemaphoreType.DMA]
+    shapes = [(GROUP, count), (GROUP, count), (3, count), (count,), (count - 1,)]
+    return [pltpu.VMEM(shape + tile, f32) for shape in shapes] + sems
+
+
+def trade_body(inward, widths, sender, side, small, *refs):
     base, t, tx, ty, td, c = places()
     partners = [td, tx, ty]
     friends = [(base + who, c) for who in partners]
-    if kv:
-        ins, refs = refs[: count + 1], refs[count + 1 :]
-        outs, refs = refs[:2], refs[2:]
-        send, recv, local = refs
-        plane = lax.axis_index("dp") // GROUP
-        late = plane % kv
+    flat = [(i, sum(ws[:j]), w) for i, ws in enumerate(widths) for j, w in enumerate(ws)]
+    count = len(flat)
+    packed, loose = len(widths), count
+    ins, refs = refs[: loose if inward else packed], refs[loose if inward else packed :]
+    if sender is not None:
+        pair_ref, refs = refs[0], refs[1:]
+    if side:
+        tall_ref, wide_ref, refs = *refs[:2], refs[2:]
+    if small:
+        small_ref, refs = refs[0], refs[1:]
+    outs, refs = refs[: packed if inward else loose], refs[packed if inward else loose :]
+    if sender is not None:
+        pair_out, refs = refs[0], refs[1:]
+    if side:
+        grad_ref, refs = refs[0], refs[1:]
+    if small:
+        small_out, refs = refs[0], refs[1:]
+    if side:
+        tall, wide, grad, fetch, refs = *refs[:4], refs[4:]
+    send, recv, local, *rest = refs
+    if small:
+        friends += far_friends()
+    if sender is not None:
+        late = lax.axis_index("dp") // GROUP % 2
         friends.append((lax.axis_index("dp") + (GROUP - 2 * GROUP * late), c))
-    elif out_side:
-        ins, outs, (send, recv, local) = refs[:1], refs[1 : 1 + count], refs[1 + count :]
-    else:
-        ins, outs, (send, recv, local) = refs[:count], refs[count : count + 1], refs[count + 1 :]
     greet(friends)
-    starts = [sum(widths[:i]) for i in range(count)]
-
-    def column(who, width):
-        return pl.ds(pl.multiple_of(who * width, width), width)
-
-    def source(i, who):
-        if out_side:
-            return ins[0].at[who, :, pl.ds(starts[i], widths[i])]
-        return ins[i].at[:, column(who, widths[i])]
-
-    def target(i):
-        if out_side:
-            return outs[i].at[:, column(t, widths[i])]
-        return outs[0].at[t, :, pl.ds(starts[i], widths[i])]
-
+
+    def block(ref, i, who):
+        array, start, width = flat[i]
+        return ref[array].at[who, :, pl.ds(start, width)]
+
+    def column(ref, i, who):
+        width = flat[i][2]
+        return ref[i].at[:, pl.ds(pl.multiple_of(who * width, width), width)]
+
+    if small:
+        steps = (spread if inward else collect)(small_ref, small_out, *rest)
+        next(steps)
+    source, target = (column, block) if inward else (block, column)
     copies = []
     for j, who in enumerate(partners):
         for i in range(count):
             kind = j * count + i
             one = pltpu.make_async_remote_copy(
-                src_ref=source(i, who),
-                dst_ref=target(i),
+                src_ref=source(ins, i, who),
+                dst_ref=target(outs, i, t),
                 send_sem=send.at[kind],
                 recv_sem=recv.at[kind],
                 device_id=(base + who, c),
@@ -717,153 +901,113 @@
             )
             one.start()
             copies.append(one)
-    if kv:
+    if sender is not None:
         pair = pltpu.make_async_remote_copy(
-            src_ref=ins[count],
-            dst_ref=outs[1],
+            src_ref=pair_ref,
+            dst_ref=pair_out,
             send_sem=send.at[3 * count],
             recv_sem=recv.at[3 * count],
             device_id=friends[-1],
             device_id_type=MESH,
         )
-        keep = pltpu.make_async_copy(ins[count], outs[1], local.at[count])
-
-        @pl.when(late == 0)
+        keep = pltpu.make_async_copy(pair_ref, pair_out, local.at[count])
+
+        @pl.when(late == sender)
         def _():
             pair.start()
             keep.start()
 
-    owns = [pltpu.make_async_copy(source(i, t), target(i), local.at[i]) for i in range(count)]
+    owns = [pltpu.make_async_copy(source(ins, i, t), target(outs, i, t), local.at[i]) for i in range(count)]
     for own in owns:
         own.start()
+    if side:
+        loads = [pltpu.make_async_copy(tall_ref, tall, fetch.at[0]), pltpu.make_async_copy(wide_ref, wide, fetch.at[1])]
+        for one in loads:
+            one.start()
+        for one in loads:
+            one.wait()
+
+        def inner_product(j, _):
+            cols = pl.ds(pl.multiple_of(j * 256, 256), 256)
+            grad[cols, :] = dg(tall[:, cols], wide[...], TN).astype(bf)
+            return 0
+
+        lax.fori_loop(0, tall.shape[1] // 256, inner_product, 0)
+        put = pltpu.make_async_copy(grad, grad_ref, fetch.at[2])
+        put.start()
+    if small:
+        next(steps)
     for one in copies:
         one.wait()
     for own in owns:
         own.wait()
-    if kv:
-
-        @pl.when(late == 0)
+    if side:
+        put.wait()
+    if sender is not None:
+
+        @pl.when(late == sender)
         def _():
             pair.wait_send()
             keep.wait()
 
-        @pl.when(late == 1)
+        @pl.when(late == 1 - sender)
         def _():
             pair.wait_recv()
 
 
-def trade_call(ins, outs, widths, key, kv, out_side):
+def trade_call(inward, ins, outs, widths, key, pair=None, sender=None, side=(), small=None):
     vmem = pl.BlockSpec(memory_space=pltpu.VMEM)
     anywhere = pl.BlockSpec(memory_space=pl.ANY)
-    kinds = 3 * len(widths) + 1
+    count = sum(len(ws) for ws in widths)
+    scratch = []
+    if sender is not None:
+        ins = list(ins) + [pair]
+        outs = outs + [jax.ShapeDtypeStruct(pair.shape, bf)]
+    if side:
+        tall, wide = side
+        grad = (tall.shape[1], wide.shape[1])
+        outs = outs + [jax.ShapeDtypeStruct(grad, bf)]
+        scratch = [pltpu.VMEM(tall.shape, bf), pltpu.VMEM(wide.shape, bf), pltpu.VMEM(grad, bf), pltpu.SemaphoreType.DMA((3,))]
+    smalls = [] if small is None else [small]
+    out_specs = [anywhere] * len(outs) + [vmem] * len(smalls)
+    rest = []
+    if smalls:
+        tile = small.shape[-2:]
+        result = (2, GROUP, lax.axis_size("dp") // GROUP) + tile if inward else tile
+        outs = outs + [jax.ShapeDtypeStruct(result, f32)]
+        rest = small_scratch(tile, inward)
     return pl.pallas_call(
-        partial(trade_body, widths, kv, out_side),
+        partial(trade_body, inward, widths, sender, bool(side), bool(smalls)),
         out_shape=outs,
-        in_specs=[vmem] * len(ins),
-        out_specs=[anywhere] * len(outs),
-        scratch_shapes=[
-            pltpu.SemaphoreType.DMA((kinds,)),
-            pltpu.SemaphoreType.DMA((kinds,)),
-            pltpu.SemaphoreType.DMA((len(widths) + 1,)),
-        ],
+        in_specs=[vmem] * len(ins) + [anywhere] * len(side) + [vmem] * len(smalls),
+        out_specs=out_specs,
+        scratch_shapes=scratch
+        + [
+            pltpu.SemaphoreType.DMA((3 * count + 1,)),
+            pltpu.SemaphoreType.DMA((3 * count + 1,)),
+            pltpu.SemaphoreType.DMA((count + 1,)),
+        ]
+        + rest,
         compiler_params=pltpu.CompilerParams(collective_id=key, has_side_effects=True),
         cost_estimate=QUICK,
         name="trade_group",
-    )(*ins)
-
-
-def trade_group(weights, key, pair=None, planes=2):
+    )(*ins, *side, *smalls)
+
+
+def trade_group(weights, key, pair=None, small=None):
     rows = weights[0].shape[0]
-    widths = tuple(w.shape[1] // GROUP for w in weights)
-    outs = [jax.ShapeDtypeStruct((GROUP, rows, sum(widths)), bf)]
+    widths = (tuple(w.shape[1] // GROUP for w in weights),)
+    outs = [jax.ShapeDtypeStruct((GROUP, rows, sum(widths[0])), bf)]
     if pair is None:
-        return trade_call(weights, outs, widths, key, 0, False)[0]
-    outs.append(jax.ShapeDtypeStruct(pair.shape, bf))
-    return trade_call(list(weights) + [pair], outs, widths, key, planes, False)
-
-
-def trade_back(grad, widths, key):
-    rows = grad.shape[1]
-    outs = [jax.ShapeDtypeStruct((rows, GROUP * w), bf) for w in widths]
-    return trade_call([grad], outs, tuple(widths), key, 0, True)
-
-
-def far_places():
-    dp = lax.axis_index("dp")
-    return dp // GROUP, lax.axis_size("dp") // GROUP
-
-def gather_all_body(x_ref, out_ref, send, recv, local):
-    base, t, tx, ty, td, c = places()
-    r, count = far_places()
-    mates = [td, tx, ty]
-    others = [(r + i) % count for i in range(1, count)]
-    greet([(z * GROUP + t, c) for z in others] + [(base + who, c) for who in mates] + [(base + t, 1 - c)])
-    def copy(kind, src, dst, device):
-        return pltpu.make_async_remote_copy(src_ref=src, dst_ref=dst, send_sem=send.at[kind], recv_sem=recv.at[kind], device_id=device, device_id_type=MESH)
-    own = pltpu.make_async_copy(x_ref, out_ref.at[c, t, r], local)
-    own.start()
-    stage = [copy(i, x_ref, out_ref.at[c, t, r], (z * GROUP + t, c)) for i, z in enumerate(others)]
-    for one in stage: one.start()
-    own.wait()
-    for one in stage: one.wait()
-    stage = [copy(count - 1 + i, out_ref.at[c, t], out_ref.at[c, t], (base + who, c)) for i, who in enumerate(mates)]
-    for one in stage: one.start()
-    for one in stage: one.wait()
-    last = copy(count + 2, out_ref.at[c], out_ref.at[c], (base + t, 1 - c))
-    last.start()
-    last.wait()
-
-def gather_all(x):
-    count = lax.axis_size("dp") // GROUP
-    return pl.pallas_call(
-        gather_all_body,
-        out_shape=jax.ShapeDtypeStruct((2, GROUP, count) + x.shape, x.dtype),
-        in_specs=[pl.BlockSpec(memory_space=pltpu.VMEM)],
-        out_specs=pl.BlockSpec(memory_space=pltpu.VMEM),
-        scratch_shapes=[pltpu.SemaphoreType.DMA((count + 3,)), pltpu.SemaphoreType.DMA((count + 3,)), pltpu.SemaphoreType.DMA],
-        compiler_params=pltpu.CompilerParams(collective_id=11, has_side_effects=True),
-        cost_estimate=QUICK,
-        name="gather_all",
-    )(x)
-
-def reduce_all_body(x_ref, out_ref, one_in, one_sum, two_in, two_sum, far_in, send, recv):
-    base, t, tx, ty, td, c = places()
-    r, count = far_places()
-    mates = [td, tx, ty]
-    others = [(r + i) % count for i in range(1, count)]
-    greet([(z * GROUP + t, c) for z in others] + [(base + who, c) for who in mates] + [(base + t, 1 - c)])
-    def copy(kind, src, dst, device):
-        return pltpu.make_async_remote_copy(src_ref=src, dst_ref=dst, send_sem=send.at[kind], recv_sem=recv.at[kind], device_id=device, device_id_type=MESH)
-    first = copy(0, x_ref.at[1 - c], one_in, (base + t, 1 - c))
-    first.start()
-    first.wait()
-    one_sum[...] = x_ref[c] + one_in[...]
-    stage = [copy(1 + i, one_sum.at[who], two_in.at[i], (base + who, c)) for i, who in enumerate(mates)]
-    for one in stage: one.start()
-    for one in stage: one.wait()
-    two_sum[...] = one_sum[t] + two_in[0] + two_in[1] + two_in[2]
-    stage = [copy(4 + i, two_sum.at[z], far_in.at[i], (z * GROUP + t, c)) for i, z in enumerate(others)]
-    for one in stage: one.start()
-    for one in stage: one.wait()
-    total = two_sum[r]
-    for i in range(count - 1):
-        total = total + far_in[i]
-    out_ref[...] = total
-
-def reduce_all(x):
-    tile = x.shape[3:]
-    count = lax.axis_size("dp") // GROUP
-    return pl.pallas_call(
-        reduce_all_body,
-        out_shape=jax.ShapeDtypeStruct(tile, x.dtype),
-        in_specs=[pl.BlockSpec(memory_space=pltpu.VMEM)],
-        out_specs=pl.BlockSpec(memory_space=pltpu.VMEM),
-        scratch_shapes=[pltpu.VMEM((GROUP, count) + tile, f32), pltpu.VMEM((GROUP, count) + tile, f32), pltpu.VMEM((3, count) + tile, f32), pltpu.VMEM((count,) + tile, f32), pltpu.VMEM((count - 1,) + tile, f32),
-            pltpu.SemaphoreType.DMA((count + 3,)), pltpu.SemaphoreType.DMA((count + 3,))],
-        compiler_params=pltpu.CompilerParams(collective_id=12, has_side_effects=True),
-        cost_estimate=QUICK,
-        name="reduce_all",
-    )(x)
+        result = trade_call(True, weights, outs, widths, key, small=small)
+        return result[0] if small is None else result
+    return trade_call(True, weights, outs, widths, key, pair, 0)
+
+
+def trade_back(grads, widths, key, pair=None, side=(), small=None):
+    rows = grads[0].shape[1]
+    outs = [jax.ShapeDtypeStruct((rows, GROUP * w), bf) for ws in widths for w in ws]
+    return trade_call(False, grads, outs, widths, key, pair, None if pair is None else 1, side, small)
 
 
 def row_norm(values, gain):
@@ -1019,9 +1163,6 @@
         mine = lax.psum_scatter(grad, "dp", scatter_dimension=0, tiled=True, axis_index_groups=far)
         return mine.reshape(GROUP, rows_here, -1)
 
-    mine_attn = trade_group([query_weight, key_matrix, value_matrix, pieces_gates], 3)
-    full_attn = far_gather(mine_attn)
-
     sizes = [attn_gain.shape[0], mlp_gain.shape[0], query_norm_gain.shape[0], key_gain.shape[0]]
     cuts = [sum(sizes[:i]) for i in range(5)]
     tile = (8, 128)
@@ -1029,7 +1170,8 @@
     gain_tile = jnp.pad(
         jnp.concatenate([attn_gain, mlp_gain, query_norm_gain, key_gain]).astype(f32), (0, spare)
     ).reshape(tile)
-    all_gains = gather_all(after(gain_tile, mine_attn))
+    mine_attn, all_gains = trade_group([query_weight, key_matrix, value_matrix, pieces_gates], 3, small=gain_tile)
+    full_attn = far_gather(mine_attn)
     gains = all_gains.transpose(2, 1, 0, 3, 4).reshape(data_count * model_count, -1)
     gain_one, gain_two, gain_query, gain_key = [
         gains[:, cuts[i] : cuts[i + 1]].reshape(-1) for i in range(4)
@@ -1051,9 +1193,7 @@
     k_width = key_matrix.shape[1] // GROUP
     heads = q_width // HEAD_SIZE
     query, pair = prepare(raw, cosine, sine, head_gains)
-    ahead = [(s, s + GROUP) for s in range(data_count) if (s // GROUP) % planes == 0]
-    back = [(d, s) for s, d in ahead]
-    mine_glu, pair_early = trade_group([gate_weight, up_weight], 5, pair, planes)
+    mine_glu, pair_early = trade_group([gate_weight, up_weight], 5, pair)
     full_glu = far_gather(mine_glu)
     query = after(query, mine_glu)
     own = attend(True, flags[:, key_cut:], query, pair, query_column, key_lines[key_cut:])
@@ -1067,46 +1207,33 @@
     middle = rows + branch
 
     normed_two, norm_two_back = jax.vjp(row_norm, middle, gain_two)
-    h_two, both_glu, hidden = gather_product(normed_two.astype(bf), full_glu, 14, True)
+    h_two, both_glu, hidden = gather_product(normed_two.astype(bf), full_glu, 14)
     units = full_down.shape[1]
-    gate, up = both_glu[:, :units], both_glu[:, units:]
-
-    down_part = inner(grad_tokens, hidden).astype(bf)
+
+    grad_glu = hidden_back(grad_tokens, full_down, both_glu)
+    down_part = inner(after(grad_tokens, grad_glu), hidden).astype(bf)
     down_rows = far_scatter(down_part)
-    grad_hidden = jnp.dot(after(grad_tokens, down_part), full_down, preferred_element_type=f32)
-    open_gate = jax.nn.sigmoid(gate)
-    grad_gate = grad_hidden * up * open_gate * (1 + gate * (1 - open_gate))
-    grad_up = grad_hidden * gate * open_gate
-    grad_glu = jnp.concatenate([grad_gate.astype(bf), grad_up.astype(bf)], axis=1)
-    glu_part = inner(h_two, grad_glu).astype(bf)
+    grad_h_two, glu_part = product_reduce(after(grad_glu, down_part), full_glu, 15, h_two)
     glu_rows = far_scatter(glu_part)
-    grad_h_two = product_reduce(after(grad_glu, glu_part), full_glu, 15)
     grad_mid_norm, gain_two_grad = norm_two_back(grad_h_two)
     grad_middle = out_grad.astype(f32) + grad_mid_norm
 
-    grad_branch, grad_mixed = gather_product(grad_middle.astype(bf), full_out, 16)
-    out_part = inner(after(grad_branch, grad_mixed), mixed).astype(bf)
-    out_rows = far_scatter(out_part)
-    grad_attn, grad_logit, delta = gate_back(grad_mixed, attn, raw)
+    grad_branch, grad_attn, grad_logit, delta = gather_product(grad_middle.astype(bf), full_out, 16, [attn, raw])
     query_grad, early_grad = attend_back(
-        False, flags[:, :key_cut], after(query, out_part), grad_attn, pair_early, query_line, key_column[:early], lse, delta
+        False, flags[:, :key_cut], query, grad_attn, pair_early, query_line, key_column[:early], lse, delta
     )
-    returned = lax.ppermute(early_grad, "dp", back)
     query_grad, own_grad = attend_back(
         True, flags[:, key_cut:], query, grad_attn, pair, query_line, key_column[early:], lse, delta, query_grad
     )
-    (down_grad,) = trade_back(after(down_rows, own_grad), [units], 7)
-    gate_grad, up_grad = trade_back(after(glu_rows, down_grad), [units, units], 8)
-    grad_raw, head_gain_grads = prepare_back(
-        raw, cosine, sine, head_gains, query_grad, own_grad, after(returned, gate_grad), grad_logit
-    )
-    attn_part = inner(hidden_first, grad_raw).astype(bf)
+    down_grad, out_part = trade_back([after(down_rows, own_grad)], ((units,),), 7, side=(grad_branch, mixed))
+    out_rows = far_scatter(out_part)
+    last_branch, returned = product_reduce(after(hidden, out_part), full_down, 18, pair=early_grad)
+    layer_out = (middle + last_branch).astype(bf)
+    grad_raw, head_gain_grads = prepare_back(raw, cosine, sine, head_gains, query_grad, own_grad, returned, grad_logit)
+    grad_h_one, attn_part = product_reduce(grad_raw, full_attn, 17, hidden_first)
     attn_rows = far_scatter(attn_part)
-    grad_h_one = product_reduce(after(grad_raw, attn_part), full_attn, 17)
     grad_in_norm, gain_one_grad = norm_one_back(grad_h_one)
     input_grad = (grad_middle + grad_in_norm).astype(bf)
-    last_branch = product_reduce(after(hidden, grad_h_one), full_down, 18)
-    layer_out = (middle + last_branch).astype(bf)
 
     devices = data_count * model_count
     gain_parts = jnp.concatenate(
@@ -1117,10 +1244,12 @@
         axis=1,
     )
     gain_parts = gain_parts.reshape((data_count // GROUP, GROUP, model_count) + tile).transpose(2, 1, 0, 3, 4)
-    (out_weight_grad,) = trade_back(after(out_rows, last_branch), [q_width], 9)
-    gain_sums = reduce_all(after(gain_parts, out_weight_grad)).reshape(-1)
+    gate_grad, up_grad, out_weight_grad, gain_sums = trade_back(
+        [after(glu_rows, grad_h_one), out_rows], ((units, units), (q_width,)), 8, small=gain_parts
+    )
+    gain_sums = gain_sums.reshape(-1)
     q_grad, k_grad, v_grad, gates_grad = trade_back(
-        after(attn_rows, gain_sums), [q_width, k_width, k_width, HEAD_SIZE], 10
+        [after(attn_rows, gain_sums)], ((q_width, k_width, k_width, HEAD_SIZE),), 10
     )
     gates_grad = gates_grad.reshape(rows_here, GROUP, HEAD_SIZE)[:, :, :heads].reshape(rows_here, -1)
     return (

time: 775 us -> 703 us (0.907)
  matrix products: 72.8 us -> 21.9 us
  waiting for transfers between devices: 23.6 us -> 9.97 us
    dot_general x4 -> x1, matrix products: 46.9 us -> 10.6 us  [dg(): return lax.dot_general(left, right, dims, preferred_element_type=f32)]
    ppermute x1 -> x0, waiting for transfers between devices: 23.4 us -> none  [per_device(): returned = lax.ppermute(early_grad, 'dp', back)]
    dot_general x1 -> x0, matrix products: 14.5 us -> none  [per_device(): jnp.dot(after(grad_tokens, down_part), full_down, preferred_element_type=...]
    pallas_call x17 -> x14, Pallas kernels: 426 us -> 431 us  [the longest x4 197 us: product_reduce(): pl.pallas_call(partial(reduce_body, side, back), out_shape=outs, in_specs...]
    unnamed x78 -> x56, local copies, waits for them, and re-layouts: 15.9 us -> 15.2 us
  transfers between devices with their start and end apart: 9 -> 8, of which waited for: 1 -> 2; matrix products, arithmetic and copies ran while one was open for 16% -> 7% of each run, Pallas kernels for 73% -> 78%
where the time goes in v4:
time: 703 us; the launch traced here: 694 us
  Pallas kernels  589 us (84%)
  other arithmetic  31.8 us (5%)
  local copies, waits for them, and re-layouts  25 us (4%)
  matrix products  21.9 us (3%)
  between operations  15 us (2%)
  waiting for transfers between devices  9.97 us (1%)
    pallas_call x4, Pallas kernels, product_reduce(): pl.pallas_call(partial(reduce_body, side, back), out_shape=outs, in_specs...  197 us
    pallas_call x7, Pallas kernels, trade_call(): pl.pallas_call(partial(trade_body, inward, widths, sender, bool(side), bo...  136 us
    pallas_call x2, Pallas kernels, gather_product(): pl.pallas_call(partial(gather_product_body, not gated), out_shape=outs, i...  82.9 us
    pallas_call x2, Pallas kernels, gather_group(): pl.pallas_call(gather_body, out_shape=jax.ShapeDtypeStruct((share * GROUP...  80.5 us
    pallas_call x2, Pallas kernels, attend_back(): pl.pallas_call(partial(attend_back_body, causal), grid_spec=pltpu.Prefetc...  30.2 us
    pallas_call x2, Pallas kernels, attend(): pl.pallas_call(partial(attend_body, causal, last), grid_spec=pltpu.Prefet...  24.3 us
    unnamed x56, local copies, waits for them, and re-layouts  15.2 us
    pallas_call x1, Pallas kernels, hidden_back(): pl.pallas_call(hidden_back_body, grid=(T // (2 * BQ),), in_specs=[blk(wid...  14.4 us
  transfers between devices with their start and end apart: 8, of which 2 were waited for; matrix products, arithmetic and copies ran while one was open for 7% of the time, Pallas kernels for 78%

profile of v4, /device:TPU:0, one launch (start us, length us, event | category | flops | bytes accessed | tf_op | source)
XLA Modules:
  0.0 693.8 jit_solution(13805543728090393914)
XLA Ops:
  10.3 19.2 %trade_group.7 = (bf16[4,128,640]{2,1,0:T(8,128)(2,1)}, f32[2,4,4,8,128]{4,3,2,1,0:T(8,128)}) custom-call(bf16[128,1024]{1,0:T(8,128)(2,1)} %refs_0_.2, bf16[128,512]{1,0:T(8,128)(2,1)} %refs_1_.2, bf16[128,512]{1,0:T(8,128)(2,1)} %refs_2_.1, bf16[128,512]{1,0:T(8,128)(2,1)} %bitcast.52, f32[8,128]{1,0:T(8,128)} %fusion.18.refs_4_), custom_call_target="tpu_custom_call" | custom-call | bytes 65536 | tf_op jit(solution)/shard_map/trade_group/pallas_call | solution.py:979
  30.5 7.4 %trade_group.8 = bf16[4,128,256]{2,1,0:T(8,128)(2,1)} custom-call(bf16[128,1024]{1,0:T(8,128)(2,1)} %bitcast.48), custom_call_target="tpu_custom_call" | custom-call | bytes 65536 | tf_op jit(solution)/shard_map/trade_group/pallas_call | solution.py:979
  40.7 40.3 %gather_group.2.refs_0_ = bf16[2048,2048]{1,0:T(8,128)(2,1)} custom-call(bf16[256,2048]{1,0:T(8,128)(2,1)} %fusion.2.x_ref), custom_call_target="tpu_custom_call" | custom-call | bytes 65536 | tf_op jit(solution)/shard_map/gather_group/pallas_call | solution.py:397
  94.6 11.3 %fusion.33.raw_ref.refs_2_.refs_1_ = f32[2048,640]{1,0:T(8,128)} fusion(bf16[2048,2048]{1,0:T(8,128)(2,1)} %gather_group.2.refs_0_, bf16[2048,640]{1,0:T(8,128)(2,1)} %all-gather.5.cloned.1.call-done.right_ref), kind=kOutput, calls=%fused_computation.64 | convolution fusion | flops 5368709120 | bytes 16252928 | tf_op jit(solution)/shard_map/dot_general | solution.py:1191
  106.0 8.1 %prepare_heads.1 = (bf16[2048,256]{1,0:T(8,128)(2,1)}, bf16[2048,256]{1,0:T(8,128)(2,1)}) custom-call(f32[2048,640]{1,0:T(8,128)} %fusion.33.raw_ref.refs_2_.refs_1_, f32[2048,128]{1,0:T(8,128)} %get-tuple-element.205.cos_ref, f32[2048,128]{1,0:T(8,128)} %get-tuple-element.204.sin_ref, f32[2,128]{1,0:T(2,128)} %pad_maximum_fusion.gain_ref), custom_call_target="tpu_custom_call" | custom-call | flops 8192000 | bytes 10485760 | tf_op jit(solution)/shard_map/prepare_heads/pallas_call | solution.py:239
  114.0 26.4 %trade_group.9 = (bf16[4,128,1536]{2,1,0:T(8,128)(2,1)}, bf16[2048,256]{1,0:T(8,128)(2,1)}) custom-call(bf16[128,3072]{1,0:T(8,128)(2,1)} %refs_0_.3, bf16[128,3072]{1,0:T(8,128)(2,1)} %refs_1_.3, bf16[2048,256]{1,0:T(8,128)(2,1)} %get-tuple-element.79.refs_2_.kv_ref), custom_call_target="tpu_custom_call" | custom-call | bytes 65536 | tf_op jit(solution)/shard_map/trade_group/pallas_call | solution.py:979
  143.0 14.8 %attend_own.1 = (f32[2048,256]{1,0:T(8,128)}, f32[2048,2]{1,0:T(8,128)}) custom-call(s32[8,4]{1,0:T(8,128)} %get-tuple-element.210.flags, bf16[2048,256]{1,0:T(8,128)(2,1)} %get-tuple-element.87.q_ref, bf16[2048,256]{1,0:T(8,128)(2,1)} %get-tuple-element.79.refs_2_.kv_ref, s32[2048,1]{1,0:T(8,128)} %get-tuple-element.82.qbit_ref, ...), custom_call_target="tpu_custom_call" | custom-call | flops 2147483648 | bytes 8388608 | tf_op jit(solution)/shard_map/attend_own/pallas_call | solution.py:117
  157.8 12.4 %trade_group.10 = bf16[4,128,768]{2,1,0:T(8,128)(2,1)} custom-call(bf16[128,3072]{1,0:T(8,128)(2,1)} %bitcast.44), custom_call_target="tpu_custom_call" | custom-call | bytes 65536 | tf_op jit(solution)/shard_map/trade_group/pallas_call | solution.py:979
  170.8 40.3 %gather_group.3.dout_ref = bf16[2048,2048]{1,0:T(8,128)(2,1)} custom-call(bf16[256,2048]{1,0:T(8,128)(2,1)} %x_ref), custom_call_target="tpu_custom_call" | custom-call | bytes 65536 | tf_op jit(solution)/shard_map/gather_group/pallas_call | solution.py:397
  211.1 9.5 %attend_earlier.1 = (f32[2048,256]{1,0:T(8,128)}, bf16[2048,256]{1,0:T(8,128)(2,1)}, f32[2,2048]{1,0:T(2,128)}) custom-call(s32[8,4]{1,0:T(8,128)} %get-tuple-element.211.flags, bf16[2048,256]{1,0:T(8,128)(2,1)} %get-tuple-element.87.q_ref, bf16[2048,256]{1,0:T(8,128)(2,1)} %get-tuple-element.88.kv_ref, s32[2048,1]{1,0:T(8,128)} %get-tuple-element.82.qbit_ref, ...), custom_call_target="tpu_custom_call" | custom-call | flops 4294967296 | bytes 8388608 | tf_op jit(solution)/shard_map/attend_earlier/pallas_call | solution.py:117
  220.6 43.6 %product_reduce.4 = f32[256,2048]{1,0:T(8,128)} custom-call(bf16[2048,256]{1,0:T(8,128)(2,1)} %get-tuple-element.90.left_ref.refs_2_, bf16[2048,256]{1,0:T(8,128)(2,1)} %all-gather.7.cloned.1.call-done.right_ref.w_ref), custom_call_target="tpu_custom_call" | custom-call | bytes 65536 | tf_op jit(solution)/shard_map/product_reduce/pallas_call | solution.py:581
  268.0 42.5 %gather_product.2 = (bf16[2048,2048]{1,0:T(8,128)(2,1)}, f32[2048,1536]{1,0:T(8,128)}, bf16[2048,768]{1,0:T(8,128)(2,1)S(1)}) custom-call(bf16[256,2048]{1,0:T(8,128)(2,1)S(1)} %multiply_convert_fusion.x_ref, bf16[2048,1536]{1,0:T(8,128)(2,1)} %all-gather.9.cloned.1.call-done.w_ref.right_ref), custom_call_target="tpu_custom_call" | custom-call | bytes 65536 | tf_op jit(solution)/shard_map/gather_product/pallas_call | solution.py:754
  312.1 7.1 %all-gather.11.cloned.1.call-done.down_ref.right_ref = bf16[2048,768]{1,0:T(8,128)(2,1)} async-done(((bf16[512,768]{1,0:T(8,128)(2,1)}), bf16[2048,768]{1,0:T(8,128)(2,1)}) %all-gather.11.cloned.1.call-update) | async-done | bytes 3145744 | tf_op jit(solution)/shard_map/all_gather | solution.py:1158
  319.2 14.4 %hidden_back.1.left_ref = bf16[2048,1536]{1,0:T(8,128)(2,1)} custom-call(bf16[2048,2048]{1,0:T(8,128)(2,1)} %gather_group.3.dout_ref, bf16[2048,768]{1,0:T(8,128)(2,1)} %all-gather.11.cloned.1.call-done.down_ref.right_ref, f32[2048,1536]{1,0:T(8,128)} %get-tuple-element.92.both_ref), custom_call_target="tpu_custom_call" | custom-call | flops 6442450944 | bytes 47185920 | tf_op jit(solution)/shard_map/hidden_back/pallas_call | solution.py:323
  333.6 10.6 %convolution_convert_fusion = bf16[2048,768]{1,0:T(8,128)(2,1)} fusion(bf16[2048,2048]{1,0:T(8,128)(2,1)} %gather_group.3.dout_ref, bf16[2048,768]{1,0:T(8,128)(2,1)S(1)} %copy-done.2), kind=kOutput, calls=%fused_computation.5 | convolution fusion | flops 6444023808 | bytes 14680064 | tf_op jit(solution)/shard_map/dot_general | solution.py:27
  344.3 49.6 %product_reduce.5 = (f32[256,2048]{1,0:T(8,128)}, bf16[2048,1536]{1,0:T(8,128)(2,1)}) custom-call(bf16[2048,1536]{1,0:T(8,128)(2,1)} %hidden_back.1.left_ref, bf16[2048,1536]{1,0:T(8,128)(2,1)} %all-gather.9.cloned.1.call-done.w_ref.right_ref, bf16[2048,2048]{1,0:T(8,128)(2,1)} %get-tuple-element.95.refs_0_), custom_call_target="tpu_custom_call" | custom-call | bytes 65536 | tf_op jit(solution)/shard_map/product_reduce/pallas_call | solution.py:581
  400.3 40.3 %gather_product.3 = (bf16[2048,2048]{1,0:T(8,128)(2,1)}, bf16[2048,256]{1,0:T(8,128)(2,1)S(1)}, bf16[2048,128]{1,0:T(8,128)(2,1)S(1)}, f32[2,2048]{1,0:T(2,128)S(1)}) custom-call(bf16[256,2048]{1,0:T(8,128)(2,1)S(1)} %fusion.25.x_ref, bf16[2048,256]{1,0:T(8,128)(2,1)S(1)} %copy-done, f32[2048,256]{1,0:T(8,128)S(1)} %copy-done.3, ...), custom_call_target="tpu_custom_call" | custom-call | bytes 65536 | tf_op jit(solution)/shard_map/gather_product/pallas_call | solution.py:754
  449.2 24.0 %attend_own_back.1 = (f32[2048,256]{1,0:T(8,128)}, f32[2048,256]{1,0:T(8,128)}) custom-call(s32[8,4]{1,0:T(8,128)} %get-tuple-element.210.flags, bf16[2048,256]{1,0:T(8,128)(2,1)} %get-tuple-element.87.q_ref, bf16[2048,256]{1,0:T(8,128)(2,1)} %copy-done.5, bf16[2048,256]{1,0:T(8,128)(2,1)} %get-tuple-element.79.refs_2_.kv_ref, ...), custom_call_target="tpu_custom_call" | custom-call | flops 5368709120 | bytes 12582912 | tf_op jit(solution)/shard_map/attend_own_back/pallas_call | solution.py:201
  473.3 13.2 %trade_group.11 = (bf16[128,3072]{1,0:T(8,128)(2,1)}, bf16[2048,256]{1,0:T(8,128)(2,1)}) custom-call(bf16[4,128,768]{2,1,0:T(8,128)(2,1)} %bitcast.49, bf16[2048,2048]{1,0:T(8,128)(2,1)} %get-tuple-element.106.refs_1_, bf16[2048,256]{1,0:T(8,128)(2,1)} %get-tuple-element.90.left_ref.refs_2_), custom_call_target="tpu_custom_call" | custom-call | bytes 65536 | tf_op jit(solution)/shard_map/trade_group/pallas_call | solution.py:979
  486.6 58.0 %product_reduce.6 = (f32[256,2048]{1,0:T(8,128)}, bf16[2048,256]{1,0:T(8,128)(2,1)}) custom-call(bf16[2048,768]{1,0:T(8,128)(2,1)} %copy-done.1, bf16[2048,768]{1,0:T(8,128)(2,1)} %all-gather.11.cloned.1.call-done.down_ref.right_ref, bf16[2048,256]{1,0:T(8,128)(2,1)} %get-tuple-element.109.refs_0_), custom_call_target="tpu_custom_call" | custom-call | bytes 65536 | tf_op jit(solution)/shard_map/product_reduce/pallas_call | solution.py:581
  544.6 9.8 %prepare_heads_back.1 = (bf16[2048,640]{1,0:T(8,128)(2,1)}, f32[2,128]{1,0:T(2,128)}) custom-call(f32[2048,640]{1,0:T(8,128)} %fusion.33.raw_ref.refs_2_.refs_1_, f32[2048,128]{1,0:T(8,128)} %get-tuple-element.205.cos_ref, f32[2048,128]{1,0:T(8,128)} %get-tuple-element.204.sin_ref, f32[2,128]{1,0:T(2,128)} %pad_maximum_fusion.gain_ref, ...), custom_call_target="tpu_custom_call" | custom-call | flops 16384000 | bytes 13107200 | tf_op jit(solution)/shard_map/prepare_heads_back/pallas_call | solution.py:279
  554.4 46.0 %product_reduce.7 = (f32[256,2048]{1,0:T(8,128)}, bf16[2048,640]{1,0:T(8,128)(2,1)}) custom-call(bf16[2048,640]{1,0:T(8,128)(2,1)} %get-tuple-element.114.left_ref, bf16[2048,640]{1,0:T(8,128)(2,1)} %all-gather.5.cloned.1.call-done.right_ref, bf16[2048,2048]{1,0:T(8,128)(2,1)} %gather_group.2.refs_0_), custom_call_target="tpu_custom_call" | custom-call | bytes 65536 | tf_op jit(solution)/shard_map/product_reduce/pallas_call | solution.py:581
  616.1 46.1 %trade_group.12 = (bf16[128,3072]{1,0:T(8,128)(2,1)}, bf16[128,3072]{1,0:T(8,128)(2,1)}, bf16[128,1024]{1,0:T(8,128)(2,1)}, f32[8,128]{1,0:T(8,128)}) custom-call(bf16[4,128,1536]{2,1,0:T(8,128)(2,1)} %bitcast.46, bf16[4,128,256]{2,1,0:T(8,128)(2,1)} %bitcast.61, f32[2,4,4,8,128]{4,3,2,1,0:T(8,128)} %bitcast.58), custom_call_target="tpu_custom_call" | custom-call | bytes 65536 | tf_op jit(solution)/shard_map/trade_group/pallas_call | solution.py:979
  669.9 11.5 %trade_group.13 = (bf16[128,1024]{1,0:T(8,128)(2,1)}, bf16[128,512]{1,0:T(8,128)(2,1)}, bf16[128,512]{1,0:T(8,128)(2,1)}, bf16[128,512]{1,0:T(8,128)(2,1)}) custom-call(bf16[4,128,640]{2,1,0:T(8,128)(2,1)} %bitcast.50), custom_call_target="tpu_custom_call" | custom-call | bytes 65536 | tf_op jit(solution)/shard_map/trade_group/pallas_call | solution.py:979
  (129 shorter events, 72.3 us)
Async XLA Ops:
  7.2 22.5 %copy-start.16 = (bf16[1024,128]{1,0:T(8,128)(2,1)S(1)}, bf16[1024,128]{1,0:T(8,128)(2,1)}, u32[]{:S(2)}) copy-start(bf16[1024,128]{1,0:T(8,128)(2,1)} %param.28) | copy-start | bytes 786436
  7.2 32.0 %copy-start.9 = (bf16[256,2048]{1,0:T(8,128)(2,1)S(1)}, bf16[256,2048]{1,0:T(8,128)(2,1)}, u32[]{:S(2)}) copy-start(bf16[256,2048]{1,0:T(8,128)(2,1)} %param.16) | copy-start | bytes 3145732
  7.2 87.4 %all-gather.5.cloned.1.call-start = ((), (), s32[]{:S(2)}) async-start(), calls=%async_computation.4 | async-start | bytes 3276800 | tf_op jit(solution)/shard_map/all_gather | solution.py:1158
  29.6 191.0 %all-gather.7.cloned.1.call-start = ((), (), s32[]{:S(2)}) async-start(), calls=%async_computation.5 | async-start | bytes 1310720 | tf_op jit(solution)/shard_map/all_gather | solution.py:1158
  37.9 230.0 %all-gather.9.cloned.1.call-start = ((), (), s32[]{:S(2)}) async-start(), calls=%async_computation.6 | async-start | bytes 7864320 | tf_op jit(solution)/shard_map/all_gather | solution.py:1158
  114.0 26.5 %copy-start.13 = (bf16[3072,128]{1,0:T(8,128)(2,1)S(1)}, bf16[3072,128]{1,0:T(8,128)(2,1)}, u32[]{:S(2)}) copy-start(bf16[3072,128]{1,0:T(8,128)(2,1)} %param.31) | copy-start | bytes 2359300
  140.4 1.9 copy-start.20
  140.5 178.7 %all-gather.11.cloned.1.call-start = ((), (), s32[]{:S(2)}) async-start(), calls=%async_computation.7 | async-start | bytes 3932160 | tf_op jit(solution)/shard_map/all_gather | solution.py:1158
  170.2 303.0 %reduce-scatter.5.cloned.1.call-start = ((), (), s32[]{:S(2)}) async-start(), calls=%async_computation.8 | async-start | bytes 3932160 | tf_op jit(solution)/shard_map/reduce_scatter | solution.py:1163
  310.5 1.6 copy-start.1
  319.2 14.4 %copy-start.2 = (bf16[2048,768]{1,0:T(8,128)(2,1)S(1)}, bf16[2048,768]{1,0:T(8,128)(2,1)}, u32[]{:S(2)}) copy-start(bf16[2048,768]{1,0:T(8,128)(2,1)} %copy-done.1) | copy-start | bytes 9437188
  344.2 271.9 %reduce-scatter.7.cloned.1.call-start = ((), (), s32[]{:S(2)}) async-start(), calls=%async_computation.9 | async-start | bytes 7864320 | tf_op jit(solution)/shard_map/reduce_scatter | solution.py:1163
  393.9 222.1 %reduce-scatter.9.cloned.1.call-start = ((), (), s32[]{:S(2)}) async-start(), calls=%async_computation.10 | async-start | bytes 1310720 | tf_op jit(solution)/shard_map/reduce_scatter | solution.py:1163
  394.0 3.2 copy-start.8
  394.0 3.1 copy-start.11
  398.4 1.9 copy-start.3
  486.5 183.3 %reduce-scatter.11.cloned.1.call-start = ((), (), s32[]{:S(2)}) async-start(), calls=%async_computation.11 | async-start | bytes 3276800 | tf_op jit(solution)/shard_map/reduce_scatter | solution.py:1163
  600.4 3.5 copy-start.23
  662.2 2.5 copy-start.14
  662.2 3.8 copy-start.22
  664.7 18.6 %copy-start.15 = (bf16[128,1024]{1,0:T(8,128)(2,1)S(1)}, bf16[128,1024]{1,0:T(8,128)(2,1)}, u32[]{:S(2)}) copy-start(bf16[128,1024]{1,0:T(8,128)(2,1)} %get-tuple-element.126) | copy-start | bytes 786436
  681.4 2.9 copy-start.18
  681.4 3.6 copy-start.17
  681.4 4.4 copy-start.19
  (8 other events, 8.7 us)
Sparse Core Ops, SparseCore 0:
  29.7 53.8 all-gather.4
  85.2 26.7 all-gather.6
  140.6 115.4 all-gather.8
  257.5 61.6 all-gather.10
  344.3 64.6 reduce-scatter.4
  411.2 123.1 reduce-scatter.6
  536.7 26.3 reduce-scatter.8
  600.5 69.2 reduce-scatter.10

commit v5 on v4

--- a/solution.py
+++ b/solution.py
@@ -219,7 +219,8 @@
     return pltpu.roll(values, HEAD_SIZE // 2, 1)
 
 
-def prepare_body(raw_ref, cos_ref, sin_ref, gain_ref, q_ref, kv_ref):
+def prepare_body(x_ref, w_ref, cos_ref, sin_ref, gain_ref, raw_ref, q_ref, kv_ref):
+    raw_ref[...] = dg(x_ref[...], w_ref[...], NN)
     for i in range(3):
         cols = slice(i * HEAD_SIZE, (i + 1) * HEAD_SIZE)
         u = raw_ref[:, cols]
@@ -233,18 +234,21 @@
     kv_ref[:, HEAD_SIZE:] = raw_ref[:, 3 * HEAD_SIZE : 4 * HEAD_SIZE].astype(bf)
 
 
-def prepare(raw, cos, sin, gains):
-    T, width = raw.shape
+def prepare(x, w, cos, sin, gains):
+    T, depth = x.shape
+    width = w.shape[1]
     blk = lambda w: pl.BlockSpec((BQ, w), lambda i: (i, 0))
+    whole = lambda *s: pl.BlockSpec(s, lambda i: (0, 0))
+    pair = jax.ShapeDtypeStruct((T, 2 * HEAD_SIZE), bf)
     return pl.pallas_call(
         prepare_body,
         grid=(T // BQ,),
-        in_specs=[blk(width), blk(HEAD_SIZE), blk(HEAD_SIZE), pl.BlockSpec((2, HEAD_SIZE), lambda i: (0, 0))],
-        out_specs=[blk(2 * HEAD_SIZE), blk(2 * HEAD_SIZE)],
-        out_shape=[jax.ShapeDtypeStruct((T, 2 * HEAD_SIZE), bf)] * 2,
-        cost_estimate=pl.CostEstimate(flops=T * 4000, bytes_accessed=T * 640 * 8, transcendentals=T),
+        in_specs=[blk(depth), whole(depth, width), blk(HEAD_SIZE), blk(HEAD_SIZE), whole(2, HEAD_SIZE)],
+        out_specs=[blk(width), blk(2 * HEAD_SIZE), blk(2 * HEAD_SIZE)],
+        out_shape=[jax.ShapeDtypeStruct((T, width), f32), pair, pair],
+        cost_estimate=pl.CostEstimate(flops=2 * T * depth * width, bytes_accessed=T * 640 * 12, transcendentals=T),
         name="prepare_heads",
-    )(raw, cos, sin, gains)
+    )(x, w, cos, sin, gains)
 
 
 def prepare_back_body(raw_ref, cos_ref, sin_ref, gain_ref, dq_ref, dkv_ref, back_ref, dlogit_ref, out_ref, sums_ref):
@@ -350,47 +354,67 @@
         pl.semaphore_signal(barrier, inc=1, device_id=device, device_id_type=MESH)
     pl.semaphore_wait(barrier, len(devices))
 
-def gather_body(x_ref, out_ref, send, recv, local):
+def gather_steps(x_ref, out_ref, send, recv, local):
     base, t, tx, ty, td, c = places()
     share = x_ref.shape[0]
     half = share // 2
     xdev, ydev, mate = (base + tx, c), (base + ty, c), (base + t, 1 - c)
     greet([xdev, ydev, mate])
+
     def spot(who, part=None):
         start = (2 * who + c) * share
         if part is None:
             return out_ref.at[pl.ds(pl.multiple_of(start, share), share)]
         return out_ref.at[pl.ds(pl.multiple_of(start + part * half, half), half)]
+
     def copy(kind, src, dst, device):
-        return pltpu.make_async_remote_copy(src_ref=src, dst_ref=dst, send_sem=send.at[kind], recv_sem=recv.at[kind], device_id=device, device_id_type=MESH)
+        one = pltpu.make_async_remote_copy(
+            src_ref=src, dst_ref=dst, send_sem=send.at[kind], recv_sem=recv.at[kind], device_id=device, device_id_type=MESH
+        )
+        one.start()
+        return one
+
     own = pltpu.make_async_copy(x_ref, spot(t), local)
     own.start()
     mine = [x_ref.at[pl.ds(0, half)], x_ref.at[pl.ds(half, half)]]
     k = {}
-    k[2] = copy(2, mine[0], spot(t, 0), ydev); k[2].start()
-    k[1] = copy(1, mine[1], spot(t, 1), xdev); k[1].start()
-    k[3] = copy(3, mine[1], spot(t, 1), ydev); k[3].start()
-    k[0] = copy(0, mine[0], spot(t, 0), xdev); k[0].start()
-    k[6] = copy(6, x_ref, spot(t), mate); k[6].start()
+    k[2] = copy(2, mine[0], spot(t, 0), ydev)
+    k[1] = copy(1, mine[1], spot(t, 1), xdev)
+    k[3] = copy(3, mine[1], spot(t, 1), ydev)
+    k[0] = copy(0, mine[0], spot(t, 0), xdev)
+    k[6] = copy(6, x_ref, spot(t), mate)
+    yield
     k[2].wait_recv()
-    k[4] = copy(4, spot(ty, 0), spot(ty, 0), xdev); k[4].start()
-    k[9] = copy(9, spot(ty, 0), spot(ty, 0), mate); k[9].start()
+    k[4] = copy(4, spot(ty, 0), spot(ty, 0), xdev)
+    k[9] = copy(9, spot(ty, 0), spot(ty, 0), mate)
     k[1].wait_recv()
-    k[5] = copy(5, spot(tx, 1), spot(tx, 1), ydev); k[5].start()
-    k[8] = copy(8, spot(tx, 1), spot(tx, 1), mate); k[8].start()
+    k[5] = copy(5, spot(tx, 1), spot(tx, 1), ydev)
+    k[8] = copy(8, spot(tx, 1), spot(tx, 1), mate)
+    yield
     k[0].wait_recv()
-    k[7] = copy(7, spot(tx, 0), spot(tx, 0), mate); k[7].start()
+    k[7] = copy(7, spot(tx, 0), spot(tx, 0), mate)
     k[3].wait_recv()
-    k[10] = copy(10, spot(ty, 1), spot(ty, 1), mate); k[10].start()
+    k[10] = copy(10, spot(ty, 1), spot(ty, 1), mate)
     k[4].wait_recv()
-    k[11] = copy(11, spot(td, 0), spot(td, 0), mate); k[11].start()
+    k[11] = copy(11, spot(td, 0), spot(td, 0), mate)
     k[5].wait_recv()
-    k[12] = copy(12, spot(td, 1), spot(td, 1), mate); k[12].start()
+    k[12] = copy(12, spot(td, 1), spot(td, 1), mate)
     for kind in range(6, 13):
         k[kind].wait_recv()
     for kind in range(13):
         k[kind].wait_send()
     own.wait()
+    yield
+
+
+def gather_body(x_ref, out_ref, send, recv, local):
+    for _ in gather_steps(x_ref, out_ref, send, recv, local):
+        pass
+
+
+def gather_sems():
+    return [pltpu.SemaphoreType.DMA((13,)), pltpu.SemaphoreType.DMA((13,)), pltpu.SemaphoreType.DMA]
+
 
 def gather_group(x):
     share, width = x.shape
@@ -399,11 +423,85 @@
         out_shape=jax.ShapeDtypeStruct((share * GROUP * 2, width), x.dtype),
         in_specs=[pl.BlockSpec(memory_space=pltpu.VMEM)],
         out_specs=pl.BlockSpec(memory_space=pl.ANY),
-        scratch_shapes=[pltpu.SemaphoreType.DMA((13,)), pltpu.SemaphoreType.DMA((13,)), pltpu.SemaphoreType.DMA],
+        scratch_shapes=gather_sems(),
         compiler_params=pltpu.CompilerParams(collective_id=1, has_side_effects=True),
         cost_estimate=QUICK,
         name="gather_group",
     )(x)
+
+
+def gather_attend_body(
+    x_ref, q_ref, kv_ref, qbit_ref, kbit_ref, acc_in, tot_in, raw_ref, out_ref, attn_ref, mixed_ref, lse_ref,
+    acc, tot, logit, fetch, send, recv, local
+):
+    edge = raw_ref.shape[1] - HEAD_SIZE
+    logits = pltpu.make_async_copy(raw_ref.at[:, pl.ds(edge, HEAD_SIZE)], logit, fetch)
+    logits.start()
+    steps = gather_steps(x_ref, out_ref, send, recv, local)
+    next(steps)
+    logits.wait()
+    nk, _, bk = kbit_ref.shape
+
+    def block(qb, _):
+        here = pl.ds(pl.multiple_of(qb * BQ, BQ), BQ)
+        q = halves(q_ref, here)
+        acc[...] = jnp.zeros_like(acc)
+        tot[...] = jnp.zeros_like(tot)
+
+        def step(kb, _):
+            rows = pl.ds(pl.multiple_of(kb * bk, bk), bk)
+            s = dg(q, kv_ref[rows, :HEAD_SIZE], NT) * (LOG2E * SCORE_SCALE)
+            seen = (qbit_ref[here, :] & kbit_ref[kb]) != 0
+            p = jnp.exp2(jnp.where(jnp.concatenate([seen, seen], axis=0), s, -1e30))
+            part = p[:, 0:128]
+            for i in range(1, bk // 128):
+                part = part + p[:, i * 128 : (i + 1) * 128]
+            tot[...] += part
+            acc[...] += dg(p.astype(bf), kv_ref[rows, HEAD_SIZE:], NN)
+            return 0
+
+        lax.fori_loop(0, nk, step, 0)
+        total = jnp.sum(tot[...], axis=1, keepdims=True)
+        for h in range(2):
+            rows = slice(h * BQ, (h + 1) * BQ)
+            cols = slice(h * HEAD_SIZE, (h + 1) * HEAD_SIZE)
+            sums = total[rows] + tot_in[here, h : h + 1]
+            out = (acc[rows, :] + acc_in[here, cols]) / sums
+            attn_ref[here, cols] = out
+            mixed_ref[here, cols] = (out * jax.nn.sigmoid(logit[here, h : h + 1])).astype(bf)
+            lse_ref[h : h + 1, here] = as_rows(jnp.log2(sums))
+        return 0
+
+    blocks = q_ref.shape[0] // BQ
+    lax.fori_loop(0, 3 * blocks // 8, block, 0)
+    next(steps)
+    lax.fori_loop(3 * blocks // 8, blocks, block, 0)
+    next(steps)
+
+
+def gather_attend(x, q, kv, qbit, kbit, acc, tot, raw, key):
+    share, width = x.shape
+    T, W = q.shape
+    vmem = pl.BlockSpec(memory_space=pltpu.VMEM)
+    anywhere = pl.BlockSpec(memory_space=pl.ANY)
+    shape = jax.ShapeDtypeStruct
+    return pl.pallas_call(
+        gather_attend_body,
+        out_shape=[shape((share * GROUP * 2, width), bf), shape((T, W), f32), shape((T, W), bf), shape((2, T), f32)],
+        in_specs=[vmem] * 7 + [anywhere],
+        out_specs=[anywhere] + [vmem] * 3,
+        scratch_shapes=[
+            pltpu.VMEM((2 * BQ, HEAD_SIZE), f32),
+            pltpu.VMEM((2 * BQ, HEAD_SIZE), f32),
+            pltpu.VMEM((T, HEAD_SIZE), f32),
+            pltpu.SemaphoreType.DMA,
+        ]
+        + gather_sems(),
+        compiler_params=pltpu.CompilerParams(collective_id=key, has_side_effects=True, vmem_limit_bytes=40 << 20),
+        cost_estimate=QUICK,
+        name="gather_attend",
+    )(x, q, kv, qbit, kbit, acc, tot, raw)
+
 
 def reduce_body(side, back, left_ref, right_ref, *refs):
     if side:
@@ -1188,20 +1286,18 @@
     rows = layer_in.astype(f32)
     normed_one, norm_one_back = jax.vjp(row_norm, rows, gain_one)
     hidden_first = gather_group(after(normed_one.astype(bf), mine_out))
-    raw = jnp.dot(hidden_first, full_attn, preferred_element_type=f32)
     q_width = query_weight.shape[1] // GROUP
     k_width = key_matrix.shape[1] // GROUP
     heads = q_width // HEAD_SIZE
-    query, pair = prepare(raw, cosine, sine, head_gains)
+    raw, query, pair = prepare(hidden_first, full_attn, cosine, sine, head_gains)
     mine_glu, pair_early = trade_group([gate_weight, up_weight], 5, pair)
     full_glu = far_gather(mine_glu)
     query = after(query, mine_glu)
     own = attend(True, flags[:, key_cut:], query, pair, query_column, key_lines[key_cut:])
     mine_down = trade_group([after(down_weight.T, own[0])], 6)
     full_down = far_gather(mine_down)
-    grad_tokens = gather_group(after(out_grad, mine_down))
-    attn, mixed, lse = attend(
-        False, flags[:, :key_cut], after(query, grad_tokens), pair_early, query_column, key_lines[:key_cut], (own[0], own[1], raw)
+    grad_tokens, attn, mixed, lse = gather_attend(
+        after(out_grad, mine_down), query, pair_early, query_column, key_lines[:key_cut], own[0], own[1], raw, 19
     )
     branch = product_reduce(mixed, full_out, 2)
     middle = rows + branch
@@ -1210,10 +1306,10 @@
     h_two, both_glu, hidden = gather_product(normed_two.astype(bf), full_glu, 14)
     units = full_down.shape[1]
 
-    grad_glu = hidden_back(grad_tokens, full_down, both_glu)
-    down_part = inner(after(grad_tokens, grad_glu), hidden).astype(bf)
+    down_part = inner(grad_tokens, hidden).astype(bf)
     down_rows = far_scatter(down_part)
-    grad_h_two, glu_part = product_reduce(after(grad_glu, down_part), full_glu, 15, h_two)
+    grad_glu = hidden_back(after(grad_tokens, down_part), full_down, both_glu)
+    grad_h_two, glu_part = product_reduce(grad_glu, full_glu, 15, h_two)
     glu_rows = far_scatter(glu_part)
     grad_mid_norm, gain_two_grad = norm_two_back(grad_h_two)
     grad_middle = out_grad.astype(f32) + grad_mid_norm

time: 703 us -> 683 us (0.972)
  matrix products: 21.9 us -> 10.6 us
    pallas_call x1 -> x2, Pallas kernels: 8.08 us -> 52.1 us  [the longest x1 39 us: gather_attend(): pl.pallas_call(gather_attend_body, out_shape=[shape((share * GROUP * 2, w...]
    pallas_call x2 -> x1, Pallas kernels: 80.5 us -> 40.3 us  [gather_group(): pl.pallas_call(gather_body, out_shape=jax.ShapeDtypeStruct((share * GROUP...]
    pallas_call x4, Pallas kernels: 197 us -> 214 us  [product_reduce(): pl.pallas_call(partial(reduce_body, side, back), out_shape=outs, in_specs...]
    pallas_call x7, Pallas kernels: 136 us -> 120 us  [trade_call(): pl.pallas_call(partial(trade_body, inward, widths, sender, bool(side), bo...]
    dot_general x1 -> x0, matrix products: 11.3 us -> none  [per_device(): raw = jnp.dot(hidden_first, full_attn, preferred_element_type=f32)]
    pallas_call x2 -> x1, Pallas kernels: 24.3 us -> 15.7 us  [attend(): pl.pallas_call(partial(attend_body, causal, last), grid_spec=pltpu.Prefet...]
    all_gather x4, waiting for transfers between devices: 7.17 us -> 0.04 us  [far_gather(): lax.all_gather(mine.reshape(GROUP * rows_here, -1), 'dp', axis=0, tiled=T...]
    unnamed x56 -> x70, local copies, waits for them, and re-layouts: 15.2 us -> 20.9 us
  transfers between devices with their start and end apart: 8 -> 8, of which waited for: 2 -> 1; matrix products, arithmetic and copies ran while one was open for 7% -> 8% of each run, Pallas kernels for 78% -> 82%
where the time goes in v5:
time: 683 us; the launch traced here: 677 us
  Pallas kernels  584 us (86%)
  other arithmetic  32 us (5%)
  local copies, waits for them, and re-layouts  30.7 us (4%)
  between operations  15.1 us (2%)
  matrix products  10.6 us (2%)
    pallas_call x4, Pallas kernels, product_reduce(): pl.pallas_call(partial(reduce_body, side, back), out_shape=outs, in_specs...  214 us
    pallas_call x7, Pallas kernels, trade_call(): pl.pallas_call(partial(trade_body, inward, widths, sender, bool(side), bo...  120 us
    pallas_call x2, Pallas kernels, gather_product(): pl.pallas_call(partial(gather_product_body, not gated), out_shape=outs, i...  81.7 us
    pallas_call x1, Pallas kernels, gather_group(): pl.pallas_call(gather_body, out_shape=jax.ShapeDtypeStruct((share * GROUP...  40.3 us
    pallas_call x1, Pallas kernels, gather_attend(): pl.pallas_call(gather_attend_body, out_shape=[shape((share * GROUP * 2, w...  39 us
    pallas_call x2, Pallas kernels, attend_back(): pl.pallas_call(partial(attend_back_body, causal), grid_spec=pltpu.Prefetc...  30.7 us
    unnamed x70, local copies, waits for them, and re-layouts  20.9 us
    pallas_call x1, Pallas kernels, attend(): pl.pallas_call(partial(attend_body, causal, last), grid_spec=pltpu.Prefet...  15.7 us
  transfers between devices with their start and end apart: 8, of which 1 were waited for; matrix products, arithmetic and copies ran while one was open for 8% of the time, Pallas kernels for 82%

profile of v5, /device:TPU:0, one launch (start us, length us, event | category | flops | bytes accessed | tf_op | source)
XLA Modules:
  0.0 677.1 jit_solution(1438440323879676601)
XLA Ops:
  10.3 19.3 %trade_group.7 = (bf16[4,128,640]{2,1,0:T(8,128)(2,1)}, f32[2,4,4,8,128]{4,3,2,1,0:T(8,128)}) custom-call(bf16[128,1024]{1,0:T(8,128)(2,1)} %refs_0_.2, bf16[128,512]{1,0:T(8,128)(2,1)} %refs_1_.2, bf16[128,512]{1,0:T(8,128)(2,1)} %refs_2_.1, bf16[128,512]{1,0:T(8,128)(2,1)} %bitcast.50, f32[8,128]{1,0:T(8,128)} %fusion.18.refs_4_), custom_call_target="tpu_custom_call" | custom-call | bytes 65536 | tf_op jit(solution)/shard_map/trade_group/pallas_call | solution.py:1077
  30.5 7.4 %trade_group.8 = bf16[4,128,256]{2,1,0:T(8,128)(2,1)} custom-call(bf16[128,1024]{1,0:T(8,128)(2,1)} %bitcast.46), custom_call_target="tpu_custom_call" | custom-call | bytes 65536 | tf_op jit(solution)/shard_map/trade_group/pallas_call | solution.py:1077
  40.7 40.3 %gather_group.1.x_ref.refs_0_ = bf16[2048,2048]{1,0:T(8,128)(2,1)} custom-call(bf16[256,2048]{1,0:T(8,128)(2,1)} %fusion.2.x_ref), custom_call_target="tpu_custom_call" | custom-call | bytes 65536 | tf_op jit(solution)/shard_map/gather_group/pallas_call | solution.py:421
  81.3 5.7 tables.1
  94.6 13.0 %prepare_heads.1 = (f32[2048,640]{1,0:T(8,128)}, bf16[2048,256]{1,0:T(8,128)(2,1)}, bf16[2048,256]{1,0:T(8,128)(2,1)}) custom-call(bf16[2048,2048]{1,0:T(8,128)(2,1)} %gather_group.1.x_ref.refs_0_, bf16[2048,640]{1,0:T(8,128)(2,1)} %all-gather.5.cloned.1.call-done.w_ref.right_ref, f32[2048,128]{1,0:T(8,128)} %get-tuple-element.205.cos_ref, ...), custom_call_target="tpu_custom_call" | custom-call | flops 5368709120 | bytes 15728640 | tf_op jit(solution)/shard_map/prepare_heads/pallas_call | solution.py:243
  107.7 26.4 %trade_group.9 = (bf16[4,128,1536]{2,1,0:T(8,128)(2,1)}, bf16[2048,256]{1,0:T(8,128)(2,1)}) custom-call(bf16[128,3072]{1,0:T(8,128)(2,1)} %refs_0_.3, bf16[128,3072]{1,0:T(8,128)(2,1)} %refs_1_.3, bf16[2048,256]{1,0:T(8,128)(2,1)} %get-tuple-element.79.refs_2_.kv_ref), custom_call_target="tpu_custom_call" | custom-call | bytes 65536 | tf_op jit(solution)/shard_map/trade_group/pallas_call | solution.py:1077
  136.6 15.7 %attend_own.1 = (f32[2048,256]{1,0:T(8,128)}, f32[2048,2]{1,0:T(8,128)}) custom-call(s32[8,4]{1,0:T(8,128)} %get-tuple-element.211.flags, bf16[2048,256]{1,0:T(8,128)(2,1)} %get-tuple-element.81.q_ref, bf16[2048,256]{1,0:T(8,128)(2,1)} %get-tuple-element.79.refs_2_.kv_ref, s32[2048,1]{1,0:T(8,128)} %get-tuple-element.82.qbit_ref, ...), custom_call_target="tpu_custom_call" | custom-call | flops 2147483648 | bytes 8388608 | tf_op jit(solution)/shard_map/attend_own/pallas_call | solution.py:117
  152.3 12.5 %trade_group.10 = bf16[4,128,768]{2,1,0:T(8,128)(2,1)} custom-call(bf16[128,3072]{1,0:T(8,128)(2,1)} %bitcast.42), custom_call_target="tpu_custom_call" | custom-call | bytes 65536 | tf_op jit(solution)/shard_map/trade_group/pallas_call | solution.py:1077
  169.5 39.0 %gather_attend.1 = (bf16[2048,2048]{1,0:T(8,128)(2,1)}, f32[2048,256]{1,0:T(8,128)S(1)}, bf16[2048,256]{1,0:T(8,128)(2,1)S(1)}, f32[2,2048]{1,0:T(2,128)S(1)}) custom-call(bf16[256,2048]{1,0:T(8,128)(2,1)S(1)} %copy-done, bf16[2048,256]{1,0:T(8,128)(2,1)S(1)} %copy-done.7, bf16[2048,256]{1,0:T(8,128)(2,1)S(1)} %copy-done.8, s32[2048,1]{1,0:T(8,128)S(1)} %copy-done.9, ...), custom_call_target="tpu_custom_call" | custom-call | bytes 65536 | tf_op jit(solution)/shard_map/gather_attend/pallas_call | solution.py:488
  211.5 43.6 %product_reduce.4 = f32[256,2048]{1,0:T(8,128)} custom-call(bf16[2048,256]{1,0:T(8,128)(2,1)} %copy-done.2, bf16[2048,256]{1,0:T(8,128)(2,1)} %all-gather.7.cloned.1.call-done.right_ref.w_ref), custom_call_target="tpu_custom_call" | custom-call | bytes 65536 | tf_op jit(solution)/shard_map/product_reduce/pallas_call | solution.py:679
  258.9 42.5 %gather_product.2 = (bf16[2048,2048]{1,0:T(8,128)(2,1)}, f32[2048,1536]{1,0:T(8,128)}, bf16[2048,768]{1,0:T(8,128)(2,1)S(1)}) custom-call(bf16[256,2048]{1,0:T(8,128)(2,1)S(1)} %multiply_convert_fusion.x_ref, bf16[2048,1536]{1,0:T(8,128)(2,1)} %all-gather.9.cloned.1.call-done.w_ref.right_ref), custom_call_target="tpu_custom_call" | custom-call | bytes 65536 | tf_op jit(solution)/shard_map/gather_product/pallas_call | solution.py:852
  303.0 10.6 %convolution_convert_fusion = bf16[2048,768]{1,0:T(8,128)(2,1)} fusion(bf16[2048,2048]{1,0:T(8,128)(2,1)} %get-tuple-element.93.dout_ref, bf16[2048,768]{1,0:T(8,128)(2,1)S(1)} %get-tuple-element.108.left_ref), kind=kOutput, calls=%fused_computation.5 | convolution fusion | flops 6444023808 | bytes 14680064 | tf_op jit(solution)/shard_map/dot_general | solution.py:27
  313.7 14.4 %hidden_back.1.left_ref = bf16[2048,1536]{1,0:T(8,128)(2,1)} custom-call(bf16[2048,2048]{1,0:T(8,128)(2,1)} %get-tuple-element.93.dout_ref, bf16[2048,768]{1,0:T(8,128)(2,1)} %all-gather.11.cloned.1.call-done.down_ref.right_ref, f32[2048,1536]{1,0:T(8,128)} %get-tuple-element.94.both_ref), custom_call_target="tpu_custom_call" | custom-call | flops 6442450944 | bytes 47185920 | tf_op jit(solution)/shard_map/hidden_back/pallas_call | solution.py:327
  328.0 50.3 %product_reduce.5 = (f32[256,2048]{1,0:T(8,128)}, bf16[2048,1536]{1,0:T(8,128)(2,1)}) custom-call(bf16[2048,1536]{1,0:T(8,128)(2,1)} %hidden_back.1.left_ref, bf16[2048,1536]{1,0:T(8,128)(2,1)} %all-gather.9.cloned.1.call-done.w_ref.right_ref, bf16[2048,2048]{1,0:T(8,128)(2,1)} %get-tuple-element.95.refs_0_), custom_call_target="tpu_custom_call" | custom-call | bytes 65536 | tf_op jit(solution)/shard_map/product_reduce/pallas_call | solution.py:679
  384.7 39.2 %gather_product.3 = (bf16[2048,2048]{1,0:T(8,128)(2,1)}, bf16[2048,256]{1,0:T(8,128)(2,1)S(1)}, bf16[2048,128]{1,0:T(8,128)(2,1)S(1)}, f32[2,2048]{1,0:T(2,128)S(1)}) custom-call(bf16[256,2048]{1,0:T(8,128)(2,1)S(1)} %fusion.25.x_ref, bf16[2048,256]{1,0:T(8,128)(2,1)S(1)} %copy-done.1, f32[2048,256]{1,0:T(8,128)S(1)} %copy-done.5, ...), custom_call_target="tpu_custom_call" | custom-call | bytes 65536 | tf_op jit(solution)/shard_map/gather_product/pallas_call | solution.py:852
  426.3 6.3 attend_earlier_back.1
  432.6 24.4 %attend_own_back.1 = (f32[2048,256]{1,0:T(8,128)}, f32[2048,256]{1,0:T(8,128)}) custom-call(s32[8,4]{1,0:T(8,128)} %get-tuple-element.211.flags, bf16[2048,256]{1,0:T(8,128)(2,1)} %get-tuple-element.81.q_ref, bf16[2048,256]{1,0:T(8,128)(2,1)} %copy-done.12, bf16[2048,256]{1,0:T(8,128)(2,1)} %get-tuple-element.79.refs_2_.kv_ref, ...), custom_call_target="tpu_custom_call" | custom-call | flops 5368709120 | bytes 12582912 | tf_op jit(solution)/shard_map/attend_own_back/pallas_call | solution.py:201
  457.0 13.7 %trade_group.11 = (bf16[128,3072]{1,0:T(8,128)(2,1)}, bf16[2048,256]{1,0:T(8,128)(2,1)}) custom-call(bf16[4,128,768]{2,1,0:T(8,128)(2,1)} %bitcast.47, bf16[2048,2048]{1,0:T(8,128)(2,1)} %get-tuple-element.106.refs_1_, bf16[2048,256]{1,0:T(8,128)(2,1)} %copy-done.2), custom_call_target="tpu_custom_call" | custom-call | bytes 65536 | tf_op jit(solution)/shard_map/trade_group/pallas_call | solution.py:1077
  471.0 74.5 %product_reduce.6 = (f32[256,2048]{1,0:T(8,128)}, bf16[2048,256]{1,0:T(8,128)(2,1)}) custom-call(bf16[2048,768]{1,0:T(8,128)(2,1)} %copy-done.3, bf16[2048,768]{1,0:T(8,128)(2,1)} %all-gather.11.cloned.1.call-done.down_ref.right_ref, bf16[2048,256]{1,0:T(8,128)(2,1)} %get-tuple-element.109.refs_0_), custom_call_target="tpu_custom_call" | custom-call | bytes 65536 | tf_op jit(solution)/shard_map/product_reduce/pallas_call | solution.py:679
  545.6 9.8 %prepare_heads_back.1 = (bf16[2048,640]{1,0:T(8,128)(2,1)}, f32[2,128]{1,0:T(2,128)}) custom-call(f32[2048,640]{1,0:T(8,128)} %get-tuple-element.89.raw_ref.refs_1_, f32[2048,128]{1,0:T(8,128)} %get-tuple-element.205.cos_ref, f32[2048,128]{1,0:T(8,128)} %get-tuple-element.204.sin_ref, f32[2,128]{1,0:T(2,128)} %pad_maximum_fusion.gain_ref, ...), custom_call_target="tpu_custom_call" | custom-call | flops 16384000 | bytes 13107200 | tf_op jit(solution)/shard_map/prepare_heads_back/pallas_call | solution.py:283
  555.3 45.1 %product_reduce.7 = (f32[256,2048]{1,0:T(8,128)}, bf16[2048,640]{1,0:T(8,128)(2,1)}) custom-call(bf16[2048,640]{1,0:T(8,128)(2,1)} %get-tuple-element.114.left_ref, bf16[2048,640]{1,0:T(8,128)(2,1)} %all-gather.5.cloned.1.call-done.w_ref.right_ref, bf16[2048,2048]{1,0:T(8,128)(2,1)} %gather_group.1.x_ref.refs_0_), custom_call_target="tpu_custom_call" | custom-call | bytes 65536 | tf_op jit(solution)/shard_map/product_reduce/pallas_call | solution.py:679
  609.8 5.6 fusion.6
  615.3 29.4 %trade_group.12 = (bf16[128,3072]{1,0:T(8,128)(2,1)}, bf16[128,3072]{1,0:T(8,128)(2,1)}, bf16[128,1024]{1,0:T(8,128)(2,1)}, f32[8,128]{1,0:T(8,128)}) custom-call(bf16[4,128,1536]{2,1,0:T(8,128)(2,1)} %bitcast.44, bf16[4,128,256]{2,1,0:T(8,128)(2,1)} %bitcast.59, f32[2,4,4,8,128]{4,3,2,1,0:T(8,128)} %bitcast.56), custom_call_target="tpu_custom_call" | custom-call | bytes 65536 | tf_op jit(solution)/shard_map/trade_group/pallas_call | solution.py:1077
  653.1 11.6 %trade_group.13 = (bf16[128,1024]{1,0:T(8,128)(2,1)}, bf16[128,512]{1,0:T(8,128)(2,1)}, bf16[128,512]{1,0:T(8,128)(2,1)}, bf16[128,512]{1,0:T(8,128)(2,1)}) custom-call(bf16[4,128,640]{2,1,0:T(8,128)(2,1)} %bitcast.48), custom_call_target="tpu_custom_call" | custom-call | bytes 65536 | tf_op jit(solution)/shard_map/trade_group/pallas_call | solution.py:1077
  (141 shorter events, 61.9 us)
Async XLA Ops:
  7.2 22.5 %copy-start.23 = (bf16[1024,128]{1,0:T(8,128)(2,1)S(1)}, bf16[1024,128]{1,0:T(8,128)(2,1)}, u32[]{:S(2)}) copy-start(bf16[1024,128]{1,0:T(8,128)(2,1)} %param.28) | copy-start | bytes 786436
  7.2 31.9 %copy-start.17 = (bf16[256,2048]{1,0:T(8,128)(2,1)S(1)}, bf16[256,2048]{1,0:T(8,128)(2,1)}, u32[]{:S(2)}) copy-start(bf16[256,2048]{1,0:T(8,128)(2,1)} %param.16) | copy-start | bytes 3145732
  7.2 87.4 %all-gather.5.cloned.1.call-start = ((), (), s32[]{:S(2)}) async-start(), calls=%async_computation.4 | async-start | bytes 3276800 | tf_op jit(solution)/shard_map/all_gather | solution.py:1256
  29.6 181.9 %all-gather.7.cloned.1.call-start = ((), (), s32[]{:S(2)}) async-start(), calls=%async_computation.5 | async-start | bytes 1310720 | tf_op jit(solution)/shard_map/all_gather | solution.py:1256
  37.9 220.9 %all-gather.9.cloned.1.call-start = ((), (), s32[]{:S(2)}) async-start(), calls=%async_computation.6 | async-start | bytes 7864320 | tf_op jit(solution)/shard_map/all_gather | solution.py:1256
  107.7 26.5 %copy-start.20 = (bf16[3072,128]{1,0:T(8,128)(2,1)S(1)}, bf16[3072,128]{1,0:T(8,128)(2,1)}, u32[]{:S(2)}) copy-start(bf16[3072,128]{1,0:T(8,128)(2,1)} %param.31) | copy-start | bytes 2359300
  134.1 179.6 %all-gather.11.cloned.1.call-start = ((), (), s32[]{:S(2)}) async-start(), calls=%async_computation.8 | async-start | bytes 3932160 | tf_op jit(solution)/shard_map/all_gather | solution.py:1256
  136.6 28.8 %copy-start.8 = (bf16[2048,256]{1,0:T(8,128)(2,1)S(1)}, bf16[2048,256]{1,0:T(8,128)(2,1)}, u32[]{:S(2)}) copy-start(bf16[2048,256]{1,0:T(8,128)(2,1)} %get-tuple-element.87.kv_ref) | copy-start | bytes 3145732
  152.3 13.1 %copy-start = (bf16[256,2048]{1,0:T(8,128)(2,1)S(1)}, bf16[256,2048]{1,0:T(8,128)(2,1)}, u32[]{:S(2)}) copy-start(bf16[256,2048]{1,0:T(8,128)(2,1)} %x_ref) | copy-start | bytes 3145732
  152.3 13.2 %copy-start.7 = (bf16[2048,256]{1,0:T(8,128)(2,1)S(1)}, bf16[2048,256]{1,0:T(8,128)(2,1)}, u32[]{:S(2)}) copy-start(bf16[2048,256]{1,0:T(8,128)(2,1)} %get-tuple-element.81.q_ref) | copy-start | bytes 3145732
  164.8 292.2 %reduce-scatter.5.cloned.1.call-start = ((), (), s32[]{:S(2)}) async-start(), calls=%async_computation.7 | async-start | bytes 3932160 | tf_op jit(solution)/shard_map/reduce_scatter | solution.py:1261
  211.5 43.6 %copy-start.18 = (bf16[256,2048]{1,0:T(8,128)(2,1)S(1)}, bf16[256,2048]{1,0:T(8,128)(2,1)}, u32[]{:S(2)}) copy-start(bf16[256,2048]{1,0:T(8,128)(2,1)} %param.16) | copy-start | bytes 3145732
  313.6 301.7 %reduce-scatter.7.cloned.1.call-start = ((), (), s32[]{:S(2)}) async-start(), calls=%async_computation.9 | async-start | bytes 7864320 | tf_op jit(solution)/shard_map/reduce_scatter | solution.py:1261
  378.3 237.0 %reduce-scatter.9.cloned.1.call-start = ((), (), s32[]{:S(2)}) async-start(), calls=%async_computation.10 | async-start | bytes 1310720 | tf_op jit(solution)/shard_map/reduce_scatter | solution.py:1261
  378.6 3.2 copy-start.16
  378.6 3.2 copy-start.19
  470.7 182.3 %reduce-scatter.11.cloned.1.call-start = ((), (), s32[]{:S(2)}) async-start(), calls=%async_computation.11 | async-start | bytes 3276800 | tf_op jit(solution)/shard_map/reduce_scatter | solution.py:1261
  600.5 2.7 copy-start.30
  644.8 2.5 copy-start.21
  644.8 3.8 copy-start.29
  647.3 19.2 %copy-start.22 = (bf16[128,1024]{1,0:T(8,128)(2,1)S(1)}, bf16[128,1024]{1,0:T(8,128)(2,1)}, u32[]{:S(2)}) copy-start(bf16[128,1024]{1,0:T(8,128)(2,1)} %get-tuple-element.126) | copy-start | bytes 786436
  664.6 2.9 copy-start.25
  664.6 3.6 copy-start.24
  664.7 4.4 copy-start.26
  (15 other events, 19.0 us)
Sparse Core Ops, SparseCore 0:
  29.7 53.8 all-gather.4
  85.2 26.7 all-gather.6
  134.2 115.4 all-gather.8
  251.2 61.6 all-gather.10
  315.0 59.0 reduce-scatter.4
  378.5 110.4 reduce-scatter.6
  491.3 50.0 reduce-scatter.8
  600.6 52.4 reduce-scatter.10

commit v6 on v5

--- a/solution.py
+++ b/solution.py
@@ -503,11 +503,50 @@
     )(x, q, kv, qbit, kbit, acc, tot, raw)
 
 
+def own_back(q_ref, g_ref, kv_ref, qbit_ref, kbit_ref, lse_ref, del_ref, dq_in, dq_ref, dkv_ref, dk_acc, dv_acc):
+    dq_ref[...] = dq_in[...]
+
+    def line(ref, rows):
+        return jnp.concatenate([ref[0:1, rows], ref[1:2, rows]], axis=1)
+
+    def keys(kb, _):
+        here = pl.ds(pl.multiple_of(kb * BK, BK), BK)
+        dk_acc[...] = jnp.zeros_like(dk_acc)
+        dv_acc[...] = jnp.zeros_like(dv_acc)
+
+        def step(qb, _):
+            rows = pl.ds(pl.multiple_of(qb * BQ, BQ), BQ)
+            q = halves(q_ref, rows)
+            g = halves(g_ref, rows)
+            k = kv_ref[here, :HEAD_SIZE]
+            s = dg(k, q, NT) * (LOG2E * SCORE_SCALE) - line(lse_ref, rows)
+            at = lax.broadcasted_iota(jnp.int32, (BK, BQ), 0) + kb * BK
+            row = lax.broadcasted_iota(jnp.int32, (BK, BQ), 1) + qb * BQ
+            seen = ((kbit_ref[here, :] & qbit_ref[0:1, rows]) != 0) & (at <= row)
+            p = jnp.exp2(jnp.where(jnp.concatenate([seen, seen], axis=1), s, -1e30))
+            dv_acc[...] += dg(p.astype(bf), g, NN)
+            dp = dg(kv_ref[here, HEAD_SIZE:], g, NT)
+            ds = (p * (dp - line(del_ref, rows))).astype(bf)
+            dk_acc[...] += dg(ds, q, NN)
+            dq = dg(ds, k, TN)
+            dq_ref[rows, :HEAD_SIZE] += dq[:BQ]
+            dq_ref[rows, HEAD_SIZE:] += dq[BQ:]
+            return 0
+
+        lax.fori_loop(kb * (BK // BQ), q_ref.shape[0] // BQ, step, 0)
+        dkv_ref[here, :HEAD_SIZE] = dk_acc[...] * SCORE_SCALE
+        dkv_ref[here, HEAD_SIZE:] = dv_acc[...]
+        return 0
+
+    lax.fori_loop(0, kv_ref.shape[0] // BK, keys, 0)
+
+
 def reduce_body(side, back, left_ref, right_ref, *refs):
     if side:
         tall_ref, out_ref, grad_ref, tall, grad, refs = *refs[:5], refs[5:]
     elif back:
-        pair_ref, out_ref, pair_out, refs = *refs[:3], refs[3:]
+        pair_ref, q_ref, g_ref, kv_ref, qbit_ref, kbit_ref, lse_ref, del_ref, dq_in, refs = *refs[:9], refs[9:]
+        out_ref, pair_out, dq_ref, dkv_ref, dk_acc, dv_acc, refs = *refs[:6], refs[6:]
     else:
         out_ref, refs = refs[0], refs[1:]
     left, right, fars, near, mates, sums, xin, yin, zin, turned, fetch, send, recv = refs
@@ -628,6 +667,8 @@
         lax.fori_loop(0, tall.shape[1] // 256, inner_product, 0)
         put = pltpu.make_async_copy(grad, grad_ref, fetch.at[20])
         put.start()
+    if back:
+        own_back(q_ref, g_ref, kv_ref, qbit_ref, kbit_ref, lse_ref, del_ref, dq_in, dq_ref, dkv_ref, dk_acc, dv_acc)
     k[6].wait_recv()
     add(out_ref.at[A], sums.at[3, A], xin.at[0])
     k[7].wait_recv()
@@ -654,10 +695,9 @@
             pair.wait_recv()
 
 
-def product_reduce(left, right, key, tall=None, pair=None):
+def product_reduce(left, right, key, tall=None, back=()):
     rows, depth = left.shape
     side = tall is not None
-    back = pair is not None
     width = right.shape[0]
     share = rows // (2 * GROUP)
     half = share // 2
@@ -672,12 +712,14 @@
         extra = [pltpu.VMEM(tall.shape, bf), pltpu.VMEM((tall.shape[1], depth), bf)]
     in_specs = [anywhere] * len(ins)
     if back:
-        ins.append(pair)
-        in_specs.append(pl.BlockSpec(memory_space=pltpu.VMEM))
-        outs.append(jax.ShapeDtypeStruct(pair.shape, bf))
-        out_specs.append(anywhere)
+        ins += back
+        in_specs += [pl.BlockSpec(memory_space=pltpu.VMEM)] * len(back)
+        pair, dq = back[0], back[-1]
+        outs += [jax.ShapeDtypeStruct(pair.shape, bf)] + [jax.ShapeDtypeStruct(dq.shape, f32)] * 2
+        out_specs += [anywhere] + [pl.BlockSpec(memory_space=pltpu.VMEM)] * 2
+        extra = [pltpu.VMEM((BK, HEAD_SIZE), f32), pltpu.VMEM((BK, HEAD_SIZE), f32)]
     result = pl.pallas_call(
-        partial(reduce_body, side, back),
+        partial(reduce_body, side, bool(back)),
         out_shape=outs,
         in_specs=in_specs,
         out_specs=out_specs,
@@ -1318,12 +1360,10 @@
     query_grad, early_grad = attend_back(
         False, flags[:, :key_cut], query, grad_attn, pair_early, query_line, key_column[:early], lse, delta
     )
-    query_grad, own_grad = attend_back(
-        True, flags[:, key_cut:], query, grad_attn, pair, query_line, key_column[early:], lse, delta, query_grad
-    )
-    down_grad, out_part = trade_back([after(down_rows, own_grad)], ((units,),), 7, side=(grad_branch, mixed))
+    down_grad, out_part = trade_back([after(down_rows, early_grad)], ((units,),), 7, side=(grad_branch, mixed))
     out_rows = far_scatter(out_part)
-    last_branch, returned = product_reduce(after(hidden, out_part), full_down, 18, pair=early_grad)
+    back = [early_grad, query, grad_attn, pair, query_line, key_column[early:], lse, delta, query_grad]
+    last_branch, returned, query_grad, own_grad = product_reduce(after(hidden, out_part), full_down, 18, back=back)
     layer_out = (middle + last_branch).astype(bf)
     grad_raw, head_gain_grads = prepare_back(raw, cosine, sine, head_gains, query_grad, own_grad, returned, grad_logit)
     grad_h_one, attn_part = product_reduce(grad_raw, full_attn, 17, hidden_first)

time: 683 us -> 667 us (0.977)
  Pallas kernels: 584 us -> 563 us
    pallas_call x2 -> x1, Pallas kernels: 30.7 us -> 6.29 us  [attend_back(): pl.pallas_call(partial(attend_back_body, causal), grid_spec=pltpu.Prefetc...]
    unnamed x70 -> x64, local copies, waits for them, and re-layouts: 20.9 us -> 20.5 us
  transfers between devices with their start and end apart: 8 -> 8, of which waited for: 1 -> 1; matrix products, arithmetic and copies ran while one was open for 8% -> 7% of each run, Pallas kernels for 82% -> 81%
where the time goes in v6:
time: 667 us; the launch traced here: 661 us
  Pallas kernels  563 us (84%)
  local copies, waits for them, and re-layouts  32.7 us (5%)
  other arithmetic  32.7 us (5%)
  between operations  15 us (2%)
  matrix products  10.5 us (2%)
    pallas_call x4, Pallas kernels, product_reduce(): pl.pallas_call(partial(reduce_body, side, bool(back)), out_shape=outs, in...  218 us
    pallas_call x7, Pallas kernels, trade_call(): pl.pallas_call(partial(trade_body, inward, widths, sender, bool(side), bo...  118 us
    pallas_call x2, Pallas kernels, gather_product(): pl.pallas_call(partial(gather_product_body, not gated), out_shape=outs, i...  82.3 us
    pallas_call x1, Pallas kernels, gather_group(): pl.pallas_call(gather_body, out_shape=jax.ShapeDtypeStruct((share * GROUP...  40.3 us
    pallas_call x1, Pallas kernels, gather_attend(): pl.pallas_call(gather_attend_body, out_shape=[shape((share * GROUP * 2, w...  39.1 us
    unnamed x64, local copies, waits for them, and re-layouts  20.5 us
    pallas_call x1, Pallas kernels, hidden_back(): pl.pallas_call(hidden_back_body, grid=(T // (2 * BQ),), in_specs=[blk(wid...  15.2 us
    pallas_call x1, Pallas kernels, attend(): pl.pallas_call(partial(attend_body, causal, last), grid_spec=pltpu.Prefet...  15 us
  transfers between devices with their start and end apart: 8, of which 1 were waited for; matrix products, arithmetic and copies ran while one was open for 7% of the time, Pallas kernels for 81%

profile of v6, /device:TPU:0, one launch (start us, length us, event | category | flops | bytes accessed | tf_op | source)
XLA Modules:
  0.0 660.7 jit_solution(1645047889889259783)
XLA Ops:
  10.3 19.2 %trade_group.7 = (bf16[4,128,640]{2,1,0:T(8,128)(2,1)}, f32[2,4,4,8,128]{4,3,2,1,0:T(8,128)}) custom-call(bf16[128,1024]{1,0:T(8,128)(2,1)} %refs_0_.2, bf16[128,512]{1,0:T(8,128)(2,1)} %refs_1_.2, bf16[128,512]{1,0:T(8,128)(2,1)} %refs_2_.1, bf16[128,512]{1,0:T(8,128)(2,1)} %bitcast.50, f32[8,128]{1,0:T(8,128)} %fusion.18.refs_4_), custom_call_target="tpu_custom_call" | custom-call | bytes 65536 | tf_op jit(solution)/shard_map/trade_group/pallas_call | solution.py:1119
  30.5 7.4 %trade_group.8 = bf16[4,128,256]{2,1,0:T(8,128)(2,1)} custom-call(bf16[128,1024]{1,0:T(8,128)(2,1)} %bitcast.46), custom_call_target="tpu_custom_call" | custom-call | bytes 65536 | tf_op jit(solution)/shard_map/trade_group/pallas_call | solution.py:1119
  40.6 40.3 %gather_group.1.x_ref.refs_0_ = bf16[2048,2048]{1,0:T(8,128)(2,1)} custom-call(bf16[256,2048]{1,0:T(8,128)(2,1)} %fusion.2.x_ref), custom_call_target="tpu_custom_call" | custom-call | bytes 65536 | tf_op jit(solution)/shard_map/gather_group/pallas_call | solution.py:421
  81.2 5.7 tables.1
  94.6 13.0 %prepare_heads.1 = (f32[2048,640]{1,0:T(8,128)}, bf16[2048,256]{1,0:T(8,128)(2,1)}, bf16[2048,256]{1,0:T(8,128)(2,1)}) custom-call(bf16[2048,2048]{1,0:T(8,128)(2,1)} %gather_group.1.x_ref.refs_0_, bf16[2048,640]{1,0:T(8,128)(2,1)} %all-gather.5.cloned.1.call-done.w_ref.right_ref, f32[2048,128]{1,0:T(8,128)} %get-tuple-element.205.cos_ref, ...), custom_call_target="tpu_custom_call" | custom-call | flops 5368709120 | bytes 15728640 | tf_op jit(solution)/shard_map/prepare_heads/pallas_call | solution.py:243
  107.7 26.4 %trade_group.9 = (bf16[4,128,1536]{2,1,0:T(8,128)(2,1)}, bf16[2048,256]{1,0:T(8,128)(2,1)}) custom-call(bf16[128,3072]{1,0:T(8,128)(2,1)} %refs_0_.3, bf16[128,3072]{1,0:T(8,128)(2,1)} %refs_1_.3, bf16[2048,256]{1,0:T(8,128)(2,1)} %get-tuple-element.79.refs_2_.kv_ref.refs_3_), custom_call_target="tpu_custom_call" | custom-call | bytes 65536 | tf_op jit(solution)/shard_map/trade_group/pallas_call | solution.py:1119
  136.6 15.0 %attend_own.1 = (f32[2048,256]{1,0:T(8,128)}, f32[2048,2]{1,0:T(8,128)}) custom-call(s32[8,4]{1,0:T(8,128)} %get-tuple-element.211.flags, bf16[2048,256]{1,0:T(8,128)(2,1)} %get-tuple-element.81.q_ref.refs_1_, bf16[2048,256]{1,0:T(8,128)(2,1)} %get-tuple-element.79.refs_2_.kv_ref.refs_3_, s32[2048,1]{1,0:T(8,128)} %get-tuple-element.82.qbit_ref, ...), custom_call_target="tpu_custom_call" | custom-call | flops 2147483648 | bytes 8388608 | tf_op jit(solution)/shard_map/attend_own/pallas_call | solution.py:117
  151.6 12.5 %trade_group.10 = bf16[4,128,768]{2,1,0:T(8,128)(2,1)} custom-call(bf16[128,3072]{1,0:T(8,128)(2,1)} %bitcast.42), custom_call_target="tpu_custom_call" | custom-call | bytes 65536 | tf_op jit(solution)/shard_map/trade_group/pallas_call | solution.py:1119
  168.8 39.1 %gather_attend.1 = (bf16[2048,2048]{1,0:T(8,128)(2,1)}, f32[2048,256]{1,0:T(8,128)S(1)}, bf16[2048,256]{1,0:T(8,128)(2,1)S(1)}, f32[2,2048]{1,0:T(2,128)S(1)}) custom-call(bf16[256,2048]{1,0:T(8,128)(2,1)S(1)} %copy-done, bf16[2048,256]{1,0:T(8,128)(2,1)S(1)} %copy-done.3, bf16[2048,256]{1,0:T(8,128)(2,1)S(1)} %copy-done.9, s32[2048,1]{1,0:T(8,128)S(1)} %copy-done.10, ...), custom_call_target="tpu_custom_call" | custom-call | bytes 65536 | tf_op jit(solution)/shard_map/gather_attend/pallas_call | solution.py:488
  210.9 43.7 %product_reduce.4 = f32[256,2048]{1,0:T(8,128)} custom-call(bf16[2048,256]{1,0:T(8,128)(2,1)} %copy-done.2, bf16[2048,256]{1,0:T(8,128)(2,1)} %all-gather.7.cloned.1.call-done.right_ref.w_ref), custom_call_target="tpu_custom_call" | custom-call | bytes 65536 | tf_op jit(solution)/shard_map/product_reduce/pallas_call | solution.py:721
  258.2 42.4 %gather_product.2 = (bf16[2048,2048]{1,0:T(8,128)(2,1)}, f32[2048,1536]{1,0:T(8,128)}, bf16[2048,768]{1,0:T(8,128)(2,1)S(1)}) custom-call(bf16[256,2048]{1,0:T(8,128)(2,1)S(1)} %multiply_convert_fusion.x_ref, bf16[2048,1536]{1,0:T(8,128)(2,1)} %all-gather.9.cloned.1.call-done.w_ref.right_ref), custom_call_target="tpu_custom_call" | custom-call | bytes 65536 | tf_op jit(solution)/shard_map/gather_product/pallas_call | solution.py:894
  302.2 10.5 %convolution_convert_fusion = bf16[2048,768]{1,0:T(8,128)(2,1)} fusion(bf16[2048,2048]{1,0:T(8,128)(2,1)} %get-tuple-element.93.dout_ref, bf16[2048,768]{1,0:T(8,128)(2,1)S(1)} %get-tuple-element.107.left_ref), kind=kOutput, calls=%fused_computation.5 | convolution fusion | flops 6444023808 | bytes 14680064 | tf_op jit(solution)/shard_map/dot_general | solution.py:27
  312.9 15.2 %hidden_back.1.left_ref = bf16[2048,1536]{1,0:T(8,128)(2,1)} custom-call(bf16[2048,2048]{1,0:T(8,128)(2,1)} %get-tuple-element.93.dout_ref, bf16[2048,768]{1,0:T(8,128)(2,1)} %all-gather.11.cloned.1.call-done.down_ref.right_ref, f32[2048,1536]{1,0:T(8,128)} %get-tuple-element.94.both_ref), custom_call_target="tpu_custom_call" | custom-call | flops 6442450944 | bytes 47185920 | tf_op jit(solution)/shard_map/hidden_back/pallas_call | solution.py:327
  328.0 49.5 %product_reduce.5 = (f32[256,2048]{1,0:T(8,128)}, bf16[2048,1536]{1,0:T(8,128)(2,1)}) custom-call(bf16[2048,1536]{1,0:T(8,128)(2,1)} %hidden_back.1.left_ref, bf16[2048,1536]{1,0:T(8,128)(2,1)} %all-gather.9.cloned.1.call-done.w_ref.right_ref, bf16[2048,2048]{1,0:T(8,128)(2,1)} %get-tuple-element.95.refs_0_), custom_call_target="tpu_custom_call" | custom-call | bytes 65536 | tf_op jit(solution)/shard_map/product_reduce/pallas_call | solution.py:721
  383.6 39.9 %gather_product.3 = (bf16[2048,2048]{1,0:T(8,128)(2,1)}, bf16[2048,256]{1,0:T(8,128)(2,1)S(1)}, bf16[2048,128]{1,0:T(8,128)(2,1)S(1)}, f32[2,2048]{1,0:T(2,128)S(1)}) custom-call(bf16[256,2048]{1,0:T(8,128)(2,1)S(1)} %fusion.25.x_ref, bf16[2048,256]{1,0:T(8,128)(2,1)S(1)} %copy-done.1, f32[2048,256]{1,0:T(8,128)S(1)} %copy-done.6, ...), custom_call_target="tpu_custom_call" | custom-call | bytes 65536 | tf_op jit(solution)/shard_map/gather_product/pallas_call | solution.py:894
  425.8 6.3 attend_earlier_back.1
  432.1 12.9 %trade_group.11 = (bf16[128,3072]{1,0:T(8,128)(2,1)}, bf16[2048,256]{1,0:T(8,128)(2,1)}) custom-call(bf16[4,128,768]{2,1,0:T(8,128)(2,1)} %bitcast.47, bf16[2048,2048]{1,0:T(8,128)(2,1)} %get-tuple-element.105.refs_1_, bf16[2048,256]{1,0:T(8,128)(2,1)} %copy-done.2), custom_call_target="tpu_custom_call" | custom-call | bytes 65536 | tf_op jit(solution)/shard_map/trade_group/pallas_call | solution.py:1119
  445.1 79.9 %product_reduce.6 = (f32[256,2048]{1,0:T(8,128)}, bf16[2048,256]{1,0:T(8,128)(2,1)}, f32[2048,256]{1,0:T(8,128)}, f32[2048,256]{1,0:T(8,128)}) custom-call(bf16[2048,768]{1,0:T(8,128)(2,1)} %copy-done.4, bf16[2048,768]{1,0:T(8,128)(2,1)} %all-gather.11.cloned.1.call-done.down_ref.right_ref, bf16[2048,256]{1,0:T(8,128)(2,1)} %get-tuple-element.103.refs_0_, ...), custom_call_target="tpu_custom_call" | custom-call | bytes 65536 | tf_op jit(solution)/shard_map/product_reduce/pallas_call | solution.py:721
  525.0 9.8 %prepare_heads_back.1 = (bf16[2048,640]{1,0:T(8,128)(2,1)}, f32[2,128]{1,0:T(2,128)}) custom-call(f32[2048,640]{1,0:T(8,128)} %get-tuple-element.89.raw_ref.refs_1_, f32[2048,128]{1,0:T(8,128)} %get-tuple-element.205.cos_ref, f32[2048,128]{1,0:T(8,128)} %get-tuple-element.204.sin_ref, f32[2,128]{1,0:T(2,128)} %pad_maximum_fusion.gain_ref, ...), custom_call_target="tpu_custom_call" | custom-call | flops 16384000 | bytes 13107200 | tf_op jit(solution)/shard_map/prepare_heads_back/pallas_call | solution.py:283
  534.8 45.4 %product_reduce.7 = (f32[256,2048]{1,0:T(8,128)}, bf16[2048,640]{1,0:T(8,128)(2,1)}) custom-call(bf16[2048,640]{1,0:T(8,128)(2,1)} %get-tuple-element.114.left_ref, bf16[2048,640]{1,0:T(8,128)(2,1)} %all-gather.5.cloned.1.call-done.w_ref.right_ref, bf16[2048,2048]{1,0:T(8,128)(2,1)} %gather_group.1.x_ref.refs_0_), custom_call_target="tpu_custom_call" | custom-call | bytes 65536 | tf_op jit(solution)/shard_map/product_reduce/pallas_call | solution.py:721
  589.6 5.6 fusion.6
  595.2 27.9 %trade_group.12 = (bf16[128,3072]{1,0:T(8,128)(2,1)}, bf16[128,3072]{1,0:T(8,128)(2,1)}, bf16[128,1024]{1,0:T(8,128)(2,1)}, f32[8,128]{1,0:T(8,128)}) custom-call(bf16[4,128,1536]{2,1,0:T(8,128)(2,1)} %bitcast.44, bf16[4,128,256]{2,1,0:T(8,128)(2,1)} %bitcast.59, f32[2,4,4,8,128]{4,3,2,1,0:T(8,128)} %bitcast.56), custom_call_target="tpu_custom_call" | custom-call | bytes 65536 | tf_op jit(solution)/shard_map/trade_group/pallas_call | solution.py:1119
  625.8 5.6 reduce-scatter.11.cloned.1.call-done
  631.4 11.6 %trade_group.13 = (bf16[128,1024]{1,0:T(8,128)(2,1)}, bf16[128,512]{1,0:T(8,128)(2,1)}, bf16[128,512]{1,0:T(8,128)(2,1)}, bf16[128,512]{1,0:T(8,128)(2,1)}) custom-call(bf16[4,128,640]{2,1,0:T(8,128)(2,1)} %bitcast.48), custom_call_target="tpu_custom_call" | custom-call | bytes 65536 | tf_op jit(solution)/shard_map/trade_group/pallas_call | solution.py:1119
  (134 shorter events, 61.0 us)
Async XLA Ops:
  7.2 22.5 %copy-start.24 = (bf16[1024,128]{1,0:T(8,128)(2,1)S(1)}, bf16[1024,128]{1,0:T(8,128)(2,1)}, u32[]{:S(2)}) copy-start(bf16[1024,128]{1,0:T(8,128)(2,1)} %param.28) | copy-start | bytes 786436
  7.2 31.9 %copy-start.17 = (bf16[256,2048]{1,0:T(8,128)(2,1)S(1)}, bf16[256,2048]{1,0:T(8,128)(2,1)}, u32[]{:S(2)}) copy-start(bf16[256,2048]{1,0:T(8,128)(2,1)} %param.16) | copy-start | bytes 3145732
  7.2 87.4 %all-gather.5.cloned.1.call-start = ((), (), s32[]{:S(2)}) async-start(), calls=%async_computation.4 | async-start | bytes 3276800 | tf_op jit(solution)/shard_map/all_gather | solution.py:1298
  29.6 181.3 %all-gather.7.cloned.1.call-start = ((), (), s32[]{:S(2)}) async-start(), calls=%async_computation.5 | async-start | bytes 1310720 | tf_op jit(solution)/shard_map/all_gather | solution.py:1298
  37.9 220.2 %all-gather.9.cloned.1.call-start = ((), (), s32[]{:S(2)}) async-start(), calls=%async_computation.6 | async-start | bytes 7864320 | tf_op jit(solution)/shard_map/all_gather | solution.py:1298
  107.7 26.5 %copy-start.20 = (bf16[3072,128]{1,0:T(8,128)(2,1)S(1)}, bf16[3072,128]{1,0:T(8,128)(2,1)}, u32[]{:S(2)}) copy-start(bf16[3072,128]{1,0:T(8,128)(2,1)} %param.31) | copy-start | bytes 2359300
  134.1 2.0 copy-start.25
  134.1 178.8 %all-gather.11.cloned.1.call-start = ((), (), s32[]{:S(2)}) async-start(), calls=%async_computation.8 | async-start | bytes 3932160 | tf_op jit(solution)/shard_map/all_gather | solution.py:1298
  136.6 28.2 %copy-start.9 = (bf16[2048,256]{1,0:T(8,128)(2,1)S(1)}, bf16[2048,256]{1,0:T(8,128)(2,1)}, u32[]{:S(2)}) copy-start(bf16[2048,256]{1,0:T(8,128)(2,1)} %get-tuple-element.87.kv_ref) | copy-start | bytes 3145732
  151.6 13.2 %copy-start = (bf16[256,2048]{1,0:T(8,128)(2,1)S(1)}, bf16[256,2048]{1,0:T(8,128)(2,1)}, u32[]{:S(2)}) copy-start(bf16[256,2048]{1,0:T(8,128)(2,1)} %x_ref) | copy-start | bytes 3145732
  151.6 13.2 %copy-start.3 = (bf16[2048,256]{1,0:T(8,128)(2,1)S(1)}, bf16[2048,256]{1,0:T(8,128)(2,1)}, u32[]{:S(2)}) copy-start(bf16[2048,256]{1,0:T(8,128)(2,1)} %get-tuple-element.81.q_ref.refs_1_) | copy-start | bytes 3145732
  164.2 267.9 %reduce-scatter.5.cloned.1.call-start = ((), (), s32[]{:S(2)}) async-start(), calls=%async_computation.7 | async-start | bytes 3932160 | tf_op jit(solution)/shard_map/reduce_scatter | solution.py:1303
  210.9 43.7 %copy-start.18 = (bf16[256,2048]{1,0:T(8,128)(2,1)S(1)}, bf16[256,2048]{1,0:T(8,128)(2,1)}, u32[]{:S(2)}) copy-start(bf16[256,2048]{1,0:T(8,128)(2,1)} %param.16) | copy-start | bytes 3145732
  300.6 1.6 copy-start.4
  312.8 282.4 %reduce-scatter.7.cloned.1.call-start = ((), (), s32[]{:S(2)}) async-start(), calls=%async_computation.9 | async-start | bytes 7864320 | tf_op jit(solution)/shard_map/reduce_scatter | solution.py:1303
  377.5 217.7 %reduce-scatter.9.cloned.1.call-start = ((), (), s32[]{:S(2)}) async-start(), calls=%async_computation.10 | async-start | bytes 1310720 | tf_op jit(solution)/shard_map/reduce_scatter | solution.py:1303
  377.8 3.2 copy-start.16
  377.8 3.1 copy-start.19
  381.7 1.9 copy-start.6
  445.0 186.4 %reduce-scatter.11.cloned.1.call-start = ((), (), s32[]{:S(2)}) async-start(), calls=%async_computation.11 | async-start | bytes 3276800 | tf_op jit(solution)/shard_map/reduce_scatter | solution.py:1303
  580.2 2.7 copy-start.27
  623.1 26.7 %copy-start.23 = (bf16[128,1024]{1,0:T(8,128)(2,1)S(1)}, bf16[128,1024]{1,0:T(8,128)(2,1)}, u32[]{:S(2)}) copy-start(bf16[128,1024]{1,0:T(8,128)(2,1)} %get-tuple-element.126) | copy-start | bytes 786436
  631.4 19.4 %copy-start.22 = (bf16[128,3072]{1,0:T(8,128)(2,1)S(1)}, bf16[128,3072]{1,0:T(8,128)(2,1)}, u32[]{:S(2)}) copy-start(bf16[128,3072]{1,0:T(8,128)(2,1)} %get-tuple-element.127) | copy-start | bytes 2359300
  649.8 2.4 copy-start.21
  (12 other events, 13.2 us)
Sparse Core Ops, SparseCore 0:
  29.7 53.8 all-gather.4
  85.2 26.7 all-gather.6
  134.2 115.5 all-gather.8
  251.2 61.6 all-gather.10
  315.0 59.4 reduce-scatter.4
  377.7 131.8 reduce-scatter.6
  511.8 30.3 reduce-scatter.8
  580.3 51.0 reduce-scatter.10
